TPU v7x, 32 devices: a whole 2x2x4 slice. The times are simulated.
32 devices in a mesh: tp: 4 (over x, core), ep: 2 (over y), dp: 4 (over z).
Axes of the slice: x: 2, y: 2, z: 4, core: 2. Of those that a mesh axis runs over, the one named last changes fastest.
Arguments:
- tokens: bfloat16 [8, 512, 768], P(('ep', 'dp'), 'tp'), may hold values from -6 to 6
- segment: int32 [8, 512], P(('ep', 'dp')), may hold values from 0 to 7, never falling along the last dimension, each value on 1 to 256 neighbouring positions
- key_mask: int32 [8, 512], P(('ep', 'dp')), may hold values 0 or 1
- routes: int32 [8, 512, 2], P(('ep', 'dp'), 'tp'), may hold values from 0 to 3, all different within a row; in each aligned block of 128 rows (0 to 127, 128 to 255, ..., all dimensions but the last counted through in order) at most 128 rows name the same one
- gates: float32 [8, 512, 2], P(('ep', 'dp'), 'tp'), may hold values from 0.25 to 1
- ln1_gain: float32 [768], replicated, may hold values from 0.5 to 1.5
- ln1_bias: float32 [768], replicated, may hold values from -0.5 to 0.5
- query_weight: bfloat16 [768, 768], P(None, 'tp'), may hold values from -0.21875 to 0.21875
- key_weight: bfloat16 [768, 768], P(None, 'tp'), may hold values from -0.21875 to 0.21875
- value_weight: bfloat16 [768, 768], P(None, 'tp'), may hold values from -0.21875 to 0.21875
- out_weight: bfloat16 [768, 768], P('tp'), may hold values from -2.5 to 2.5
- ln2_gain: float32 [768], replicated, may hold values from 0.5 to 1.5
- ln2_bias: float32 [768], replicated, may hold values from -0.5 to 0.5
- frozen_in: bfloat16 [2, 768, 3072], P('ep'), may hold values from -0.21875 to 0.21875
- frozen_out: bfloat16 [2, 3072, 768], P('ep'), may hold values from -0.109375 to 0.109375
- train_in: bfloat16 [2, 768, 3072], P('ep'), may hold values from -0.21875 to 0.21875
- train_out: bfloat16 [2, 3072, 768], P('ep'), may hold values from -0.109375 to 0.109375
- cotangent: bfloat16 [8, 512, 768], P(('ep', 'dp'), 'tp'), may hold values from -6 to 6
Outputs:
- layer_out: bfloat16 [8, 512, 768], P(('ep', 'dp'), 'tp')
- tokens_grad: float32 [8, 512, 768], P(('ep', 'dp'), 'tp')
- ln1_gain_grad: float32 [768], replicated
- ln1_bias_grad: float32 [768], replicated
- query_grad: float32 [768, 768], P(None, 'tp')
- key_grad: float32 [768, 768], P(None, 'tp')
- value_grad: float32 [768, 768], P(None, 'tp')
- out_grad: float32 [768, 768], P('tp')
- ln2_gain_grad: float32 [768], replicated
- ln2_bias_grad: float32 [768], replicated
- train_in_grad: float32 [2, 768, 3072], P('ep')
- train_out_grad: float32 [2, 3072, 768], P('ep')
- expert_counts: int32 [4], replicated
Inputs may be any that keep to these rules, and one draw needn't show every extreme that they name: `segment`: segment numbers never fall along a group; each sequence holds 1 to 256 tokens, one exactly 256. `routes`: the two experts of a token differ. In the tokens of one device (aligned blocks of 128 tokens) no expert is named more than 128 times, a bound that some block reaches.
All inputs are finite; a program needn't handle non-finite values. No bound on the sum of `key_mask` on one device may be relied on, other than what follows from the above.
Results may differ from a plain program's by a relative error of at most 0.017.
Values may be sent and summed in bfloat16 or wider, within the bound.
A program may use at most 192 MiB of HBM per device.

v0:
```python
import jax
import jax.numpy as jnp
from jax import lax
from jax.sharding import PartitionSpec as P

HD = 64
EXP_DEV = 2


EPSILON = 1e-05
MASKED = -1e30


def layer_norm(values, gain, bias):
    center = jnp.mean(values, axis=-1, keepdims=True)
    shifted = values - center
    spread = jnp.mean(shifted * shifted, axis=-1, keepdims=True)
    return shifted * lax.rsqrt(spread + EPSILON) * gain + bias


def gelu_exact(values):
    return jax.nn.gelu(values, approximate=False)


def contract(left, right, left_dim, right_dim):
    return lax.dot_general(
        left, right, (((left_dim,), (right_dim,)), ((), ())), preferred_element_type=jnp.float32
    )


def masked_scores(queries, query_segment, keys, segment_row, keep_row):
    scale = queries.shape[-1] ** (-0.5)
    scores = jnp.einsum("hqd,hkd->hqk", queries, keys, preferred_element_type=jnp.float32) * scale
    allowed = (query_segment[:, None] == segment_row[None, :]) & keep_row[None, :]
    return jnp.where(allowed[None], scores, MASKED)


def to_owners(buffer):
    return lax.all_to_all(buffer, "ep", split_axis=0, concat_axis=0, tiled=True)


def to_sources(buffer):
    return lax.all_to_all(buffer, "ep", split_axis=0, concat_axis=0, tiled=True)


def expert_forward(inputs, inner, outer):
    hidden = contract(inputs, inner, 1, 0)
    active = gelu_exact(hidden).astype(jnp.bfloat16)
    return (hidden, active, contract(active, outer, 1, 0))


def expert_backward(inputs, hidden, active, upstream, inner, outer, trainable):
    through = contract(upstream, outer, 1, 1)
    slope = jax.vjp(gelu_exact, hidden)[1](through)[0].astype(jnp.bfloat16)
    back_in = contract(slope, inner, 1, 1)
    if trainable:
        return (back_in, contract(inputs, slope, 0, 0), contract(active, upstream, 0, 0))
    return (back_in, None, None)


def local(
    tokens,
    segment,
    key_mask,
    routes,
    gates,
    ln1_gain,
    ln1_bias,
    query_weight,
    key_weight,
    value_weight,
    out_weight,
    ln2_gain,
    ln2_bias,
    frozen_in,
    frozen_out,
    train_in,
    train_out,
    cotangent,
):
    tp_count = lax.axis_size("tp")
    ep_count = lax.axis_size("ep")
    local_rows = tokens.shape[1]
    width = tokens.shape[2]
    group_rows = local_rows * tp_count
    head_cols = query_weight.shape[1]
    local_heads = head_cols // HD
    residual = tokens[0].astype(jnp.float32)
    joined = jnp.concatenate([query_weight, key_weight, value_weight], axis=1)
    first_normed = layer_norm(residual, ln1_gain, ln1_bias).astype(jnp.bfloat16)
    piece = lax.all_gather(first_normed, "tp", axis=0, tiled=True)
    projected = contract(piece, joined, 1, 0)
    gathered = piece
    projected, normed_group = (projected, gathered)
    projected = projected.astype(jnp.bfloat16)
    block = min(512, group_rows)
    blocks = group_rows // block

    def split_heads(matrix):
        return matrix.reshape(group_rows, local_heads, HD).transpose(1, 0, 2)

    def merge_heads(tensor):
        return tensor.transpose(1, 0, 2).reshape(group_rows, head_cols)

    queries = split_heads(projected[:, :head_cols])
    keys = split_heads(projected[:, head_cols : 2 * head_cols])
    values = split_heads(projected[:, 2 * head_cols :])
    query_blocks = queries.reshape(local_heads, blocks, block, HD).transpose(1, 0, 2, 3)
    segment_row = segment[0]
    starts = jnp.concatenate(
        [segment_row[:1] == segment_row[:1], segment_row[1:] != segment_row[:-1]]
    )
    keep_row = (key_mask[0] == 1) | starts
    segment_blocks = segment_row.reshape(blocks, block)

    def forward_block(item):
        block_queries, block_segment = item
        scores = masked_scores(block_queries, block_segment, keys, segment_row, keep_row)
        highest = jnp.max(scores, axis=-1, keepdims=True)
        weights = jnp.exp(scores - highest)
        totals = jnp.sum(weights, axis=-1, keepdims=True)
        probs = (weights / totals).astype(jnp.bfloat16)
        outputs = jnp.einsum("hqk,hkd->hqd", probs, values, preferred_element_type=jnp.float32)
        return (outputs, (highest + jnp.log(totals))[..., 0])

    head_blocks, log_totals = lax.map(forward_block, (query_blocks, segment_blocks))
    attn_heads = (
        head_blocks.transpose(0, 2, 1, 3).reshape(group_rows, head_cols).astype(jnp.bfloat16)
    )
    middle = residual + lax.psum_scatter(
        contract(attn_heads, out_weight, 1, 0), "tp", scatter_dimension=0, tiled=True
    )
    second_normed = layer_norm(middle, ln2_gain, ln2_bias).astype(jnp.bfloat16)
    experts = EXP_DEV * ep_count
    capacity = 4 * local_rows // experts
    slots = experts * capacity
    route = routes[0]
    marks = (route.reshape(-1)[:, None] == jnp.arange(experts, dtype=jnp.int32)[None, :]).astype(
        jnp.int32
    )
    places = jnp.sum((jnp.cumsum(marks, axis=0) - 1) * marks, axis=1).reshape(local_rows, 2)
    slot_ids = route * capacity + places
    slot_range = jnp.arange(slots, dtype=jnp.int32)[None, :]
    pick_first = (slot_ids[:, 0:1] == slot_range).astype(jnp.bfloat16)
    pick_second = (slot_ids[:, 1:2] == slot_range).astype(jnp.bfloat16)
    local_counts = jnp.sum(marks, axis=0).astype(jnp.float32)
    send = contract(pick_first + pick_second, second_normed, 0, 0).astype(jnp.bfloat16)
    arrived = to_owners(send.reshape(ep_count, EXP_DEV, capacity, width))
    inner_list = (frozen_in[0], train_in[0])
    outer_list = (frozen_out[0], train_out[0])
    kept = []
    produced = []
    for index in range(EXP_DEV):
        inputs = arrived[:, index].reshape(-1, width)
        hidden, active, result = expert_forward(inputs, inner_list[index], outer_list[index])
        kept.append((inputs, hidden, active))
        produced.append(result.reshape(ep_count, -1, width))
    produced = jnp.stack(produced, axis=1)
    returned = to_sources(produced.astype(jnp.bfloat16)).reshape(slots, width)
    gate_rows = gates[0]
    mixture = gate_rows[:, 0:1] * contract(pick_first, returned, 1, 0) + gate_rows[
        :, 1:2
    ] * contract(pick_second, returned, 1, 0)
    layer_out = (middle + mixture).astype(jnp.bfloat16)
    upstream = cotangent[0].astype(jnp.float32)
    first_share = (gate_rows[:, 0:1] * upstream).astype(jnp.bfloat16)
    second_share = (gate_rows[:, 1:2] * upstream).astype(jnp.bfloat16)
    back_send = (
        contract(pick_first, first_share, 0, 0) + contract(pick_second, second_share, 0, 0)
    ).astype(jnp.bfloat16)
    back_arrived = to_owners(back_send.reshape(ep_count, EXP_DEV, capacity, width))
    input_terms = []
    grad_in = None
    grad_out = None
    for index in range(EXP_DEV):
        inputs, hidden, active = kept[index]
        back_in, maybe_in, maybe_out = expert_backward(
            inputs,
            hidden,
            active,
            back_arrived[:, index].reshape(-1, width),
            inner_list[index],
            outer_list[index],
            index == EXP_DEV - 1,
        )
        if index == EXP_DEV - 1:
            grad_in, grad_out = (maybe_in, maybe_out)
        input_terms.append(back_in.reshape(ep_count, -1, width))
    input_terms = jnp.stack(input_terms, axis=1)
    back_returned = to_sources(input_terms.astype(jnp.bfloat16)).reshape(slots, width)
    grad_in, grad_out = (
        lax.psum(grad_in.astype(jnp.bfloat16), ("tp", "dp")).astype(jnp.float32),
        lax.psum(grad_out.astype(jnp.bfloat16), ("tp", "dp")).astype(jnp.float32),
    )
    second_grad = contract(pick_first, back_returned, 1, 0) + contract(
        pick_second, back_returned, 1, 0
    )
    middle_part, ln2_gain_grad, ln2_bias_grad = jax.vjp(layer_norm, middle, ln2_gain, ln2_bias)[1](
        second_grad
    )
    middle_grad = upstream + middle_part
    attn_grad = middle_grad.astype(jnp.bfloat16)
    piece = lax.all_gather(attn_grad, "tp", axis=0, tiled=True)
    head_grad = contract(piece, out_weight, 1, 1)
    out_part = contract(attn_heads, piece, 0, 0)
    head_grad, out_part = (head_grad, out_part)
    upstream_blocks = (
        split_heads(head_grad.astype(jnp.bfloat16))
        .reshape(local_heads, blocks, block, HD)
        .transpose(1, 0, 2, 3)
    )

    def backward_block(carry, item):
        key_sum, value_sum = carry
        block_queries, block_segment, block_totals, block_upstream = item
        scores = masked_scores(block_queries, block_segment, keys, segment_row, keep_row)
        probs = jnp.exp(scores - block_totals[..., None])
        prob_grad = jnp.einsum(
            "hqd,hkd->hqk", block_upstream, values, preferred_element_type=jnp.float32
        )
        centered = jnp.sum(probs * prob_grad, axis=-1, keepdims=True)
        score_grad = (probs * (prob_grad - centered)).astype(jnp.bfloat16)
        scale = block_queries.shape[-1] ** (-0.5)
        query_part = (
            jnp.einsum("hqk,hkd->hqd", score_grad, keys, preferred_element_type=jnp.float32) * scale
        )
        key_sum = (
            key_sum
            + jnp.einsum(
                "hqk,hqd->hkd", score_grad, block_queries, preferred_element_type=jnp.float32
            )
            * scale
        )
        value_sum = value_sum + jnp.einsum(
            "hqk,hqd->hkd",
            probs.astype(jnp.bfloat16),
            block_upstream,
            preferred_element_type=jnp.float32,
        )
        return ((key_sum, value_sum), query_part)

    zero_heads = jnp.zeros((local_heads, group_rows, HD), jnp.float32)
    (key_sum, value_sum), query_parts = lax.scan(
        backward_block,
        (zero_heads, zero_heads),
        (query_blocks, segment_blocks, log_totals, upstream_blocks),
    )
    query_full = query_parts.transpose(0, 2, 1, 3).reshape(group_rows, head_cols)
    projected_grad = jnp.concatenate(
        [query_full, merge_heads(key_sum), merge_heads(value_sum)], axis=1
    ).astype(jnp.bfloat16)
    joined_grad = contract(normed_group, projected_grad, 0, 0)
    first_grad = lax.psum_scatter(
        contract(projected_grad, joined, 1, 1).astype(jnp.bfloat16),
        "tp",
        scatter_dimension=0,
        tiled=True,
    ).astype(jnp.float32)
    residual_part, ln1_gain_grad, ln1_bias_grad = jax.vjp(layer_norm, residual, ln1_gain, ln1_bias)[
        1
    ](first_grad)
    tokens_grad = middle_grad + residual_part
    summed = (
        lax.psum(joined_grad[:, :head_cols].astype(jnp.bfloat16), ("ep", "dp")).astype(jnp.float32),
        lax.psum(
            joined_grad[:, head_cols : 2 * head_cols].astype(jnp.bfloat16), ("ep", "dp")
        ).astype(jnp.float32),
        lax.psum(joined_grad[:, 2 * head_cols :].astype(jnp.bfloat16), ("ep", "dp")).astype(
            jnp.float32
        ),
        lax.psum(out_part.astype(jnp.bfloat16), ("ep", "dp")).astype(jnp.float32),
    )
    counts, gain_one, bias_one, gain_two, bias_two = lax.psum(
        (local_counts, ln1_gain_grad, ln1_bias_grad, ln2_gain_grad, ln2_bias_grad),
        ("tp", "ep", "dp"),
    )
    return (
        layer_out[None],
        tokens_grad[None],
        gain_one,
        bias_one,
        summed[0],
        summed[1],
        summed[2],
        summed[3],
        gain_two,
        bias_two,
        grad_in[None],
        grad_out[None],
        counts.astype(jnp.int32),
    )


def solution(mesh):
    in_specs = (
        P(("ep", "dp"), "tp", None),
        P(("ep", "dp"), None),
        P(("ep", "dp"), None),
        P(("ep", "dp"), "tp", None),
        P(("ep", "dp"), "tp", None),
        P(),
        P(),
        P(None, "tp"),
        P(None, "tp"),
        P(None, "tp"),
        P("tp", None),
        P(),
        P(),
        P("ep", None, None),
        P("ep", None, None),
        P("ep", None, None),
        P("ep", None, None),
        P(("ep", "dp"), "tp", None),
    )
    out_specs = (
        P(("ep", "dp"), "tp", None),
        P(("ep", "dp"), "tp", None),
        P(),
        P(),
        P(None, "tp"),
        P(None, "tp"),
        P(None, "tp"),
        P("tp", None),
        P(),
        P(),
        P("ep", None, None),
        P("ep", None, None),
        P(),
    )
    return jax.shard_map(local, mesh=mesh, in_specs=in_specs, out_specs=out_specs, check_vma=False)
```

profile of v0, /device:TPU:0, one launch (start us, length us, event | category | flops | bytes accessed | tf_op | source)
XLA Modules:
  0.0 457.1 jit_solution(4886164368282397368)
XLA Ops:
  9.9 1.1 fusion.84
  11.1 1.1 fusion.83
  12.2 10.1 %all_gather.6 = bf16[512,768]{1,0:T(8,128)(2,1)S(1)} all-gather(bf16[128,768]{1,0:T(8,128)(2,1)S(1)} %fusion.83), channel_id=1, replica_groups=mesh['tp'=4,'ep'=2,'dp'=4] {'tp'}, dimensions={0}, use_global_device_ids=true | all-gather | bytes 983040 | tf_op jit(solution)/shard_map/all_gather | solution.py:91
  22.3 1.2 constant_dynamic-update-slice_fusion.2
  29.4 1.6 fusion.132
  31.4 1.2 reduce-window.6
  34.9 1.4 fusion.91
  36.4 2.4 add_convert_fusion.2
  38.7 4.3 all-to-all-start.2
  43.0 16.9 %reduce-scatter.3.cloned.1.call-done = f32[128,768]{1,0:T(8,128)} async-done(((f32[512,768]{1,0:T(8,128)}), f32[128,768]{1,0:T(8,128)}) %reduce-scatter.3.cloned.1.call-update) | async-done | bytes 393232 | tf_op jit(solution)/shard_map/reduce_scatter | solution.py:130
  59.9 1.2 fusion.125
  61.8 1.4 convolution_convert_fusion.4
  63.2 4.5 all-to-all-start
  67.7 2.0 fusion.128
  69.8 8.8 %all-to-all-done = bf16[2,2,128,768]{3,2,1,0:T(8,128)(2,1)} async-done(((bf16[2,2,128,768]{3,2,1,0:T(8,128)(2,1)}), bf16[2,2,128,768]{3,2,1,0:T(8,128)(2,1)}, u32[]{:S(2)}, u32[]{:S(2)}) %all-to-all-start) | async-done | bytes 786464 | tf_op jit(solution)/shard_map/all_to_all | solution.py:39
  78.6 1.3 fusion.129
  80.0 11.0 %multiply_convert_fusion.2 = (bf16[256,3072]{1,0:T(8,128)(2,1)}, f32[256,3072]{1,0:T(8,128)S(1)}, f32[256,3072]{1,0:T(8,128)S(1)}) fusion(bf16[256,768]{1,0:T(8,128)(2,1)S(1)} %bitcast.231, bf16[1,768,3072]{2,1,0:T(8,128)(2,1)} %param.31), kind=kOutput, calls=%fused_computation.42 | convolution fusion | flops 1259077632 | bytes 12976128 | tf_op jit(solution)/shard_map/dot_general | solution.py:26
  91.0 2.0 add_convert_fusion.1
  93.1 1.4 fusion.55
  94.6 9.0 %multiply_convert_fusion.1 = (bf16[256,3072]{1,0:T(8,128)(2,1)}, f32[256,3072]{1,0:T(8,128)S(1)}, f32[256,3072]{1,0:T(8,128)S(1)}) fusion(bf16[256,768]{1,0:T(8,128)(2,1)S(1)} %bitcast.215, bf16[1,768,3072]{2,1,0:T(8,128)(2,1)S(1)} %bitcast.244), kind=kOutput, calls=%fused_computation.29 | convolution fusion | flops 1259077632 | bytes 12976128 | tf_op jit(solution)/shard_map/dot_general | solution.py:26
  103.6 2.0 add_convert_fusion
  105.6 1.4 fusion.52
  108.1 4.3 all-to-all-start.3
  112.5 10.1 %all-to-all-done.3 = bf16[2,2,128,768]{3,2,1,0:T(8,128)(2,1)} async-done(((bf16[2,2,128,768]{3,2,1,0:T(8,128)(2,1)}), bf16[2,2,128,768]{3,2,1,0:T(8,128)(2,1)}, u32[]{:S(2)}, u32[]{:S(2)}) %all-to-all-start.3) | async-done | bytes 786464 | tf_op jit(solution)/shard_map/all_to_all | solution.py:43
  122.6 1.5 fusion.90
  124.1 1.7 multiply_reduce_fusion.1
  126.9 7.8 %all_gather.7 = bf16[512,768]{1,0:T(8,128)(2,1)S(1)} all-gather(bf16[128,768]{1,0:T(8,128)(2,1)S(1)} %fusion.94), channel_id=1, replica_groups=mesh['tp'=4,'ep'=2,'dp'=4] {'tp'}, dimensions={0}, use_global_device_ids=true | all-gather | bytes 983040 | tf_op jit(solution)/shard_map/all_gather | solution.py:203
  141.2 2.7 convolution_convert_fusion.3
  144.2 5.2 %fusion.16 = bf16[1,768,3072]{2,1,0:T(8,128)(2,1)} fusion(bf16[256,768]{1,0:T(8,128)(2,1)S(1)} %bitcast.216, bf16[256,3072]{1,0:T(8,128)(2,1)} %copy-done.19), kind=kOutput, calls=%fused_computation.20 | convolution fusion | flops 1210318848 | bytes 6684672 | tf_op jit(solution)/shard_map/dot_general | solution.py:26
  149.4 3.6 fusion.17
  153.1 1.4 copy-done.37
  154.5 3.7 fusion.61
  158.2 3.8 fusion.58
  163.0 3.5 all-to-all-start.1
  166.6 13.7 %all-to-all-done.1 = bf16[2,2,128,768]{3,2,1,0:T(8,128)(2,1)S(1)} async-done(((bf16[2,2,128,768]{3,2,1,0:T(8,128)(2,1)}), bf16[2,2,128,768]{3,2,1,0:T(8,128)(2,1)S(1)}, u32[]{:S(2)}, u32[]{:S(2)}) %all-to-all-start.1) | async-done | bytes 786464 | tf_op jit(solution)/shard_map/all_to_all | solution.py:43
  181.6 42.1 %all-reduce.9.cloned.1.call-done = (bf16[768,192]{0,1:T(8,128)(2,1)}, bf16[768,192]{0,1:T(8,128)(2,1)}, bf16[768,192]{0,1:T(8,128)(2,1)}, bf16[192,768]{1,0:T(8,128)(2,1)}) async-done(((bf16[768,192]{0,1:T(8,128)(2,1)}, bf16[768,192]{0,1:T(8,128)(2,1)}, bf16[768,192]{0,1:T(8,128)(2,1)}, bf16[192,768]{1,0:T(8,128)(2,1)}), (bf16[768,192]{0,1:T(8,128)(2,1)}, bf16[768,192]{0,1:T(8,128)(2,1)}, ...) | async-done | bytes 1179664 | tf_op jit(solution)/shard_map/psum | solution.py:264
  223.7 1.8 convert_element_type.162
  225.5 1.8 convert_element_type.163
  227.3 1.8 convert_element_type.164
  229.1 1.8 convert_element_type.166
  230.9 17.7 %reduce-scatter.5.cloned.1.call-done = bf16[128,768]{1,0:T(8,128)(2,1)} async-done(((bf16[512,768]{1,0:T(8,128)(2,1)}), bf16[128,768]{1,0:T(8,128)(2,1)}) %reduce-scatter.5.cloned.1.call-update) | async-done | bytes 196624 | tf_op jit(solution)/shard_map/reduce_scatter | solution.py:253
  248.6 1.1 convert_reduce_fusion
  249.8 1.2 fusion.86
  251.0 41.6 %all-reduce.1 = (f32[768]{0:T(1024)}, f32[768]{0:T(1024)}, f32[768]{0:T(1024)}, f32[768]{0:T(1024)}, f32[4]{0:T(128)S(1)}) all-reduce(f32[768]{0:T(1024)S(1)} %get-tuple-element.61, f32[768]{0:T(1024)S(1)} %get-tuple-element.64, f32[768]{0:T(1024)S(1)} %get-tuple-element.59, ...), channel_id=1, replica_groups=mesh['tp'=4,'ep'=2,'dp'=4] {'tp','ep','dp'}, use_global_device_ids=true, to_apply=%region_17.18 | all-reduce | flops 3076 | bytes 24608 | tf_op jit(solution)/shard_map/psum | solution.py:273
  293.2 1.9 add_bitcast_fusion
  295.1 143.5 %all-reduce.7.cloned.1.call-done = (bf16[1,768,3072]{2,1,0:T(8,128)(2,1)}, bf16[1,3072,768]{2,1,0:T(8,128)(2,1)}) async-done(((bf16[1,768,3072]{2,1,0:T(8,128)(2,1)}, bf16[1,3072,768]{2,1,0:T(8,128)(2,1)}), (bf16[1,768,3072]{2,1,0:T(8,128)(2,1)}, bf16[1,3072,768]{2,1,0:T(8,128)(2,1)})) %all-reduce.7.cloned.1.call-update) | async-done | bytes 9437200 | tf_op jit(solution)/shard_map/psum | solution.py:192
  438.5 7.5 %broadcast_in_dim.113 = f32[1,768,3072]{2,1,0:T(8,128)} convert(bf16[1,768,3072]{2,1,0:T(8,128)(2,1)} %get-tuple-element.86) | non-fusion elementwise | flops 2359296 | bytes 14155776 | tf_op jit(solution)/shard_map/broadcast_in_dim | solution.py:288
  446.1 4.5 broadcast_in_dim.115
  (160 shorter events, 23.9 us)
Async XLA Ops:
  7.2 22.2 %copy-start = (bf16[192,768]{1,0:T(8,128)(2,1)S(1)}, bf16[192,768]{1,0:T(8,128)(2,1)}, u32[]{:S(2)}) copy-start(bf16[192,768]{1,0:T(8,128)(2,1)} %param.28) | copy-start | bytes 884740
  7.2 17.2 %copy-start.27 = (bf16[768,192]{0,1:T(8,128)(2,1)S(1)}, bf16[768,192]{0,1:T(8,128)(2,1)}, u32[]{:S(2)}) copy-start(bf16[768,192]{0,1:T(8,128)(2,1)} %param.27) | copy-start | bytes 884740
  7.2 52.7 %reduce-scatter.3.cloned.1.call-start = ((), (), s32[]{:S(2)}) async-start(), calls=%async_computation.6 | async-start | bytes 1966080 | tf_op jit(solution)/shard_map/reduce_scatter | solution.py:130
  12.2 14.0 %copy-start.33 = (s32[1,512]{1,0:T(1,128)S(1)}, s32[1,512]{1,0:T(1,128)}, u32[]{:S(2)}) copy-start(s32[1,512]{1,0:T(1,128)} %param.19) | copy-start | bytes 6148
  22.3 4.2 copy-start.22
  26.1 1.4 copy-start.15
  26.1 1.9 copy-start.20
  28.7 2.3 copy-start.35
  28.7 6.2 %copy-start.36 = (f32[1,128,2]{1,2,0:T(2,128)S(1)}, f32[1,128,2]{1,2,0:T(2,128)}, u32[]{:S(2)}) copy-start(f32[1,128,2]{1,2,0:T(2,128)} %param.22) | copy-start | bytes 3076
  36.3 25.5 %copy-start.32 = (f32[768]{0:T(1024)S(1)}, f32[768]{0:T(1024)}, u32[]{:S(2)}) copy-start(f32[768]{0:T(1024)} %param.29) | copy-start | bytes 9220
  36.3 25.5 %copy-start.34 = (f32[768]{0:T(1024)S(1)}, f32[768]{0:T(1024)}, u32[]{:S(2)}) copy-start(f32[768]{0:T(1024)} %param.30) | copy-start | bytes 9220
  38.7 24.5 %all-to-all-start.2 = ((bf16[2,2,128,768]{3,2,1,0:T(8,128)(2,1)}), bf16[2,2,128,768]{3,2,1,0:T(8,128)(2,1)}, u32[]{:S(2)}, u32[]{:S(2)}) async-start(bf16[2,2,128,768]{3,2,1,0:T(8,128)(2,1)} %bitcast.214), calls=%async_computation.3 | async-start | bytes 1572864 | tf_op jit(solution)/shard_map/all_to_all | solution.py:39
  63.2 15.3 %all-to-all-start = ((bf16[2,2,128,768]{3,2,1,0:T(8,128)(2,1)}), bf16[2,2,128,768]{3,2,1,0:T(8,128)(2,1)}, u32[]{:S(2)}, u32[]{:S(2)}) async-start(bf16[2,2,128,768]{3,2,1,0:T(8,128)(2,1)} %bitcast.213), calls=%async_computation.1 | async-start | bytes 1572864 | tf_op jit(solution)/shard_map/all_to_all | solution.py:39
  78.6 12.4 %slice-start.4 = ((s8[4718592]{0:T(1024)(128)(4,1)}), s8[4194304]{0:T(1024)(128)(4,1)S(1)}, s32[]{:S(2)}) async-start(s8[4718592]{0:T(1024)(128)(4,1)} %bitcast.245), calls=%async_computation.14 | async-start | bytes 8388608
  78.6 14.5 %slice-start = ((s8[4718592]{0:T(1024)(128)(4,1)}), s8[4194304]{0:T(1024)(128)(4,1)S(1)}, s32[]{:S(2)}) async-start(s8[4718592]{0:T(1024)(128)(4,1)} %bitcast.241), calls=%async_computation.10 | async-start | bytes 8388608
  78.6 15.9 %slice-start.2 = ((s8[4718592]{0:T(1024)(128)(4,1)}), s8[4194304]{0:T(1024)(128)(4,1)S(1)}, s32[]{:S(2)}) async-start(s8[4718592]{0:T(1024)(128)(4,1)} %bitcast.243), calls=%async_computation.12 | async-start | bytes 8388608
  79.9 14.6 %copy-start.11 = (bf16[2,1,128,768]{3,2,1,0:T(8,128)(2,1)}, bf16[2,1,128,768]{3,2,1,0:T(8,128)(2,1)S(1)}, u32[]{:S(2)}) copy-start(bf16[2,1,128,768]{3,2,1,0:T(8,128)(2,1)S(1)} %get-tuple-element.106) | copy-start | bytes 1179652
  79.9 11.1 %copy-start.26 = (bf16[2,1,128,768]{3,2,1,0:T(8,128)(2,1)S(1)}, bf16[2,1,128,768]{3,2,1,0:T(8,128)(2,1)}, u32[]{:S(2)}) copy-start(bf16[2,1,128,768]{3,2,1,0:T(8,128)(2,1)} %get-tuple-element.103) | copy-start | bytes 1179652
  79.9 11.1 %slice-start.5 = ((s8[4718592]{0:T(1024)(128)(4,1)}), s8[524288]{0:T(1024)(128)(4,1)S(1)}, s32[]{:S(2)}) async-start(s8[4718592]{0:T(1024)(128)(4,1)} %bitcast.245), calls=%async_computation.15 | async-start | bytes 1048576
  79.9 13.1 %slice-start.1 = ((s8[4718592]{0:T(1024)(128)(4,1)}), s8[524288]{0:T(1024)(128)(4,1)S(1)}, s32[]{:S(2)}) async-start(s8[4718592]{0:T(1024)(128)(4,1)} %bitcast.241), calls=%async_computation.11 | async-start | bytes 1048576
  79.9 14.6 %slice-start.3 = ((s8[4718592]{0:T(1024)(128)(4,1)}), s8[524288]{0:T(1024)(128)(4,1)S(1)}, s32[]{:S(2)}) async-start(s8[4718592]{0:T(1024)(128)(4,1)} %bitcast.243), calls=%async_computation.13 | async-start | bytes 1048576
  93.0 10.5 %slice-start.6 = ((s8[4718592]{0:T(1024)(128)(4,1)}), s8[4194304]{0:T(1024)(128)(4,1)S(1)}, s32[]{:S(2)}) async-start(s8[4718592]{0:T(1024)(128)(4,1)} %bitcast.247), calls=%async_computation.16 | async-start | bytes 8388608
  94.5 9.0 %copy-start.17 = (bf16[2,1,128,768]{3,2,1,0:T(8,128)(2,1)S(1)}, bf16[2,1,128,768]{3,2,1,0:T(8,128)(2,1)}, u32[]{:S(2)}) copy-start(bf16[2,1,128,768]{3,2,1,0:T(8,128)(2,1)} %get-tuple-element.104) | copy-start | bytes 1179652
  94.5 9.0 %slice-start.7 = ((s8[4718592]{0:T(1024)(128)(4,1)}), s8[524288]{0:T(1024)(128)(4,1)S(1)}, s32[]{:S(2)}) async-start(s8[4718592]{0:T(1024)(128)(4,1)} %bitcast.247), calls=%async_computation.17 | async-start | bytes 1048576
  105.6 1.5 copy-start.19
  108.1 14.5 %all-to-all-start.3 = ((bf16[2,2,128,768]{3,2,1,0:T(8,128)(2,1)}), bf16[2,2,128,768]{3,2,1,0:T(8,128)(2,1)}, u32[]{:S(2)}, u32[]{:S(2)}) async-start(bf16[2,2,128,768]{3,2,1,0:T(8,128)(2,1)} %copy.66), calls=%async_computation.4 | async-start | bytes 1572864 | tf_op jit(solution)/shard_map/all_to_all | solution.py:43
  112.4 111.2 %all-reduce.9.cloned.1.call-start = ((), (), s32[]{:S(2)}) async-start(), calls=%async_computation.9 | async-start | bytes 2359296 | tf_op jit(solution)/shard_map/psum | solution.py:264
  122.6 3.2 copy-start.2
  122.6 4.2 copy-start.9
  122.6 12.1 %copy-start.25 = (bf16[3,512,64]{1,2,0:T(8,128)(2,1)S(1)}, bf16[3,512,64]{1,2,0:T(8,128)(2,1)}, u32[]{:S(2)}) copy-start(bf16[3,512,64]{1,2,0:T(8,128)(2,1)} %copy-done.24) | copy-start | bytes 589828
  134.7 2.1 copy-start.21
  136.8 2.7 copy-start.28
  137.5 1.5 copy-start.14
  138.4 1.2 copy-start.23
  139.6 1.6 copy-start.30
  141.1 3.1 copy-start.12
  141.2 107.5 %reduce-scatter.5.cloned.1.call-start = ((), (), s32[]{:S(2)}) async-start(), calls=%async_computation.7 | async-start | bytes 983040 | tf_op jit(solution)/shard_map/reduce_scatter | solution.py:253
  143.9 5.5 %copy-start.6 = (bf16[256,3072]{1,0:T(8,128)(2,1)S(1)}, bf16[256,3072]{1,0:T(8,128)(2,1)}, u32[]{:S(2)}) copy-start(bf16[256,3072]{1,0:T(8,128)(2,1)} %get-tuple-element.96) | copy-start | bytes 4718596
  143.9 5.5 %copy-start.18 = (bf16[2,1,128,768]{3,2,1,0:T(8,128)(2,1)S(1)}, bf16[2,1,128,768]{3,2,1,0:T(8,128)(2,1)}, u32[]{:S(2)}) copy-start(bf16[2,1,128,768]{3,2,1,0:T(8,128)(2,1)} %get-tuple-element.104) | copy-start | bytes 1179652
  143.9 294.6 %all-reduce.7.cloned.1.call-start = ((), (), s32[]{:S(2)}) async-start(), calls=%async_computation.8 | async-start | bytes 18874368 | tf_op jit(solution)/shard_map/psum | solution.py:192
  153.1 1.4 copy-start.37
  162.0 18.6 %copy-start.3 = (f32[128,768]{1,0:T(8,128)S(1)}, f32[128,768]{1,0:T(8,128)}, u32[]{:S(2)}) copy-start(f32[128,768]{1,0:T(8,128)} %copy-done.1) | copy-start | bytes 1179652
  163.0 17.2 %all-to-all-start.1 = ((bf16[2,2,128,768]{3,2,1,0:T(8,128)(2,1)}), bf16[2,2,128,768]{3,2,1,0:T(8,128)(2,1)S(1)}, u32[]{:S(2)}, u32[]{:S(2)}) async-start(bf16[2,2,128,768]{3,2,1,0:T(8,128)(2,1)} %copy.65), calls=%async_computation.2 | async-start | bytes 1572864 | tf_op jit(solution)/shard_map/all_to_all | solution.py:43
  180.2 68.4 %copy-start.4 = (bf16[1,128,768]{2,1,0:T(8,128)(2,1)S(1)}, bf16[1,128,768]{2,1,0:T(8,128)(2,1)}, u32[]{:S(2)}) copy-start(bf16[1,128,768]{2,1,0:T(8,128)(2,1)} %param.18) | copy-start | bytes 589828
  180.2 68.4 %copy-start.31 = (f32[768]{0:T(1024)S(1)}, f32[768]{0:T(1024)}, u32[]{:S(2)}) copy-start(f32[768]{0:T(1024)} %param.23) | copy-start | bytes 9220
  180.6 112.6 %copy-start.8 = (f32[128,768]{1,0:T(8,128)S(1)}, f32[128,768]{1,0:T(8,128)}, u32[]{:S(2)}) copy-start(f32[128,768]{1,0:T(8,128)} %copy-done.7) | copy-start | bytes 1179652
  180.6 112.6 %copy-start.10 = (bf16[1,128,768]{2,1,0:T(8,128)(2,1)S(1)}, bf16[1,128,768]{2,1,0:T(8,128)(2,1)}, u32[]{:S(2)}) copy-start(bf16[1,128,768]{2,1,0:T(8,128)(2,1)} %param.35) | copy-start | bytes 589828
  438.5 7.5 %copy-start.5 = (bf16[1,3072,768]{2,1,0:T(8,128)(2,1)S(1)}, bf16[1,3072,768]{2,1,0:T(8,128)(2,1)}, u32[]{:S(2)}) copy-start(bf16[1,3072,768]{2,1,0:T(8,128)(2,1)} %get-tuple-element.87) | copy-start | bytes 14155780
  (6 other events, 4.7 us)
Sparse Core Ops, SparseCore 0:
  31.1 28.8 reduce-scatter.2
  141.3 82.3 all-reduce.8
  226.2 22.3 reduce-scatter.4
  252.8 185.7 all-reduce.6
where the time goes:
time: 458 us; the launch traced here: 457 us
  waiting for transfers between devices  253 us (55%)
  matrix products  63.5 us (14%)
  blocking collectives  59.5 us (13%)
  other arithmetic  34.8 us (8%)
  starting transfers between devices  17.1 us (4%)
  local copies, waits for them, and re-layouts  14.9 us (3%)
  between operations  14.5 us (3%)
    psum x1, waiting for transfers between devices, local(): lax.psum(grad_in.astype(jnp.bfloat16), ('tp', 'dp')).astype(jnp.float32)  143 us
    dot_general x23, matrix products, contract(): lax.dot_general(left, right, (((left_dim,), (right_dim,)), ((), ())), pre...  59.8 us
    psum x1, waiting for transfers between devices, local(): lax.psum(joined_grad[:, :head_cols].astype(jnp.bfloat16), ('ep', 'dp'))  42.1 us
    psum x1, blocking collectives, local(): lax.psum((local_counts, ln1_gain_grad, ln1_bias_grad, ln2_gain_grad, ln2_...  41.6 us
    all_to_all x2, waiting for transfers between devices, to_sources(): return lax.all_to_all(buffer, 'ep', split_axis=0, concat_axis=0, tiled=True)  23.7 us
    reduce_scatter x1, waiting for transfers between devices, local(): lax.psum_scatter(contract(projected_grad, joined, 1, 1).astype(jnp.bfloat...  17.7 us
    reduce_scatter x1, waiting for transfers between devices, local(): lax.psum_scatter(contract(attn_heads, out_weight, 1, 0), 'tp', scatter_di...  16.9 us
    all_gather x1, blocking collectives, local(): piece = lax.all_gather(first_normed, 'tp', axis=0, tiled=True)  10.1 us
  transfers between devices with their start and end apart: 8, of which 7 were waited for; matrix products, arithmetic and copies ran while one was open for 10% of the time, Pallas kernels for 0%

commit v1 on v0

--- a/solution.py
+++ b/solution.py
@@ -1,14 +1,453 @@
+import functools
+import math
+
 import jax
 import jax.numpy as jnp
 from jax import lax
+from jax.experimental import pallas as pl
+from jax.experimental.pallas import tpu as pltpu
 from jax.sharding import PartitionSpec as P
 
 HD = 64
 EXP_DEV = 2
-
-
 EPSILON = 1e-05
 MASKED = -1e30
+MESH = pl.DeviceIdType.MESH
+BF = jnp.bfloat16
+F32 = jnp.float32
+CHUNK = 64
+
+
+def tp_peers():
+    me = lax.axis_index("tp")
+    one = me + 1 - 2 * (me % 2)
+    return (me, one, (me + 2) % 4, (one + 2) % 4)
+
+
+def remote(src, dst, send, recv, where):
+    return pltpu.make_async_remote_copy(
+        src_ref=src, dst_ref=dst, send_sem=send, recv_sem=recv,
+        device_id=where, device_id_type=MESH,
+    )
+
+
+def entry_barrier(ep_count, dp_count):
+    barrier = pltpu.get_barrier_semaphore()
+    _, tp1, tp2, tp3 = tp_peers()
+    ep, dp = lax.axis_index("ep"), lax.axis_index("dp")
+    for peer in (tp1, tp2, tp3):
+        pl.semaphore_signal(barrier, inc=1, device_id={"tp": peer}, device_id_type=MESH)
+    for off in range(1, ep_count):
+        pl.semaphore_signal(
+            barrier, inc=1, device_id={"ep": (ep + off) % ep_count}, device_id_type=MESH
+        )
+    for off in range(1, dp_count):
+        pl.semaphore_signal(
+            barrier, inc=1, device_id={"dp": (dp + off) % dp_count}, device_id_type=MESH
+        )
+    pl.semaphore_wait(barrier, 3 + ep_count - 1 + dp_count - 1)
+
+
+def gelu_pair(hidden):
+    phi = 0.5 * (1.0 + lax.erf(hidden * math.sqrt(0.5)))
+    dens = jnp.exp(-0.5 * hidden * hidden) * (1.0 / math.sqrt(2.0 * math.pi))
+    return hidden * phi, phi + hidden * dens
+
+
+def grads_kernel(
+    ep_count, dp_count, n,
+    xs_ref, w_in_hbm, w_out_hbm, pg_ref, small_ref,
+    rg_hbm, full_ref, small_out,
+    gx, gs, w_in, w_out, act, slope, own, red, stage, fin, pslot, acc1, dslot, acc2, sm_tp, sm_ep, sm_dp, sm_a, sm_b,
+    g_send, g_recv, w_sem, red_send, red_recv, bc_send, bc_recv, x_send, x_recv, out_sem,
+    p_send, p_recv, d_send, d_recv, e_send, e_recv, f_send, f_recv, s_send, s_recv,
+):
+    tp, tp1, tp2, tp3 = tp_peers()
+    ep, dp = lax.axis_index("ep"), lax.axis_index("dp")
+    last = dp_count - 1
+    quarter = w_in.shape[1]
+    width = w_in.shape[0]
+    start = pl.multiple_of(tp * quarter, quarter)
+    in_copy = pltpu.make_async_copy(w_in_hbm.at[:, pl.ds(start, quarter)], w_in, w_sem.at[0])
+    out_copy = pltpu.make_async_copy(w_out_hbm.at[pl.ds(start, quarter), :], w_out, w_sem.at[1])
+    in_copy.start()
+    out_copy.start()
+    entry_barrier(ep_count, dp_count)
+
+    token_copies = {}
+    for part, buf in ((0, gx), (1, gs)):
+        for hop, peer in ((1, tp1), (2, tp2)):
+            token_copies[part, hop] = remote(
+                xs_ref.at[part], buf.at[hop], g_send.at[part, hop - 1], g_recv.at[part, hop - 1], {"tp": peer}
+            )
+            token_copies[part, hop].start()
+    ep_copies = []
+    for off in range(1, ep_count):
+        peer = (ep + off) % ep_count
+        ep_copies.append(
+            remote(pg_ref.at[peer], pslot.at[off - 1], p_send.at[off - 1], p_recv.at[off - 1], {"ep": peer})
+        )
+        ep_copies[-1].start()
+    small_copies = []
+    for hop, peer in ((1, tp1), (2, tp2), (3, tp3)):
+        small_copies.append(
+            remote(small_ref, sm_tp.at[hop - 1], s_send.at[hop - 1], s_recv.at[hop - 1], {"tp": peer})
+        )
+        small_copies[-1].start()
+
+    gx[0] = xs_ref[0]
+    gs[0] = xs_ref[1]
+    in_copy.wait()
+    out_copy.wait()
+
+    def hidden_block(index):
+        rows = gx.shape[1]
+        hidden = jnp.dot(gx[index], w_in[...], preferred_element_type=F32)
+        through = lax.dot_general(gs[index], w_out[...], (((1,), (1,)), ((), ())), preferred_element_type=F32)
+        value, grad = gelu_pair(hidden)
+        act[pl.ds(index * rows, rows), :] = value.astype(BF)
+        slope[pl.ds(index * rows, rows), :] = (through * grad).astype(BF)
+
+    hidden_block(0)
+    for part in (0, 1):
+        token_copies[part, 1].wait_recv()
+    hidden_block(1)
+    forward = []
+    for part, buf in ((0, gx), (1, gs)):
+        token_copies[part, 2].wait_recv()
+        forward.append(remote(buf.at[2], buf.at[3], g_send.at[part, 2], g_recv.at[part, 2], {"tp": tp1}))
+        forward[-1].start()
+    hidden_block(2)
+    for copy in forward:
+        copy.wait_recv()
+    hidden_block(3)
+
+    for copy in small_copies:
+        copy.wait()
+    sm_a[...] = small_ref[...] + sm_tp[0] + sm_tp[1] + sm_tp[2]
+    small_ep = []
+    for off in range(1, ep_count):
+        small_ep.append(
+            remote(sm_a, sm_ep.at[off - 1], s_send.at[2 + off], s_recv.at[2 + off], {"ep": (ep + off) % ep_count})
+        )
+        small_ep[-1].start()
+    for copy in ep_copies:
+        copy.wait()
+    total = pg_ref[ep].astype(F32)
+    for off in range(1, ep_count):
+        total = total + pslot[off - 1].astype(F32)
+    acc1[...] = total.astype(BF)
+    dp_copies = []
+    for off in range(1, dp_count):
+        peer = (dp + off) % dp_count
+        dp_copies.append(
+            remote(acc1.at[peer], dslot.at[off - 1], d_send.at[off - 1], d_recv.at[off - 1], {"dp": peer})
+        )
+        dp_copies[-1].start()
+
+    step_rows = 2 * CHUNK
+
+    def outer(index, _):
+        rows = pl.ds(pl.multiple_of(index * step_rows, step_rows), step_rows)
+        x_all = gx[:, :, rows].reshape(-1, step_rows)
+        s_all = gs[...].reshape(-1, width)
+        piece = lax.dot_general(x_all, slope[...], (((0,), (0,)), ((), ())), preferred_element_type=F32)
+        own[0, rows, :] = piece
+        piece = lax.dot_general(act[:, rows], s_all, (((0,), (0,)), ((), ())), preferred_element_type=F32)
+        own[1, rows, :] = piece
+        return 0
+
+    for index in range(width // step_rows):
+        outer(index, 0)
+
+    for copy in small_ep:
+        copy.wait()
+    total = sm_a[...]
+    for off in range(1, ep_count):
+        total = total + sm_ep[off - 1]
+    sm_b[...] = total
+    small_dp = []
+    for off in range(1, dp_count):
+        slot = 2 + ep_count - 1 + off
+        small_dp.append(
+            remote(sm_b, sm_dp.at[off - 1], s_send.at[slot], s_recv.at[slot], {"dp": (dp + off) % dp_count})
+        )
+        small_dp[-1].start()
+
+    def chain(half):
+        place = last - dp if half == 0 else dp
+        onward = (dp + last) % dp_count if half == 0 else (dp + 1) % dp_count
+        backward = (dp + 1) % dp_count if half == 0 else (dp + last) % dp_count
+        return place, onward, backward
+
+    def red_copy(half, index, onward):
+        return remote(
+            stage.at[half, index], red.at[half, index], red_send.at[half, index], red_recv.at[half, index],
+            {"dp": onward},
+        )
+
+    def bc_copy(half, index, backward):
+        return remote(
+            fin.at[half, index, 0], fin.at[half, index, 0], bc_send.at[half, index], bc_recv.at[half, index],
+            {"dp": backward},
+        )
+
+    def x_copy(half, index, hop):
+        source, peer = ((0, tp1), (0, tp2), (2, tp1))[hop - 1]
+        return remote(
+            fin.at[half, index, source], fin.at[half, index, hop],
+            x_send.at[hop - 1, half, index], x_recv.at[hop - 1, half, index], {"tp": peer},
+        )
+
+    def out_copy_of(half, index):
+        return pltpu.make_async_copy(fin.at[half, index], rg_hbm.at[half, index], out_sem.at[half, index])
+
+    def step(s, _):
+        for half in (0, 1):
+            place, onward, backward = chain(half)
+            index = s - place
+            rows = pl.ds(pl.multiple_of(index * CHUNK, CHUNK), CHUNK)
+
+            @pl.when((index >= 0) & (index < n))
+            def _():
+                @pl.when(place == 0)
+                def _():
+                    stage[half, index] = own[half, rows, :].astype(BF)
+
+                @pl.when(place > 0)
+                def _():
+                    red_copy(half, index, onward).wait_recv()
+                    total = (own[half, rows, :] + red[half, index].astype(F32)).astype(BF)
+
+                    @pl.when(place < last)
+                    def _():
+                        stage[half, index] = total
+
+                    @pl.when(place == last)
+                    def _():
+                        fin[half, index, 0] = total
+
+                @pl.when(place < last)
+                def _():
+                    red_copy(half, index, onward).start()
+
+        for half in (0, 1):
+            place, onward, backward = chain(half)
+            far = last - place
+            done = s - last - far
+
+            @pl.when((done >= 0) & (done < n))
+            def _():
+                @pl.when(far > 0)
+                def _():
+                    bc_copy(half, done, backward).wait_recv()
+
+                @pl.when(far < last)
+                def _():
+                    bc_copy(half, done, backward).start()
+
+                x_copy(half, done, 1).start()
+                x_copy(half, done, 2).start()
+
+            second = done - 1
+
+            @pl.when((second >= 0) & (second < n))
+            def _():
+                x_copy(half, second, 2).wait_recv()
+                x_copy(half, second, 3).start()
+
+            third = done - 2
+
+            @pl.when((third >= 0) & (third < n))
+            def _():
+                x_copy(half, third, 1).wait_recv()
+                x_copy(half, third, 3).wait_recv()
+                out_copy_of(half, third).start()
+
+        return 0
+
+    mid = last + 3
+    lax.fori_loop(0, mid, step, 0)
+
+    for copy in dp_copies:
+        copy.wait()
+    total = acc1[dp].astype(F32)
+    for off in range(1, dp_count):
+        total = total + dslot[off - 1].astype(F32)
+    acc2[...] = total.astype(BF)
+    full_ref[ep, dp] = acc2[...]
+    dp_gather = []
+    for off in range(1, dp_count):
+        dp_gather.append(
+            remote(
+                acc2, full_ref.at[ep, dp], e_send.at[off - 1], e_recv.at[off - 1], {"dp": (dp + off) % dp_count}
+            )
+        )
+        dp_gather[-1].start()
+    for copy in small_dp:
+        copy.wait()
+    total = sm_b[...]
+    for off in range(1, dp_count):
+        total = total + sm_dp[off - 1]
+    small_out[...] = total
+
+    lax.fori_loop(mid, mid + 5, step, 0)
+    for off in range(1, dp_count):
+        source = (dp + dp_count - off) % dp_count
+        dp_gather[off - 1].wait_send()
+        remote(
+            acc2, full_ref.at[ep, source], e_send.at[off - 1], e_recv.at[off - 1], {"dp": source}
+        ).wait_recv()
+    ep_gather = []
+    for off in range(1, ep_count):
+        ep_gather.append(
+            remote(
+                full_ref.at[ep], full_ref.at[ep], f_send.at[off - 1], f_recv.at[off - 1],
+                {"ep": (ep + off) % ep_count},
+            )
+        )
+        ep_gather[-1].start()
+    lax.fori_loop(mid + 5, n + 2 * last + 2, step, 0)
+    for off in range(1, ep_count):
+        source = (ep + ep_count - off) % ep_count
+        ep_gather[off - 1].wait_send()
+        remote(
+            full_ref.at[source], full_ref.at[source], f_send.at[off - 1], f_recv.at[off - 1], {"ep": source}
+        ).wait_recv()
+
+    for copy in token_copies.values():
+        copy.wait_send()
+    for copy in forward:
+        copy.wait_send()
+
+    def drain(index, _):
+        for half in (0, 1):
+            place, onward, backward = chain(half)
+
+            @pl.when(place < last)
+            def _():
+                red_copy(half, index, onward).wait_send()
+
+            @pl.when(place > 0)
+            def _():
+                bc_copy(half, index, backward).wait_send()
+
+            for hop in (1, 2, 3):
+                x_copy(half, index, hop).wait_send()
+            out_copy_of(half, index).wait()
+        return 0
+
+    lax.fori_loop(0, n, drain, 0)
+
+
+def reduce_grads(xs, w_in, w_out, proj, small):
+    ep_count, dp_count = lax.axis_size("ep"), lax.axis_size("dp")
+    _, rows, width = xs.shape
+    hidden = w_in.shape[1]
+    quarter = hidden // 4
+    n = width // CHUNK
+    assert quarter == width
+    shard = width // (ep_count * dp_count)
+    pg = proj.reshape(ep_count, dp_count, shard, width)
+    dma = pltpu.SemaphoreType.DMA
+    vmem = pl.BlockSpec(memory_space=pltpu.VMEM)
+    hbm = pl.BlockSpec(memory_space=pl.ANY)
+    many = 2 + (ep_count - 1) + (dp_count - 1) + 1
+    return pl.pallas_call(
+        functools.partial(grads_kernel, ep_count, dp_count, n),
+        out_shape=(
+            jax.ShapeDtypeStruct((2, n, 4, CHUNK, width), BF),
+            jax.ShapeDtypeStruct(pg.shape, BF),
+            jax.ShapeDtypeStruct(small.shape, F32),
+        ),
+        in_specs=[vmem, hbm, hbm, vmem, vmem],
+        out_specs=(hbm, vmem, vmem),
+        scratch_shapes=[
+            pltpu.VMEM((4, rows, width), BF),
+            pltpu.VMEM((4, rows, width), BF),
+            pltpu.VMEM((width, quarter), BF),
+            pltpu.VMEM((quarter, width), BF),
+            pltpu.VMEM((4 * rows, quarter), BF),
+            pltpu.VMEM((4 * rows, quarter), BF),
+            pltpu.VMEM((2, width, width), F32),
+            pltpu.VMEM((2, n, CHUNK, width), BF),
+            pltpu.VMEM((2, n, CHUNK, width), BF),
+            pltpu.VMEM((2, n, 4, CHUNK, width), BF),
+            pltpu.VMEM((ep_count - 1, dp_count, shard, width), BF),
+            pltpu.VMEM((dp_count, shard, width), BF),
+            pltpu.VMEM((dp_count - 1, shard, width), BF),
+            pltpu.VMEM((shard, width), BF),
+            pltpu.VMEM((3,) + small.shape, F32),
+            pltpu.VMEM((ep_count - 1,) + small.shape, F32),
+            pltpu.VMEM((dp_count - 1,) + small.shape, F32),
+            pltpu.VMEM(small.shape, F32),
+            pltpu.VMEM(small.shape, F32),
+            dma((2, 3)), dma((2, 3)), dma((2,)),
+            dma((2, n)), dma((2, n)), dma((2, n)), dma((2, n)),
+            dma((3, 2, n)), dma((3, 2, n)), dma((2, n)),
+            dma((ep_count - 1,)), dma((ep_count - 1,)),
+            dma((dp_count - 1,)), dma((dp_count - 1,)),
+            dma((dp_count - 1,)), dma((dp_count - 1,)),
+            dma((ep_count - 1,)), dma((ep_count - 1,)),
+            dma((many,)), dma((many,)),
+        ],
+        compiler_params=pltpu.CompilerParams(
+            collective_id=0, has_side_effects=True, vmem_limit_bytes=60 * 1024 * 1024
+        ),
+        name="grads",
+    )(xs, w_in, w_out, pg, small)
+
+
+def finish_kernel(tp_ref, rg_ref, full_ref, gin_ref, gout_ref, q_ref, k_ref, v_ref, o_ref):
+    width = gin_ref.shape[0]
+    gin_ref[...] = rg_ref[0, :, 0].reshape(width, -1).astype(F32)
+    gout_ref[...] = rg_ref[1, :, 0].reshape(-1, width).astype(F32)
+
+    @pl.when(pl.program_id(0) == 0)
+    def _():
+        cols = q_ref.shape[1]
+        for index, ref in enumerate((q_ref, k_ref, v_ref)):
+            ref[...] = full_ref[:, index * cols : (index + 1) * cols].astype(F32)
+        o_ref[...] = full_ref[:, 3 * cols :].astype(F32).T
+
+
+def finish(rg, full, cols):
+    _, n, _, chunk, width = rg.shape
+    hidden = 4 * width
+    me = lax.axis_index("tp").astype(jnp.int32).reshape(1)
+
+    def where(quarter, me_ref):
+        mine = me_ref[0]
+        low = (quarter % 2) != (mine % 2)
+        high = (quarter // 2) != (mine // 2)
+        return jnp.where(low, 1, 0) + jnp.where(high, 2, 0)
+
+    whole = lambda shape: pl.BlockSpec(shape, lambda q, t: (0, 0))
+    return pl.pallas_call(
+        finish_kernel,
+        grid_spec=pltpu.PrefetchScalarGridSpec(
+            num_scalar_prefetch=1,
+            grid=(4,),
+            in_specs=[
+                pl.BlockSpec((2, n, 1, chunk, width), lambda q, t: (0, 0, where(q, t), 0, 0)),
+                whole((width, width)),
+            ],
+            out_specs=[
+                pl.BlockSpec((width, width), lambda q, t: (0, q)),
+                pl.BlockSpec((width, width), lambda q, t: (q, 0)),
+                whole((width, cols)), whole((width, cols)), whole((width, cols)), whole((cols, width)),
+            ],
+        ),
+        out_shape=[
+            jax.ShapeDtypeStruct((width, hidden), F32),
+            jax.ShapeDtypeStruct((hidden, width), F32),
+            jax.ShapeDtypeStruct((width, cols), F32),
+            jax.ShapeDtypeStruct((width, cols), F32),
+            jax.ShapeDtypeStruct((width, cols), F32),
+            jax.ShapeDtypeStruct((cols, width), F32),
+        ],
+        name="finish",
+    )(me, rg, full.reshape(width, width))
 
 
 def layer_norm(values, gain, bias):
@@ -53,9 +492,7 @@
     through = contract(upstream, outer, 1, 1)
     slope = jax.vjp(gelu_exact, hidden)[1](through)[0].astype(jnp.bfloat16)
     back_in = contract(slope, inner, 1, 1)
-    if trainable:
-        return (back_in, contract(inputs, slope, 0, 0), contract(active, upstream, 0, 0))
-    return (back_in, None, None)
+    return back_in
 
 
 def local(
@@ -170,11 +607,9 @@
     ).astype(jnp.bfloat16)
     back_arrived = to_owners(back_send.reshape(ep_count, EXP_DEV, capacity, width))
     input_terms = []
-    grad_in = None
-    grad_out = None
     for index in range(EXP_DEV):
         inputs, hidden, active = kept[index]
-        back_in, maybe_in, maybe_out = expert_backward(
+        back_in = expert_backward(
             inputs,
             hidden,
             active,
@@ -183,15 +618,9 @@
             outer_list[index],
             index == EXP_DEV - 1,
         )
-        if index == EXP_DEV - 1:
-            grad_in, grad_out = (maybe_in, maybe_out)
         input_terms.append(back_in.reshape(ep_count, -1, width))
     input_terms = jnp.stack(input_terms, axis=1)
     back_returned = to_sources(input_terms.astype(jnp.bfloat16)).reshape(slots, width)
-    grad_in, grad_out = (
-        lax.psum(grad_in.astype(jnp.bfloat16), ("tp", "dp")).astype(jnp.float32),
-        lax.psum(grad_out.astype(jnp.bfloat16), ("tp", "dp")).astype(jnp.float32),
-    )
     second_grad = contract(pick_first, back_returned, 1, 0) + contract(
         pick_second, back_returned, 1, 0
     )
@@ -260,20 +689,17 @@
         1
     ](first_grad)
     tokens_grad = middle_grad + residual_part
-    summed = (
-        lax.psum(joined_grad[:, :head_cols].astype(jnp.bfloat16), ("ep", "dp")).astype(jnp.float32),
-        lax.psum(
-            joined_grad[:, head_cols : 2 * head_cols].astype(jnp.bfloat16), ("ep", "dp")
-        ).astype(jnp.float32),
-        lax.psum(joined_grad[:, 2 * head_cols :].astype(jnp.bfloat16), ("ep", "dp")).astype(
-            jnp.float32
-        ),
-        lax.psum(out_part.astype(jnp.bfloat16), ("ep", "dp")).astype(jnp.float32),
-    )
-    counts, gain_one, bias_one, gain_two, bias_two = lax.psum(
-        (local_counts, ln1_gain_grad, ln1_bias_grad, ln2_gain_grad, ln2_bias_grad),
-        ("tp", "ep", "dp"),
-    )
+    proj = jnp.concatenate([joined_grad, out_part.T], axis=1).astype(jnp.bfloat16)
+    counts_row = jnp.zeros((width,), jnp.float32).at[:experts].set(local_counts)
+    small = jnp.stack(
+        [ln1_gain_grad, ln1_bias_grad, ln2_gain_grad, ln2_bias_grad, counts_row]
+        + [jnp.zeros((width,), jnp.float32)] * 3
+    )
+    xs = jnp.stack([kept[-1][0], back_arrived[:, EXP_DEV - 1].reshape(-1, width)])
+    rg, full, sums = reduce_grads(xs, train_in[0], train_out[0], proj, small)
+    grad_in, grad_out, *summed = finish(rg, full, head_cols)
+    gain_one, bias_one, gain_two, bias_two = sums[0], sums[1], sums[2], sums[3]
+    counts = sums[4, :experts]
     return (
         layer_out[None],
         tokens_grad[None],

time: 458 us -> 336 us (0.73); the launches traced: 457 us -> 329 us
  waiting for transfers between devices: 253 us -> 35.9 us
  Pallas kernels: 0 us -> 144 us
  blocking collectives: 59.5 us -> 17.9 us
  other arithmetic: 34.8 us -> 17.5 us
  local copies, waits for them, and re-layouts: 14.9 us -> 23.9 us
  matrix products: 63.5 us -> 57.7 us
    psum x2 -> x0, waiting for transfers between devices: 186 us -> none  [the longest x1 143 us: local(): lax.psum(grad_in.astype(jnp.bfloat16), ('tp', 'dp')).astype(jnp.float32)]
    pallas_call x0 -> x2, Pallas kernels: none -> 144 us  [the longest x1 132 us: reduce_grads(): pl.pallas_call(functools.partial(grads_kernel, ep_count, dp_count, n), ou...]
    psum x1 -> x0, blocking collectives: 41.6 us -> none  [local(): lax.psum((local_counts, ln1_gain_grad, ln1_bias_grad, ln2_gain_grad, ln2_...]
    reduce_scatter x1, waiting for transfers between devices: 17.7 us -> 1.91 us  [local(): lax.psum_scatter(contract(projected_grad, joined, 1, 1).astype(jnp.bfloat...]
    all_to_all x2, waiting for transfers between devices: 23.7 us -> 8.17 us  [to_sources(): return lax.all_to_all(buffer, 'ep', split_axis=0, concat_axis=0, tiled=True)]
    broadcast_in_dim x2 -> x0, other arithmetic: 12 us -> none  [the longest x1 7.52 us: local(): grad_in[None]]
    convert_element_type x4 -> x0, other arithmetic: 7.26 us -> none  [the longest x1 1.81 us: local(): lax.psum(joined_grad[:, 2 * head_cols:].astype(jnp.bfloat16), ('ep', 'dp'))]
    dot_general x23 -> x21, matrix products: 59.8 us -> 53.9 us  [contract(): lax.dot_general(left, right, (((left_dim,), (right_dim,)), ((), ())), pre...]
  transfers between devices with their start and end apart: 8 -> 6, of which waited for: 7 -> 5; matrix products, arithmetic and copies ran while one was open for 10% -> 10% of each run, Pallas kernels for 0% -> 0%
where the time goes in v1:
time: 336 us; the launch traced here: 329 us
  Pallas kernels  144 us (43%)
  matrix products  57.7 us (17%)
  waiting for transfers between devices  35.9 us (11%)
  local copies, waits for them, and re-layouts  23.9 us (7%)
  blocking collectives  17.9 us (5%)
  other arithmetic  17.5 us (5%)
  starting transfers between devices  16.8 us (5%)
  between operations  15.4 us (5%)
    pallas_call x1, Pallas kernels, reduce_grads(): pl.pallas_call(functools.partial(grads_kernel, ep_count, dp_count, n), ou...  132 us
    dot_general x21, matrix products, contract(): lax.dot_general(left, right, (((left_dim,), (right_dim,)), ((), ())), pre...  53.9 us
    reduce_scatter x1, waiting for transfers between devices, local(): lax.psum_scatter(contract(attn_heads, out_weight, 1, 0), 'tp', scatter_di...  16.9 us
    unnamed x104, local copies, waits for them, and re-layouts  12.8 us
    pallas_call x1, Pallas kernels, finish(): pl.pallas_call(finish_kernel, grid_spec=pltpu.PrefetchScalarGridSpec(num_...  12.2 us
    all_gather x1, blocking collectives, local(): piece = lax.all_gather(first_normed, 'tp', axis=0, tiled=True)  10.1 us
    all_to_all x2, waiting for transfers between devices, to_owners(): return lax.all_to_all(buffer, 'ep', split_axis=0, concat_axis=0, tiled=True)  8.91 us
    all_to_all x2, starting transfers between devices, to_owners(): return lax.all_to_all(buffer, 'ep', split_axis=0, concat_axis=0, tiled=True)  8.82 us
  transfers between devices with their start and end apart: 6, of which 5 were waited for; matrix products, arithmetic and copies ran while one was open for 10% of the time, Pallas kernels for 0%

profile of v1, /device:TPU:0, one launch (start us, length us, event | category | flops | bytes accessed | tf_op | source)
XLA Modules:
  0.0 329.0 jit_solution(845064628629984305)
XLA Ops:
  8.9 1.0 convert_reduce_fusion.1
  9.9 1.1 fusion.76
  11.1 1.1 fusion.75
  12.2 10.1 %all_gather.6 = bf16[512,768]{1,0:T(8,128)(2,1)S(1)} all-gather(bf16[128,768]{1,0:T(8,128)(2,1)S(1)} %fusion.75), channel_id=1, replica_groups=mesh['tp'=4,'ep'=2,'dp'=4] {'tp'}, dimensions={0}, use_global_device_ids=true | all-gather | bytes 983040 | tf_op jit(solution)/shard_map/all_gather | solution.py:528
  22.3 1.2 constant_dynamic-update-slice_fusion.2
  29.4 1.6 fusion.129
  31.3 1.2 reduce-window.6
  34.9 1.4 fusion.83
  36.4 2.4 add_convert_fusion.2
  38.7 4.3 %all-to-all-start.2 = ((bf16[2,2,128,768]{3,2,1,0:T(8,128)(2,1)}), bf16[2,2,128,768]{3,2,1,0:T(8,128)(2,1)}, u32[]{:S(2)}, u32[]{:S(2)}) async-start(bf16[2,2,128,768]{3,2,1,0:T(8,128)(2,1)} %bitcast.230), calls=%async_computation.3 | async-start | bytes 1572864 | tf_op jit(solution)/shard_map/all_to_all | solution.py:478
  43.1 16.9 %reduce-scatter.3.cloned.1.call-done = f32[128,768]{1,0:T(8,128)} async-done(((f32[512,768]{1,0:T(8,128)}), f32[128,768]{1,0:T(8,128)}) %reduce-scatter.3.cloned.1.call-update) | async-done | bytes 393232 | tf_op jit(solution)/shard_map/reduce_scatter | solution.py:567
  59.9 1.2 fusion.123
  61.8 1.4 convolution_convert_fusion.2
  63.2 4.5 %all-to-all-start = ((bf16[2,2,128,768]{3,2,1,0:T(8,128)(2,1)}), bf16[2,2,128,768]{3,2,1,0:T(8,128)(2,1)}, u32[]{:S(2)}, u32[]{:S(2)}) async-start(bf16[2,2,128,768]{3,2,1,0:T(8,128)(2,1)} %bitcast.229), calls=%async_computation.1 | async-start | bytes 1572864 | tf_op jit(solution)/shard_map/all_to_all | solution.py:478
  67.7 2.0 fusion.125
  69.8 8.9 %all-to-all-done = bf16[2,2,128,768]{3,2,1,0:T(8,128)(2,1)} async-done(((bf16[2,2,128,768]{3,2,1,0:T(8,128)(2,1)}), bf16[2,2,128,768]{3,2,1,0:T(8,128)(2,1)}, u32[]{:S(2)}, u32[]{:S(2)}) %all-to-all-start) | async-done | bytes 786464 | tf_op jit(solution)/shard_map/all_to_all | solution.py:478
  78.7 1.3 fusion.126
  80.1 11.0 %multiply_convert_fusion.2 = (bf16[256,3072]{1,0:T(8,128)(2,1)}, f32[256,3072]{1,0:T(8,128)S(1)}, f32[256,3072]{1,0:T(8,128)S(1)}) fusion(bf16[256,768]{1,0:T(8,128)(2,1)S(1)} %bitcast.248, bf16[1,768,3072]{2,1,0:T(8,128)(2,1)} %param.33), kind=kOutput, calls=%fused_computation.34 | convolution fusion | flops 1259077632 | bytes 12976128 | tf_op jit(solution)/shard_map/dot_general | solution.py:465
  91.1 2.0 add_convert_fusion.1
  93.1 1.4 fusion.47
  94.7 9.2 %multiply_convert_fusion.1 = (bf16[256,3072]{1,0:T(8,128)(2,1)}, f32[256,3072]{1,0:T(8,128)S(1)}, f32[256,3072]{1,0:T(8,128)S(1)}) fusion(bf16[256,768]{1,0:T(8,128)(2,1)S(1)} %bitcast.240, bf16[1,768,3072]{2,1,0:T(8,128)(2,1)S(1)} %bitcast.224), kind=kOutput, calls=%fused_computation.21 | convolution fusion | flops 1259077632 | bytes 12976128 | tf_op jit(solution)/shard_map/dot_general | solution.py:465
  103.9 2.0 add_convert_fusion
  105.9 1.4 fusion.44
  108.4 4.3 %all-to-all-start.3 = ((bf16[2,2,128,768]{3,2,1,0:T(8,128)(2,1)}), bf16[2,2,128,768]{3,2,1,0:T(8,128)(2,1)}, u32[]{:S(2)}, u32[]{:S(2)}) async-start(bf16[2,2,128,768]{3,2,1,0:T(8,128)(2,1)} %copy.87), calls=%async_computation.4 | async-start | bytes 1572864 | tf_op jit(solution)/shard_map/all_to_all | solution.py:482
  112.7 4.9 %fusion.53 = bf16[2,1,128,768]{3,2,0,1:T(8,128)(2,1)} fusion(bf16[2,128,3072]{2,1,0:T(8,128)(2,1)} %bitcast.265, bf16[1,3072,768]{2,1,0:T(8,128)(2,1)} %param.34), kind=kOutput, calls=%fused_computation.70 | convolution fusion | flops 1208156160 | bytes 6684672 | tf_op jit(solution)/shard_map/dot_general | solution.py:465
  117.7 5.2 %all-to-all-done.3 = bf16[2,2,128,768]{3,2,1,0:T(8,128)(2,1)} async-done(((bf16[2,2,128,768]{3,2,1,0:T(8,128)(2,1)}), bf16[2,2,128,768]{3,2,1,0:T(8,128)(2,1)}, u32[]{:S(2)}, u32[]{:S(2)}) %all-to-all-start.3) | async-done | bytes 786464 | tf_op jit(solution)/shard_map/all_to_all | solution.py:482
  122.8 1.5 fusion.82
  124.3 1.7 multiply_reduce_fusion.1
  127.2 7.8 %all_gather.7 = bf16[512,768]{1,0:T(8,128)(2,1)S(1)} all-gather(bf16[128,768]{1,0:T(8,128)(2,1)S(1)} %fusion.86), channel_id=1, replica_groups=mesh['tp'=4,'ep'=2,'dp'=4] {'tp'}, dimensions={0}, use_global_device_ids=true | all-gather | bytes 983040 | tf_op jit(solution)/shard_map/all_gather | solution.py:632
  140.2 1.7 convolution_convert_fusion.1
  142.0 3.8 %fusion.50 = bf16[2,1,128,768]{3,2,0,1:T(8,128)(2,1)S(1)} fusion(bf16[2,128,3072]{2,1,0:T(8,128)(2,1)S(1)} %bitcast.264, bf16[1,3072,768]{2,1,0:T(8,128)(2,1)} %param.36), kind=kOutput, calls=%fused_computation.69 | convolution fusion | flops 1208156160 | bytes 6684672 | tf_op jit(solution)/shard_map/dot_general | solution.py:465
  146.8 3.6 %all-to-all-start.1 = ((bf16[2,2,128,768]{3,2,1,0:T(8,128)(2,1)}), bf16[2,2,128,768]{3,2,1,0:T(8,128)(2,1)S(1)}, u32[]{:S(2)}, u32[]{:S(2)}) async-start(bf16[2,2,128,768]{3,2,1,0:T(8,128)(2,1)} %copy.86), calls=%async_computation.2 | async-start | bytes 1572864 | tf_op jit(solution)/shard_map/all_to_all | solution.py:482
  151.7 2.9 convolution_convert_fusion
  154.6 1.8 copy.91
  156.4 1.3 convolution_convert_fusion.4
  157.7 1.2 pad_maximum_fusion.pg_ref
  159.0 3.0 all-to-all-done.1
  162.3 1.0 fusion.65
  163.3 1.9 reduce-scatter.5.cloned.1.call-done
  165.2 1.1 convert_reduce_fusion
  166.4 1.2 fusion.78
  168.3 132.0 %grads.1 = (bf16[2,12,4,64,768]{4,3,2,1,0:T(8,128)(2,1)}, bf16[2,4,96,768]{3,2,1,0:T(8,128)(2,1)}, f32[8,768]{1,0:T(8,128)}) custom-call(bf16[2,256,768]{2,1,0:T(8,128)(2,1)} %pad_maximum_fusion.3.xs_ref, bf16[768,3072]{1,0:T(8,128)(2,1)} %bitcast.222, bf16[3072,768]{1,0:T(8,128)(2,1)} %bitcast.225, bf16[2,4,96,768]{3,2,1,0:T(8,128)(2,1)} %pad_maximum_fusion.pg_ref, ...), custom_call_target="tpu_custom_call" | custom-call | tf_op jit(solution)/shard_map/grads/pallas_call | solution.py:356
  300.2 1.2 convert_bitcast_fusion.1
  301.4 1.6 slice_reduce_fusion.2
  303.0 12.2 %finish.1 = (f32[768,3072]{1,0:T(8,128)}, f32[3072,768]{1,0:T(8,128)}, f32[768,192]{1,0:T(8,128)}, f32[768,192]{1,0:T(8,128)}, f32[768,192]{1,0:T(8,128)}, /*index=5*/f32[192,768]{1,0:T(8,128)}) custom-call(s32[1]{0:T(128)} %bitcast.68.tp_ref, bf16[2,12,4,64,768]{4,3,2,1,0:T(8,128)(2,1)} %get-tuple-element.92.rg_ref, bf16[768,768]{1,0:T(8,128)(2,1)} %bitcast.242), custom_call_target="tpu_custom_call" | custom-call | tf_op jit(solution)/shard_map/finish/pallas_call | solution.py:426
  315.2 2.3 copy.93
  317.5 2.2 copy.94
  319.7 1.1 copy.95
  (168 shorter events, 22.7 us)
Async XLA Ops:
  7.2 22.2 %copy-start = (bf16[192,768]{1,0:T(8,128)(2,1)S(1)}, bf16[192,768]{1,0:T(8,128)(2,1)}, u32[]{:S(2)}) copy-start(bf16[192,768]{1,0:T(8,128)(2,1)} %param.30) | copy-start | bytes 884740
  7.2 17.2 %copy-start.27 = (bf16[768,192]{0,1:T(8,128)(2,1)S(1)}, bf16[768,192]{0,1:T(8,128)(2,1)}, u32[]{:S(2)}) copy-start(bf16[768,192]{0,1:T(8,128)(2,1)} %param.29) | copy-start | bytes 884740
  7.2 52.7 %reduce-scatter.3.cloned.1.call-start = ((), (), s32[]{:S(2)}) async-start(), calls=%async_computation.6 | async-start | bytes 1966080 | tf_op jit(solution)/shard_map/reduce_scatter | solution.py:567
  12.2 14.0 %copy-start.36 = (s32[1,512]{1,0:T(1,128)S(1)}, s32[1,512]{1,0:T(1,128)}, u32[]{:S(2)}) copy-start(s32[1,512]{1,0:T(1,128)} %param.21) | copy-start | bytes 6148
  22.3 4.2 %copy-start.22 = (bf16[512,768]{1,0:T(8,128)(2,1)}, bf16[512,768]{1,0:T(8,128)(2,1)S(1)}, u32[]{:S(2)}) copy-start(bf16[512,768]{1,0:T(8,128)(2,1)S(1)} %all_gather.6) | copy-start | bytes 2359300
  24.5 0.9 copy-start.32
  26.1 1.4 copy-start.14
  26.1 1.9 copy-start.20
  28.7 2.2 copy-start.38
  28.7 6.2 %copy-start.39 = (f32[1,128,2]{1,2,0:T(2,128)S(1)}, f32[1,128,2]{1,2,0:T(2,128)}, u32[]{:S(2)}) copy-start(f32[1,128,2]{1,2,0:T(2,128)} %param.24) | copy-start | bytes 3076
  36.3 25.5 %copy-start.35 = (f32[768]{0:T(1024)S(1)}, f32[768]{0:T(1024)}, u32[]{:S(2)}) copy-start(f32[768]{0:T(1024)} %param.31) | copy-start | bytes 9220
  36.3 25.5 %copy-start.37 = (f32[768]{0:T(1024)S(1)}, f32[768]{0:T(1024)}, u32[]{:S(2)}) copy-start(f32[768]{0:T(1024)} %param.32) | copy-start | bytes 9220
  38.7 24.5 %all-to-all-start.2 = ((bf16[2,2,128,768]{3,2,1,0:T(8,128)(2,1)}), bf16[2,2,128,768]{3,2,1,0:T(8,128)(2,1)}, u32[]{:S(2)}, u32[]{:S(2)}) async-start(bf16[2,2,128,768]{3,2,1,0:T(8,128)(2,1)} %bitcast.230), calls=%async_computation.3 | async-start | bytes 1572864 | tf_op jit(solution)/shard_map/all_to_all | solution.py:478
  63.2 15.5 %all-to-all-start = ((bf16[2,2,128,768]{3,2,1,0:T(8,128)(2,1)}), bf16[2,2,128,768]{3,2,1,0:T(8,128)(2,1)}, u32[]{:S(2)}, u32[]{:S(2)}) async-start(bf16[2,2,128,768]{3,2,1,0:T(8,128)(2,1)} %bitcast.229), calls=%async_computation.1 | async-start | bytes 1572864 | tf_op jit(solution)/shard_map/all_to_all | solution.py:478
  78.7 12.3 %slice-start.6 = ((s8[4718592]{0:T(1024)(128)(4,1)}), s8[4194304]{0:T(1024)(128)(4,1)S(1)}, s32[]{:S(2)}) async-start(s8[4718592]{0:T(1024)(128)(4,1)} %bitcast.262), calls=%async_computation.14 | async-start | bytes 8388608
  78.7 14.4 %slice-start.4 = ((s8[4718592]{0:T(1024)(128)(4,1)}), s8[4194304]{0:T(1024)(128)(4,1)S(1)}, s32[]{:S(2)}) async-start(s8[4718592]{0:T(1024)(128)(4,1)} %bitcast.260), calls=%async_computation.12 | async-start | bytes 8388608
  78.7 15.9 %slice-start = ((s8[4718592]{0:T(1024)(128)(4,1)}), s8[4194304]{0:T(1024)(128)(4,1)S(1)}, s32[]{:S(2)}) async-start(s8[4718592]{0:T(1024)(128)(4,1)} %bitcast.223), calls=%async_computation.8 | async-start | bytes 8388608
  80.0 14.6 %copy-start.18 = (bf16[2,1,128,768]{3,2,1,0:T(8,128)(2,1)}, bf16[2,1,128,768]{3,2,1,0:T(8,128)(2,1)S(1)}, u32[]{:S(2)}) copy-start(bf16[2,1,128,768]{3,2,1,0:T(8,128)(2,1)S(1)} %get-tuple-element.178) | copy-start | bytes 1179652
  80.0 11.0 %copy-start.26 = (bf16[2,1,128,768]{3,2,1,0:T(8,128)(2,1)S(1)}, bf16[2,1,128,768]{3,2,1,0:T(8,128)(2,1)}, u32[]{:S(2)}) copy-start(bf16[2,1,128,768]{3,2,1,0:T(8,128)(2,1)} %get-tuple-element.175) | copy-start | bytes 1179652
  80.1 11.0 %slice-start.7 = ((s8[4718592]{0:T(1024)(128)(4,1)}), s8[524288]{0:T(1024)(128)(4,1)S(1)}, s32[]{:S(2)}) async-start(s8[4718592]{0:T(1024)(128)(4,1)} %bitcast.262), calls=%async_computation.15 | async-start | bytes 1048576
  80.1 13.1 %slice-start.5 = ((s8[4718592]{0:T(1024)(128)(4,1)}), s8[524288]{0:T(1024)(128)(4,1)S(1)}, s32[]{:S(2)}) async-start(s8[4718592]{0:T(1024)(128)(4,1)} %bitcast.260), calls=%async_computation.13 | async-start | bytes 1048576
  80.1 14.5 %slice-start.1 = ((s8[4718592]{0:T(1024)(128)(4,1)}), s8[524288]{0:T(1024)(128)(4,1)S(1)}, s32[]{:S(2)}) async-start(s8[4718592]{0:T(1024)(128)(4,1)} %bitcast.223), calls=%async_computation.9 | async-start | bytes 1048576
  93.1 10.7 %slice-start.2 = ((s8[4718592]{0:T(1024)(128)(4,1)}), s8[4194304]{0:T(1024)(128)(4,1)S(1)}, s32[]{:S(2)}) async-start(s8[4718592]{0:T(1024)(128)(4,1)} %bitcast.226), calls=%async_computation.10 | async-start | bytes 8388608
  94.6 9.2 %slice-start.3 = ((s8[4718592]{0:T(1024)(128)(4,1)}), s8[524288]{0:T(1024)(128)(4,1)S(1)}, s32[]{:S(2)}) async-start(s8[4718592]{0:T(1024)(128)(4,1)} %bitcast.226), calls=%async_computation.11 | async-start | bytes 1048576
  94.6 9.2 %copy-start.16 = (bf16[2,1,128,768]{3,2,1,0:T(8,128)(2,1)S(1)}, bf16[2,1,128,768]{3,2,1,0:T(8,128)(2,1)}, u32[]{:S(2)}) copy-start(bf16[2,1,128,768]{3,2,1,0:T(8,128)(2,1)} %get-tuple-element.176) | copy-start | bytes 1179652
  108.4 14.5 %all-to-all-start.3 = ((bf16[2,2,128,768]{3,2,1,0:T(8,128)(2,1)}), bf16[2,2,128,768]{3,2,1,0:T(8,128)(2,1)}, u32[]{:S(2)}, u32[]{:S(2)}) async-start(bf16[2,2,128,768]{3,2,1,0:T(8,128)(2,1)} %copy.87), calls=%async_computation.4 | async-start | bytes 1572864 | tf_op jit(solution)/shard_map/all_to_all | solution.py:482
  112.7 52.5 %reduce-scatter.5.cloned.1.call-start = ((), (), s32[]{:S(2)}) async-start(), calls=%async_computation.7 | async-start | bytes 983040 | tf_op jit(solution)/shard_map/reduce_scatter | solution.py:682
  122.8 3.2 copy-start.2
  122.8 4.2 %copy-start.9 = (bf16[1,128,768]{2,1,0:T(8,128)(2,1)S(1)}, bf16[1,128,768]{2,1,0:T(8,128)(2,1)}, u32[]{:S(2)}) copy-start(bf16[1,128,768]{2,1,0:T(8,128)(2,1)} %param.37) | copy-start | bytes 589828
  127.1 9.8 %copy-start.21 = (bf16[512,192]{0,1:T(8,128)(2,1)S(1)}, bf16[512,192]{0,1:T(8,128)(2,1)}, u32[]{:S(2)}) copy-start(bf16[512,192]{0,1:T(8,128)(2,1)} %copy-done.20) | copy-start | bytes 589828
  136.9 2.7 copy-start.28
  137.6 0.9 copy-start.15
  137.6 1.5 copy-start.13
  138.5 1.7 copy-start.33
  139.2 2.8 copy-start.40
  142.0 3.8 %copy-start.25 = (bf16[2,1,128,768]{3,2,0,1:T(8,128)(2,1)S(1)}, bf16[2,1,128,768]{3,2,0,1:T(8,128)(2,1)}, u32[]{:S(2)}) copy-start(bf16[2,1,128,768]{3,2,0,1:T(8,128)(2,1)} %fusion.53) | copy-start | bytes 1179652
  145.8 4.6 %copy-start.17 = (bf16[2,1,128,768]{3,2,1,0:T(8,128)(2,1)S(1)}, bf16[2,1,128,768]{3,2,1,0:T(8,128)(2,1)}, u32[]{:S(2)}) copy-start(bf16[2,1,128,768]{3,2,1,0:T(8,128)(2,1)} %get-tuple-element.176) | copy-start | bytes 1179652
  145.8 4.6 %copy-start.19 = (bf16[2,1,128,768]{3,2,1,0:T(8,128)(2,1)S(1)}, bf16[2,1,128,768]{3,2,1,0:T(8,128)(2,1)}, u32[]{:S(2)}) copy-start(bf16[2,1,128,768]{3,2,1,0:T(8,128)(2,1)} %copy-done.18) | copy-start | bytes 1179652
  145.8 5.6 %copy-start.6 = (bf16[512,768]{1,0:T(8,128)(2,1)S(1)}, bf16[512,768]{1,0:T(8,128)(2,1)}, u32[]{:S(2)}) copy-start(bf16[512,768]{1,0:T(8,128)(2,1)} %copy-done.5) | copy-start | bytes 2359300
  145.9 5.8 %copy-start.29 = (bf16[3,512,64]{1,2,0:T(8,128)(2,1)S(1)}, bf16[3,512,64]{1,2,0:T(8,128)(2,1)}, u32[]{:S(2)}) copy-start(bf16[3,512,64]{1,2,0:T(8,128)(2,1)} %copy-done.28) | copy-start | bytes 589828
  146.8 15.1 %all-to-all-start.1 = ((bf16[2,2,128,768]{3,2,1,0:T(8,128)(2,1)}), bf16[2,2,128,768]{3,2,1,0:T(8,128)(2,1)S(1)}, u32[]{:S(2)}, u32[]{:S(2)}) async-start(bf16[2,2,128,768]{3,2,1,0:T(8,128)(2,1)} %copy.86), calls=%async_computation.2 | async-start | bytes 1572864 | tf_op jit(solution)/shard_map/all_to_all | solution.py:482
  154.6 7.7 %copy-start.3 = (f32[128,768]{1,0:T(8,128)S(1)}, f32[128,768]{1,0:T(8,128)}, u32[]{:S(2)}) copy-start(f32[128,768]{1,0:T(8,128)} %copy-done.1) | copy-start | bytes 1179652
  156.3 8.9 %copy-start.4 = (bf16[1,128,768]{2,1,0:T(8,128)(2,1)S(1)}, bf16[1,128,768]{2,1,0:T(8,128)(2,1)}, u32[]{:S(2)}) copy-start(bf16[1,128,768]{2,1,0:T(8,128)(2,1)} %param.20) | copy-start | bytes 589828
  156.4 8.9 %copy-start.34 = (f32[768]{0:T(1024)S(1)}, f32[768]{0:T(1024)}, u32[]{:S(2)}) copy-start(f32[768]{0:T(1024)} %param.25) | copy-start | bytes 9220
  315.2 4.6 %copy-start.23 = (f32[768,192]{1,0:T(8,128)S(1)}, f32[768,192]{1,0:T(8,128)}, u32[]{:S(2)}) copy-start(f32[768,192]{1,0:T(8,128)} %get-tuple-element.145) | copy-start | bytes 1769476
  315.2 5.6 %copy-start.8 = (f32[128,768]{1,0:T(8,128)S(1)}, f32[128,768]{1,0:T(8,128)}, u32[]{:S(2)}) copy-start(f32[128,768]{1,0:T(8,128)} %copy-done.7) | copy-start | bytes 1179652
  315.2 5.6 %copy-start.10 = (bf16[1,128,768]{2,1,0:T(8,128)(2,1)S(1)}, bf16[1,128,768]{2,1,0:T(8,128)(2,1)}, u32[]{:S(2)}) copy-start(bf16[1,128,768]{2,1,0:T(8,128)(2,1)} %param.37) | copy-start | bytes 589828
  315.2 5.6 %copy-start.11 = (bf16[128,768]{1,0:T(8,128)(2,1)S(1)}, bf16[128,768]{1,0:T(8,128)(2,1)}, u32[]{:S(2)}) copy-start(bf16[128,768]{1,0:T(8,128)(2,1)} %reduce-scatter.5.cloned.1.call-done) | copy-start | bytes 589828
  (7 other events, 5.1 us)
Sparse Core Ops, SparseCore 0:
  31.1 28.8 reduce-scatter.2
  142.1 23.0 reduce-scatter.4

commit v2 on v1

--- a/solution.py
+++ b/solution.py
@@ -54,12 +54,307 @@
     return hidden * phi, phi + hidden * dens
 
 
+def ln_rows(values, gain, bias):
+    center = jnp.mean(values, axis=-1, keepdims=True)
+    shifted = values - center
+    spread = jnp.mean(shifted * shifted, axis=-1, keepdims=True)
+    return shifted * lax.rsqrt(spread + EPSILON) * gain + bias
+
+
+def route_picks(routes_ref, capacity, slots):
+    first, second = routes_ref[:, 0:1], routes_ref[:, 1:2]
+    rows = first.shape[0]
+    lane = lax.broadcasted_iota(jnp.int32, (rows, 128), 1)
+    marks = jnp.where((lane == first) | (lane == second), 1.0, 0.0)
+    row_id = lax.broadcasted_iota(jnp.int32, (rows, rows), 0)
+    col_id = lax.broadcasted_iota(jnp.int32, (rows, rows), 1)
+    lower = jnp.where(row_id > col_id, 1.0, 0.0).astype(BF)
+    before = jnp.dot(lower, marks.astype(BF), preferred_element_type=F32)
+    slot = lax.broadcasted_iota(jnp.int32, (rows, slots), 1)
+    picks = []
+    for route in (first, second):
+        place = jnp.sum(jnp.where(lane == route, before, 0.0), axis=1, keepdims=True)
+        chosen = route * capacity + place.astype(jnp.int32)
+        picks.append(jnp.where(slot == chosen, 1.0, 0.0).astype(BF))
+    return picks[0], picks[1], marks
+
+
+def dot_tn(left, right):
+    return lax.dot_general(left, right, (((0,), (0,)), ((), ())), preferred_element_type=F32)
+
+
+def dot_nt(left, right):
+    return lax.dot_general(left, right, (((1,), (1,)), ((), ())), preferred_element_type=F32)
+
+
+def dot_nn(left, right):
+    return jnp.dot(left, right, preferred_element_type=F32)
+
+
+def front_kernel(
+    ep_count, heads,
+    tok_ref, seg_ref, key_ref, routes_ref, gates_ref, cot_ref, g1_ref, b1_ref, wq_ref, wk_ref, wv_ref, wo_ref,
+    g2_ref, b2_ref, fin_hbm, fout_hbm, tin_hbm, tout_hbm,
+    group_ref, qkv_ref, heads_ref, lse_ref, middle_ref, back_ref, out_ref, gx, gs,
+    weights, joined, bias, part, core_slot, mix, x_slot, sx, ss, ax, as_, out_acc, back_acc,
+    w_sem, a_send, a_recv, c_send, c_recv, m_send, m_recv, e_send, e_recv, t_send, t_recv,
+):
+    tp, tp1, tp2, tp3 = tp_peers()
+    ep = lax.axis_index("ep")
+    rows, width = tok_ref.shape
+    cols = wq_ref.shape[1]
+    hidden = fin_hbm.shape[1]
+    capacity = sx.shape[2]
+    slots = ep_count * EXP_DEV * capacity
+    loads = []
+    for index, source in enumerate((fin_hbm, tin_hbm)):
+        loads.append(pltpu.make_async_copy(source, weights[0].at[index], w_sem.at[0, index]))
+    for index, source in enumerate((fout_hbm, tout_hbm)):
+        loads.append(pltpu.make_async_copy(source, weights[1].at[index], w_sem.at[1, index]))
+
+    barrier = pltpu.get_barrier_semaphore()
+    for peer in (tp1, tp2, tp3):
+        pl.semaphore_signal(barrier, inc=1, device_id={"tp": peer}, device_id_type=MESH)
+    for off in range(1, ep_count):
+        pl.semaphore_signal(
+            barrier, inc=1, device_id={"ep": (ep + off) % ep_count}, device_id_type=MESH
+        )
+    residual = tok_ref[...].astype(F32)
+    group_ref[tp] = ln_rows(residual, g1_ref[...], b1_ref[...]).astype(BF)
+    pl.semaphore_wait(barrier, 3 + ep_count - 1)
+
+    def gather_copy(slot, index, peer):
+        return remote(group_ref.at[slot], group_ref.at[slot], a_send.at[index], a_recv.at[index], {"tp": peer})
+
+    sends = [gather_copy(tp, 1, tp2), gather_copy(tp, 0, tp1)]
+    for copy in sends:
+        copy.start()
+    for copy in (loads[0], loads[2], loads[1], loads[3]):
+        copy.start()
+
+    pick0, pick1, _ = route_picks(routes_ref, capacity, slots)
+    upstream = cot_ref[...].astype(F32)
+    share0 = (gates_ref[:, 0:1] * upstream).astype(BF)
+    share1 = (gates_ref[:, 1:2] * upstream).astype(BF)
+    ss[...] = (dot_tn(pick0, share0) + dot_tn(pick1, share1)).astype(BF).reshape(ss.shape)
+
+    def owner_copies(kind, source, target):
+        return [
+            remote(
+                source.at[(ep + off) % ep_count], target.at[ep], e_send.at[kind, off - 1], e_recv.at[kind, off - 1],
+                {"ep": (ep + off) % ep_count},
+            )
+            for off in range(1, ep_count)
+        ]
+
+    def owner_waits(kind, target):
+        for off in range(1, ep_count):
+            source = (ep + ep_count - off) % ep_count
+            remote(
+                target.at[source], target.at[source], e_send.at[kind, off - 1], e_recv.at[kind, off - 1],
+                {"ep": source},
+            ).wait_recv()
+
+    share_sends = owner_copies(1, ss, as_)
+    for copy in share_sends:
+        copy.start()
+    as_[ep] = ss[ep]
+
+    for index, ref in enumerate((wq_ref, wk_ref, wv_ref)):
+        joined[:, index * cols : (index + 1) * cols] = ref[...]
+
+    segment = seg_ref[...]
+    group_rows = segment.shape[1]
+    lane = lax.broadcasted_iota(jnp.int32, segment.shape, 1)
+    starts = (segment != pltpu.roll(segment, 1, 1)) | (lane == 0)
+    keep = (key_ref[...] == 1) | starts
+    segment = segment.astype(F32)
+    column = jnp.broadcast_to(segment, (8, group_rows)).T[:, 0:1]
+    kept = jnp.where(keep, segment, -1.0)
+    bias[...] = jnp.where(column == kept, 0.0, MASKED)
+
+    def project(slot):
+        at = pl.ds(pl.multiple_of(slot * rows, rows), rows)
+        qkv_ref[at, :] = dot_nn(group_ref[slot], joined[...]).astype(BF)
+
+    project(tp)
+    gather_copy(tp1, 0, tp1).wait_recv()
+    project(tp1)
+    gather_copy(tp2, 1, tp2).wait_recv()
+    sends.append(gather_copy(tp2, 2, tp1))
+    sends[-1].start()
+    project(tp2)
+    gather_copy(tp3, 2, tp1).wait_recv()
+    project(tp3)
+
+    def token_copy(kind, buf, source, hop, peer):
+        return remote(source, buf.at[hop], t_send.at[kind, hop - 1], t_recv.at[kind, hop - 1], {"tp": peer})
+
+    owner_waits(1, as_)
+    train = EXP_DEV - 1
+    token_sends = [
+        token_copy(1, gs, as_.at[:, train], 2, tp2), token_copy(1, gs, as_.at[:, train], 1, tp1)
+    ]
+    for copy in token_sends:
+        copy.start()
+    gs[0] = as_[:, train]
+
+    scale = HD ** (-0.5)
+    block = min(256, group_rows)
+    for head in range(heads):
+        def attend(index, _, head=head):
+            at = pl.ds(pl.multiple_of(index * block, block), block)
+            query = qkv_ref[at, head * HD : (head + 1) * HD]
+            keys = qkv_ref[:, cols + head * HD : cols + (head + 1) * HD]
+            values = qkv_ref[:, 2 * cols + head * HD : 2 * cols + (head + 1) * HD]
+            scores = dot_nt(query, keys) * scale + bias[at, :]
+            highest = jnp.max(scores, axis=-1, keepdims=True)
+            weight = jnp.exp(scores - highest)
+            total = jnp.sum(weight, axis=-1, keepdims=True)
+            probs = (weight * (1.0 / total)).astype(BF)
+            heads_ref[at, head * HD : (head + 1) * HD] = dot_nn(probs, values).astype(BF)
+            lse_ref[at, head : head + 1] = highest + jnp.log(total)
+            return 0
+
+        for index in range(group_rows // block):
+            attend(index, 0)
+
+    def partial(slot):
+        at = pl.ds(pl.multiple_of(slot * rows, rows), rows)
+        return dot_nn(heads_ref[at, :], wo_ref[...])
+
+    def core_copy(index):
+        return remote(part.at[index], core_slot.at[index], c_send.at[index], c_recv.at[index], {"tp": tp1})
+
+    part[0] = partial(tp3)
+    core_copy(0).start()
+    part[1] = partial(tp1)
+    core_copy(1).start()
+    crossing = partial(tp2)
+    own = residual + partial(tp)
+    token_copy(1, gs, as_.at[:, train], 2, tp2).wait_recv()
+    token_sends.append(token_copy(1, gs, gs.at[2], 3, tp1))
+    token_sends[-1].start()
+    core_copy(0).wait_recv()
+    mix[...] = (crossing + core_slot[0]).astype(BF)
+    cross = remote(mix, x_slot, m_send, m_recv, {"tp": tp2})
+    cross.start()
+    core_copy(1).wait_recv()
+    own = own + core_slot[1]
+    cross.wait_recv()
+    middle = own + x_slot[...].astype(F32)
+    middle_ref[...] = middle
+    normed = ln_rows(middle, g2_ref[...], b2_ref[...]).astype(BF)
+    sx[...] = dot_tn(pick0 + pick1, normed).astype(BF).reshape(sx.shape)
+    input_sends = owner_copies(0, sx, ax)
+    for copy in input_sends:
+        copy.start()
+    ax[ep] = sx[ep]
+    for copy in loads:
+        copy.wait()
+    owner_waits(0, ax)
+    token_sends.append(token_copy(0, gx, ax.at[:, train], 2, tp2))
+    token_sends.append(token_copy(0, gx, ax.at[:, train], 1, tp1))
+    for copy in token_sends[-2:]:
+        copy.start()
+    gx[0] = ax[:, train]
+
+    step = width
+    for expert in range(EXP_DEV):
+        inputs = ax[:, expert].reshape(-1, width)
+        shares = as_[:, expert].reshape(-1, width)
+
+        def piece(index, _, expert=expert, inputs=inputs, shares=shares):
+            at = pl.ds(pl.multiple_of(index * step, step), step)
+            inner, outer = weights[0].at[expert], weights[1].at[expert]
+            before = dot_nn(inputs, inner[:, at])
+            through = dot_nt(shares, outer[at, :])
+            value, grad = gelu_pair(before)
+            slope = (through * grad).astype(BF)
+            produced = dot_nn(value.astype(BF), outer[at, :])
+            returned = dot_nt(slope, inner[:, at])
+
+            @pl.when(index == 0)
+            def _():
+                out_acc[...] = produced
+                back_acc[...] = returned
+
+            @pl.when(index > 0)
+            def _():
+                out_acc[...] += produced
+                back_acc[...] += returned
+
+            return 0
+
+        lax.fori_loop(0, hidden // step, piece, 0)
+        out_ref[:, expert] = out_acc[...].astype(BF).reshape(ep_count, capacity, width)
+        back_ref[:, expert] = back_acc[...].astype(BF).reshape(ep_count, capacity, width)
+        if expert == 0:
+            token_copy(0, gx, ax.at[:, train], 2, tp2).wait_recv()
+            token_sends.append(token_copy(0, gx, gx.at[2], 3, tp1))
+            token_sends[-1].start()
+
+    for kind, buf in ((0, gx), (1, gs)):
+        token_copy(kind, buf, buf.at[1], 1, tp1).wait_recv()
+        token_copy(kind, buf, buf.at[3], 3, tp1).wait_recv()
+    for copy in sends + share_sends + input_sends + token_sends + [core_copy(0), core_copy(1), cross]:
+        copy.wait_send()
+
+
+def front(tokens, segment, key_mask, routes, gates, cot, g1, b1, wq, wk, wv, wo, g2, b2, fin, fout, tin, tout):
+    ep_count = lax.axis_size("ep")
+    rows, width = tokens.shape
+    group_rows = segment.shape[1]
+    cols = wq.shape[1]
+    hidden = fin.shape[1]
+    experts = EXP_DEV * ep_count
+    capacity = 4 * rows // experts
+    dma = pltpu.SemaphoreType.DMA
+    vmem = pl.BlockSpec(memory_space=pltpu.VMEM)
+    hbm = pl.BlockSpec(memory_space=pl.ANY)
+    struct = jax.ShapeDtypeStruct
+    block = (ep_count, EXP_DEV, capacity, width)
+    gathered = (4, ep_count, capacity, width)
+    others = ep_count - 1
+    return pl.pallas_call(
+        functools.partial(front_kernel, ep_count, cols // HD),
+        out_shape=(
+            struct((4, rows, width), BF),
+            struct((group_rows, 3 * cols), BF),
+            struct((group_rows, cols), BF),
+            struct((group_rows, 8), F32),
+            struct((rows, width), F32),
+            struct(block, BF), struct(block, BF), struct(gathered, BF), struct(gathered, BF),
+        ),
+        in_specs=[vmem] * 14 + [hbm] * 4,
+        out_specs=tuple([vmem] * 9),
+        scratch_shapes=[
+            [pltpu.VMEM((2, width, hidden), BF), pltpu.VMEM((2, hidden, width), BF)],
+            pltpu.VMEM((width, 3 * cols), BF),
+            pltpu.VMEM((group_rows, group_rows), F32),
+            pltpu.VMEM((2, rows, width), F32),
+            pltpu.VMEM((2, rows, width), F32),
+            pltpu.VMEM((rows, width), BF),
+            pltpu.VMEM((rows, width), BF),
+            pltpu.VMEM(block, BF), pltpu.VMEM(block, BF), pltpu.VMEM(block, BF), pltpu.VMEM(block, BF),
+            pltpu.VMEM((ep_count * capacity, width), F32),
+            pltpu.VMEM((ep_count * capacity, width), F32),
+            dma((2, 2)), dma((3,)), dma((3,)), dma((2,)), dma((2,)), dma(()), dma(()),
+            dma((2, others)), dma((2, others)), dma((2, 3)), dma((2, 3)),
+        ],
+        compiler_params=pltpu.CompilerParams(
+            collective_id=1, has_side_effects=True, vmem_limit_bytes=62 * 1024 * 1024
+        ),
+        name="front",
+    )(tokens, segment, key_mask, routes, gates, cot, g1, b1, wq, wk, wv, wo, g2, b2, fin, fout, tin, tout)
+
+
 def grads_kernel(
     ep_count, dp_count, n,
-    xs_ref, w_in_hbm, w_out_hbm, pg_ref, small_ref,
+    gx_ref, gs_ref, w_in_hbm, w_out_hbm, pg_ref, small_ref,
     rg_hbm, full_ref, small_out,
-    gx, gs, w_in, w_out, act, slope, own, red, stage, fin, pslot, acc1, dslot, acc2, sm_tp, sm_ep, sm_dp, sm_a, sm_b,
-    g_send, g_recv, w_sem, red_send, red_recv, bc_send, bc_recv, x_send, x_recv, out_sem,
+    w_in, w_out, act, slope, own, red, stage, fin, pslot, acc1, dslot, acc2, sm_tp, sm_ep, sm_dp, sm_a, sm_b,
+    w_sem, red_send, red_recv, bc_send, bc_recv, x_send, x_recv, out_sem,
     p_send, p_recv, d_send, d_recv, e_send, e_recv, f_send, f_recv, s_send, s_recv,
 ):
     tp, tp1, tp2, tp3 = tp_peers()
@@ -74,13 +369,6 @@
     out_copy.start()
     entry_barrier(ep_count, dp_count)
 
-    token_copies = {}
-    for part, buf in ((0, gx), (1, gs)):
-        for hop, peer in ((1, tp1), (2, tp2)):
-            token_copies[part, hop] = remote(
-                xs_ref.at[part], buf.at[hop], g_send.at[part, hop - 1], g_recv.at[part, hop - 1], {"tp": peer}
-            )
-            token_copies[part, hop].start()
     ep_copies = []
     for off in range(1, ep_count):
         peer = (ep + off) % ep_count
@@ -95,32 +383,21 @@
         )
         small_copies[-1].start()
 
-    gx[0] = xs_ref[0]
-    gs[0] = xs_ref[1]
     in_copy.wait()
     out_copy.wait()
 
-    def hidden_block(index):
-        rows = gx.shape[1]
-        hidden = jnp.dot(gx[index], w_in[...], preferred_element_type=F32)
-        through = lax.dot_general(gs[index], w_out[...], (((1,), (1,)), ((), ())), preferred_element_type=F32)
+    rows = gx_ref.shape[1] * gx_ref.shape[2]
+
+    def hidden_block(index, _):
+        hidden = jnp.dot(gx_ref[index].reshape(rows, width), w_in[...], preferred_element_type=F32)
+        through = dot_nt(gs_ref[index].reshape(rows, width), w_out[...])
         value, grad = gelu_pair(hidden)
-        act[pl.ds(index * rows, rows), :] = value.astype(BF)
-        slope[pl.ds(index * rows, rows), :] = (through * grad).astype(BF)
-
-    hidden_block(0)
-    for part in (0, 1):
-        token_copies[part, 1].wait_recv()
-    hidden_block(1)
-    forward = []
-    for part, buf in ((0, gx), (1, gs)):
-        token_copies[part, 2].wait_recv()
-        forward.append(remote(buf.at[2], buf.at[3], g_send.at[part, 2], g_recv.at[part, 2], {"tp": tp1}))
-        forward[-1].start()
-    hidden_block(2)
-    for copy in forward:
-        copy.wait_recv()
-    hidden_block(3)
+        at = pl.ds(pl.multiple_of(index * rows, rows), rows)
+        act[at, :] = value.astype(BF)
+        slope[at, :] = (through * grad).astype(BF)
+        return 0
+
+    lax.fori_loop(0, 4, hidden_block, 0)
 
     for copy in small_copies:
         copy.wait()
@@ -148,13 +425,13 @@
     step_rows = 2 * CHUNK
 
     def outer(index, _):
-        rows = pl.ds(pl.multiple_of(index * step_rows, step_rows), step_rows)
-        x_all = gx[:, :, rows].reshape(-1, step_rows)
-        s_all = gs[...].reshape(-1, width)
+        at = pl.ds(pl.multiple_of(index * step_rows, step_rows), step_rows)
+        x_all = gx_ref[:, :, :, at].reshape(-1, step_rows)
+        s_all = gs_ref[...].reshape(-1, width)
         piece = lax.dot_general(x_all, slope[...], (((0,), (0,)), ((), ())), preferred_element_type=F32)
-        own[0, rows, :] = piece
-        piece = lax.dot_general(act[:, rows], s_all, (((0,), (0,)), ((), ())), preferred_element_type=F32)
-        own[1, rows, :] = piece
+        own[0, at, :] = piece
+        piece = lax.dot_general(act[:, at], s_all, (((0,), (0,)), ((), ())), preferred_element_type=F32)
+        own[1, at, :] = piece
         return 0
 
     for index in range(width // step_rows):
@@ -315,10 +592,6 @@
             full_ref.at[source], full_ref.at[source], f_send.at[off - 1], f_recv.at[off - 1], {"ep": source}
         ).wait_recv()
 
-    for copy in token_copies.values():
-        copy.wait_send()
-    for copy in forward:
-        copy.wait_send()
 
     def drain(index, _):
         for half in (0, 1):
@@ -340,9 +613,10 @@
     lax.fori_loop(0, n, drain, 0)
 
 
-def reduce_grads(xs, w_in, w_out, proj, small):
+def reduce_grads(gx, gs, w_in, w_out, proj, small):
     ep_count, dp_count = lax.axis_size("ep"), lax.axis_size("dp")
-    _, rows, width = xs.shape
+    width = gx.shape[3]
+    rows = gx.shape[1] * gx.shape[2]
     hidden = w_in.shape[1]
     quarter = hidden // 4
     n = width // CHUNK
@@ -360,11 +634,9 @@
             jax.ShapeDtypeStruct(pg.shape, BF),
             jax.ShapeDtypeStruct(small.shape, F32),
         ),
-        in_specs=[vmem, hbm, hbm, vmem, vmem],
+        in_specs=[vmem, vmem, hbm, hbm, vmem, vmem],
         out_specs=(hbm, vmem, vmem),
         scratch_shapes=[
-            pltpu.VMEM((4, rows, width), BF),
-            pltpu.VMEM((4, rows, width), BF),
             pltpu.VMEM((width, quarter), BF),
             pltpu.VMEM((quarter, width), BF),
             pltpu.VMEM((4 * rows, quarter), BF),
@@ -382,7 +654,7 @@
             pltpu.VMEM((dp_count - 1,) + small.shape, F32),
             pltpu.VMEM(small.shape, F32),
             pltpu.VMEM(small.shape, F32),
-            dma((2, 3)), dma((2, 3)), dma((2,)),
+            dma((2,)),
             dma((2, n)), dma((2, n)), dma((2, n)), dma((2, n)),
             dma((3, 2, n)), dma((3, 2, n)), dma((2, n)),
             dma((ep_count - 1,)), dma((ep_count - 1,)),
@@ -395,7 +667,7 @@
             collective_id=0, has_side_effects=True, vmem_limit_bytes=60 * 1024 * 1024
         ),
         name="grads",
-    )(xs, w_in, w_out, pg, small)
+    )(gx, gs, w_in, w_out, pg, small)
 
 
 def finish_kernel(tp_ref, rg_ref, full_ref, gin_ref, gout_ref, q_ref, k_ref, v_ref, o_ref):
@@ -474,25 +746,8 @@
     return jnp.where(allowed[None], scores, MASKED)
 
 
-def to_owners(buffer):
-    return lax.all_to_all(buffer, "ep", split_axis=0, concat_axis=0, tiled=True)
-
-
 def to_sources(buffer):
     return lax.all_to_all(buffer, "ep", split_axis=0, concat_axis=0, tiled=True)
-
-
-def expert_forward(inputs, inner, outer):
-    hidden = contract(inputs, inner, 1, 0)
-    active = gelu_exact(hidden).astype(jnp.bfloat16)
-    return (hidden, active, contract(active, outer, 1, 0))
-
-
-def expert_backward(inputs, hidden, active, upstream, inner, outer, trainable):
-    through = contract(upstream, outer, 1, 1)
-    slope = jax.vjp(gelu_exact, hidden)[1](through)[0].astype(jnp.bfloat16)
-    back_in = contract(slope, inner, 1, 1)
-    return back_in
 
 
 def local(
@@ -524,12 +779,14 @@
     local_heads = head_cols // HD
     residual = tokens[0].astype(jnp.float32)
     joined = jnp.concatenate([query_weight, key_weight, value_weight], axis=1)
-    first_normed = layer_norm(residual, ln1_gain, ln1_bias).astype(jnp.bfloat16)
-    piece = lax.all_gather(first_normed, "tp", axis=0, tiled=True)
-    projected = contract(piece, joined, 1, 0)
-    gathered = piece
-    projected, normed_group = (projected, gathered)
-    projected = projected.astype(jnp.bfloat16)
+    line = lambda vector: vector.reshape(1, width)
+    group, projected, attn_heads, lse, middle, back_rows, out_rows, gx, gs = front(
+        tokens[0], segment, key_mask, routes[0], gates[0], cotangent[0], line(ln1_gain), line(ln1_bias),
+        query_weight, key_weight, value_weight, out_weight, line(ln2_gain), line(ln2_bias),
+        frozen_in[0], frozen_out[0], train_in[0], train_out[0],
+    )
+    normed_group = group.reshape(group_rows, width)
+    log_totals = lse[:, :local_heads].T[None]
     block = min(512, group_rows)
     blocks = group_rows // block
 
@@ -550,24 +807,6 @@
     keep_row = (key_mask[0] == 1) | starts
     segment_blocks = segment_row.reshape(blocks, block)
 
-    def forward_block(item):
-        block_queries, block_segment = item
-        scores = masked_scores(block_queries, block_segment, keys, segment_row, keep_row)
-        highest = jnp.max(scores, axis=-1, keepdims=True)
-        weights = jnp.exp(scores - highest)
-        totals = jnp.sum(weights, axis=-1, keepdims=True)
-        probs = (weights / totals).astype(jnp.bfloat16)
-        outputs = jnp.einsum("hqk,hkd->hqd", probs, values, preferred_element_type=jnp.float32)
-        return (outputs, (highest + jnp.log(totals))[..., 0])
-
-    head_blocks, log_totals = lax.map(forward_block, (query_blocks, segment_blocks))
-    attn_heads = (
-        head_blocks.transpose(0, 2, 1, 3).reshape(group_rows, head_cols).astype(jnp.bfloat16)
-    )
-    middle = residual + lax.psum_scatter(
-        contract(attn_heads, out_weight, 1, 0), "tp", scatter_dimension=0, tiled=True
-    )
-    second_normed = layer_norm(middle, ln2_gain, ln2_bias).astype(jnp.bfloat16)
     experts = EXP_DEV * ep_count
     capacity = 4 * local_rows // experts
     slots = experts * capacity
@@ -581,46 +820,14 @@
     pick_first = (slot_ids[:, 0:1] == slot_range).astype(jnp.bfloat16)
     pick_second = (slot_ids[:, 1:2] == slot_range).astype(jnp.bfloat16)
     local_counts = jnp.sum(marks, axis=0).astype(jnp.float32)
-    send = contract(pick_first + pick_second, second_normed, 0, 0).astype(jnp.bfloat16)
-    arrived = to_owners(send.reshape(ep_count, EXP_DEV, capacity, width))
-    inner_list = (frozen_in[0], train_in[0])
-    outer_list = (frozen_out[0], train_out[0])
-    kept = []
-    produced = []
-    for index in range(EXP_DEV):
-        inputs = arrived[:, index].reshape(-1, width)
-        hidden, active, result = expert_forward(inputs, inner_list[index], outer_list[index])
-        kept.append((inputs, hidden, active))
-        produced.append(result.reshape(ep_count, -1, width))
-    produced = jnp.stack(produced, axis=1)
-    returned = to_sources(produced.astype(jnp.bfloat16)).reshape(slots, width)
+    returned = to_sources(out_rows).reshape(slots, width)
     gate_rows = gates[0]
     mixture = gate_rows[:, 0:1] * contract(pick_first, returned, 1, 0) + gate_rows[
         :, 1:2
     ] * contract(pick_second, returned, 1, 0)
     layer_out = (middle + mixture).astype(jnp.bfloat16)
     upstream = cotangent[0].astype(jnp.float32)
-    first_share = (gate_rows[:, 0:1] * upstream).astype(jnp.bfloat16)
-    second_share = (gate_rows[:, 1:2] * upstream).astype(jnp.bfloat16)
-    back_send = (
-        contract(pick_first, first_share, 0, 0) + contract(pick_second, second_share, 0, 0)
-    ).astype(jnp.bfloat16)
-    back_arrived = to_owners(back_send.reshape(ep_count, EXP_DEV, capacity, width))
-    input_terms = []
-    for index in range(EXP_DEV):
-        inputs, hidden, active = kept[index]
-        back_in = expert_backward(
-            inputs,
-            hidden,
-            active,
-            back_arrived[:, index].reshape(-1, width),
-            inner_list[index],
-            outer_list[index],
-            index == EXP_DEV - 1,
-        )
-        input_terms.append(back_in.reshape(ep_count, -1, width))
-    input_terms = jnp.stack(input_terms, axis=1)
-    back_returned = to_sources(input_terms.astype(jnp.bfloat16)).reshape(slots, width)
+    back_returned = to_sources(back_rows).reshape(slots, width)
     second_grad = contract(pick_first, back_returned, 1, 0) + contract(
         pick_second, back_returned, 1, 0
     )
@@ -695,8 +902,7 @@
         [ln1_gain_grad, ln1_bias_grad, ln2_gain_grad, ln2_bias_grad, counts_row]
         + [jnp.zeros((width,), jnp.float32)] * 3
     )
-    xs = jnp.stack([kept[-1][0], back_arrived[:, EXP_DEV - 1].reshape(-1, width)])
-    rg, full, sums = reduce_grads(xs, train_in[0], train_out[0], proj, small)
+    rg, full, sums = reduce_grads(gx, gs, train_in[0], train_out[0], proj, small)
     grad_in, grad_out, *summed = finish(rg, full, head_cols)
     gain_one, bias_one, gain_two, bias_two = sums[0], sums[1], sums[2], sums[3]
     counts = sums[4, :experts]

time: 336 us -> 292 us (0.87); the launches traced: 329 us -> 290 us
  Pallas kernels: 144 us -> 192 us
  matrix products: 57.7 us -> 9.89 us
  waiting for transfers between devices: 35.9 us -> 21.3 us
  blocking collectives: 17.9 us -> 8.8 us
  starting transfers between devices: 16.8 us -> 7.91 us
  other arithmetic: 17.5 us -> 9.33 us
    pallas_call x0 -> x1, Pallas kernels: none -> 56.1 us  [front(): pl.pallas_call(functools.partial(front_kernel, ep_count, cols // HD), out...]
    dot_general x21 -> x8, matrix products: 53.9 us -> 6.54 us  [contract(): lax.dot_general(left, right, (((left_dim,), (right_dim,)), ((), ())), pre...]
    reduce_scatter x1 -> x0, waiting for transfers between devices: 16.9 us -> none  [local(): lax.psum_scatter(contract(attn_heads, out_weight, 1, 0), 'tp', scatter_di...]
    reduce_scatter x1, waiting for transfers between devices: 1.91 us -> 16.2 us  [local(): lax.psum_scatter(contract(projected_grad, joined, 1, 1).astype(jnp.bfloat...]
    all_gather x1 -> x0, blocking collectives: 10.1 us -> none  [local(): piece = lax.all_gather(first_normed, 'tp', axis=0, tiled=True)]
    all_to_all x2 -> x0, waiting for transfers between devices: 8.91 us -> none  [to_owners(): return lax.all_to_all(buffer, 'ep', split_axis=0, concat_axis=0, tiled=True)]
    all_to_all x2 -> x0, starting transfers between devices: 8.82 us -> none  [to_owners(): return lax.all_to_all(buffer, 'ep', split_axis=0, concat_axis=0, tiled=True)]
    pallas_call x1, Pallas kernels: 132 us -> 124 us  [reduce_grads(): pl.pallas_call(functools.partial(grads_kernel, ep_count, dp_count, n), ou...]
  transfers between devices with their start and end apart: 6 -> 3, of which waited for: 5 -> 2; matrix products, arithmetic and copies ran while one was open for 10% -> 7% of each run, Pallas kernels for 0% -> 0%
where the time goes in v2:
time: 292 us; the launch traced here: 290 us
  Pallas kernels  192 us (66%)
  local copies, waits for them, and re-layouts  26.5 us (9%)
  waiting for transfers between devices  21.3 us (7%)
  between operations  14.5 us (5%)
  matrix products  9.89 us (3%)
  other arithmetic  9.33 us (3%)
  blocking collectives  8.8 us (3%)
  starting transfers between devices  7.91 us (3%)
    pallas_call x1, Pallas kernels, reduce_grads(): pl.pallas_call(functools.partial(grads_kernel, ep_count, dp_count, n), ou...  124 us
    pallas_call x1, Pallas kernels, front(): pl.pallas_call(functools.partial(front_kernel, ep_count, cols // HD), out...  56.1 us
    reduce_scatter x1, waiting for transfers between devices, local(): lax.psum_scatter(contract(projected_grad, joined, 1, 1).astype(jnp.bfloat...  16.2 us
    unnamed x48, local copies, waits for them, and re-layouts  15 us
    pallas_call x1, Pallas kernels, finish(): pl.pallas_call(finish_kernel, grid_spec=pltpu.PrefetchScalarGridSpec(num_...  12.2 us
    all_gather x1, blocking collectives, local(): piece = lax.all_gather(attn_grad, 'tp', axis=0, tiled=True)  8.8 us
    all_to_all x2, starting transfers between devices, to_sources(): return lax.all_to_all(buffer, 'ep', split_axis=0, concat_axis=0, tiled=True)  7.87 us
    dot_general x8, matrix products, contract(): lax.dot_general(left, right, (((left_dim,), (right_dim,)), ((), ())), pre...  6.54 us
  transfers between devices with their start and end apart: 3, of which 2 were waited for; matrix products, arithmetic and copies ran while one was open for 7% of the time, Pallas kernels for 0%

profile of v2, /device:TPU:0, one launch (start us, length us, event | category | flops | bytes accessed | tf_op | source)
XLA Modules:
  0.0 290.2 jit_solution(4372417805100041621)
XLA Ops:
  7.2 1.3 reshape.269.b1_ref
  8.4 1.3 reshape.271.b2_ref
  9.7 1.3 reshape.270.g2_ref
  11.0 1.3 reshape.268.g1_ref
  12.2 1.4 copy.50
  13.7 1.4 copy.51
  15.1 1.9 copy.52.wq_ref
  17.0 1.9 copy.53.wk_ref
  18.8 1.9 copy.54.wv_ref
  20.7 56.1 %front.1 = (bf16[4,128,768]{2,1,0:T(8,128)(2,1)}, bf16[512,576]{1,0:T(8,128)(2,1)}, bf16[512,192]{1,0:T(8,128)(2,1)}, f32[512,8]{1,0:T(8,128)}, f32[128,768]{1,0...) custom-call(bf16[128,768]{1,0:T(8,128)(2,1)} %bitcast.108, ...), custom_call_target="tpu_custom_call" | custom-call | tf_op jit(solution)/shard_map/front/pallas_call | solution.py:319
  76.9 4.3 %all-to-all-start.1 = ((bf16[2,2,128,768]{3,2,1,0:T(8,128)(2,1)}), bf16[2,2,128,768]{3,2,1,0:T(8,128)(2,1)S(1)}, u32[]{:S(2)}, u32[]{:S(2)}) async-start(bf16[2,2,128,768]{3,2,1,0:T(8,128)(2,1)} %get-tuple-element.78), calls=%async_computation.1 | async-start | bytes 1572864 | tf_op jit(solution)/shard_map/all_to_all | solution.py:750
  81.6 1.2 reduce-window.6
  84.8 0.2 compare_and_fusion
  85.1 5.1 %all-to-all-done.1 = bf16[2,2,128,768]{3,2,1,0:T(8,128)(2,1)S(1)} async-done(((bf16[2,2,128,768]{3,2,1,0:T(8,128)(2,1)}), bf16[2,2,128,768]{3,2,1,0:T(8,128)(2,1)S(1)}, u32[]{:S(2)}, u32[]{:S(2)}) %all-to-all-start.1) | async-done | bytes 786464 | tf_op jit(solution)/shard_map/all_to_all | solution.py:750
  90.2 3.5 %all-to-all-start = ((bf16[2,2,128,768]{3,2,1,0:T(8,128)(2,1)}), bf16[2,2,128,768]{3,2,1,0:T(8,128)(2,1)S(1)}, u32[]{:S(2)}, u32[]{:S(2)}) async-start(bf16[2,2,128,768]{3,2,1,0:T(8,128)(2,1)} %get-tuple-element.77), calls=%async_computation | async-start | bytes 1572864 | tf_op jit(solution)/shard_map/all_to_all | solution.py:750
  93.8 0.3 fusion.25
  94.1 0.4 multiply_reduce_fusion.1
  94.6 0.2 fusion.38
  94.8 0.2 copy-done.2
  95.1 8.8 %all_gather.3 = bf16[512,768]{1,0:T(8,128)(2,1)S(1)} all-gather(bf16[128,768]{1,0:T(8,128)(2,1)S(1)} %fusion.27), channel_id=1, replica_groups=mesh['tp'=4,'ep'=2,'dp'=4] {'tp'}, dimensions={0}, use_global_device_ids=true | all-gather | bytes 983040 | tf_op jit(solution)/shard_map/all_gather | solution.py:839
  103.9 0.4 convolution_convert_fusion.3
  104.3 0.6 fusion.40
  105.0 1.2 multiply_reduce_fusion
  106.1 0.6 fusion.7
  106.7 0.8 multiply_convert_fusion
  107.6 0.6 fusion.5
  108.2 0.4 fusion.6
  108.6 0.3 copy-done.14
  108.9 0.4 copy-done.15
  109.3 1.7 convolution_convert_fusion.1
  111.0 2.4 copy.66
  113.8 0.4 convolution_convert_fusion.2
  114.3 2.0 convolution_convert_fusion
  116.3 1.2 pad_maximum_fusion.pg_ref
  117.6 0.3 convolution_multiply_fusion.3
  117.9 1.0 fusion.10
  118.9 16.2 %reduce-scatter.2.cloned.1.call-done = bf16[128,768]{1,0:T(8,128)(2,1)} async-done(((bf16[512,768]{1,0:T(8,128)(2,1)}), bf16[128,768]{1,0:T(8,128)(2,1)}) %reduce-scatter.2.cloned.1.call-update) | async-done | bytes 196624 | tf_op jit(solution)/shard_map/reduce_scatter | solution.py:889
  135.2 1.1 fusion.22
  136.3 1.2 fusion.24
  137.6 0.6 stack.5.small_ref
  138.2 123.7 %grads.1 = (bf16[2,12,4,64,768]{4,3,2,1,0:T(8,128)(2,1)}, bf16[2,4,96,768]{3,2,1,0:T(8,128)(2,1)}, f32[8,768]{1,0:T(8,128)}) custom-call(bf16[4,2,128,768]{3,2,1,0:T(8,128)(2,1)} %get-tuple-element.81.gx_ref, bf16[4,2,128,768]{3,2,1,0:T(8,128)(2,1)} %get-tuple-element.82.gs_ref, bf16[768,3072]{1,0:T(8,128)(2,1)} %bitcast.101, bf16[3072,768]{1,0:T(8,128)(2,1)} %bitcast.103, ...), custom_call_target="tpu_custom_call" | custom-call | tf_op jit(solution)/shard_map/grads/pallas_call | solution.py:630
  261.9 1.2 convert_bitcast_fusion
  263.1 1.5 slice_reduce_fusion.4
  264.7 12.2 %finish.1 = (f32[768,3072]{1,0:T(8,128)}, f32[3072,768]{1,0:T(8,128)}, f32[768,192]{1,0:T(8,128)}, f32[768,192]{1,0:T(8,128)}, f32[768,192]{1,0:T(8,128)}, /*index=5*/f32[192,768]{1,0:T(8,128)}) custom-call(s32[1]{0:T(128)} %bitcast.40.tp_ref, bf16[2,12,4,64,768]{4,3,2,1,0:T(8,128)(2,1)} %get-tuple-element.86.rg_ref, bf16[768,768]{1,0:T(8,128)(2,1)} %bitcast.120), custom_call_target="tpu_custom_call" | custom-call | tf_op jit(solution)/shard_map/finish/pallas_call | solution.py:698
  276.8 2.3 copy.68
  279.1 2.2 copy.69
  281.3 1.1 copy.70
  282.4 1.0 add_bitcast_fusion
  (83 shorter events, 3.1 us)
Async XLA Ops:
  20.7 60.5 %copy-start.19 = (s32[1,512]{1,0:T(1,128)S(1)}, s32[1,512]{1,0:T(1,128)}, u32[]{:S(2)}) copy-start(s32[1,512]{1,0:T(1,128)} %key_ref.1) | copy-start | bytes 6148
  20.7 60.5 %copy-start.17 = (s32[1,512]{1,0:T(1,128)S(1)}, s32[1,512]{1,0:T(1,128)}, u32[]{:S(2)}) copy-start(s32[1,512]{1,0:T(1,128)} %seg_ref.1) | copy-start | bytes 6148
  20.7 60.6 %copy-start.4 = (s32[1,128,2]{2,1,0:T(8,128)S(1)}, s32[1,128,2]{2,1,0:T(8,128)}, u32[]{:S(2)}) copy-start(s32[1,128,2]{2,1,0:T(8,128)} %copy.50) | copy-start | bytes 3076
  76.8 6.7 %copy-start = (f32[128,768]{1,0:T(8,128)S(1)}, f32[128,768]{1,0:T(8,128)}, u32[]{:S(2)}) copy-start(f32[128,768]{1,0:T(8,128)} %get-tuple-element.76) | copy-start | bytes 1179652
  76.9 7.0 %copy-start.12 = (f32[512,8]{1,0:T(8,128)S(1)}, f32[512,8]{1,0:T(8,128)}, u32[]{:S(2)}) copy-start(f32[512,8]{1,0:T(8,128)} %get-tuple-element.80) | copy-start | bytes 49156
  76.9 7.0 %copy-start.7 = (bf16[512,576]{1,0:T(8,128)(2,1)S(1)}, bf16[512,576]{1,0:T(8,128)(2,1)}, u32[]{:S(2)}) copy-start(bf16[512,576]{1,0:T(8,128)(2,1)} %get-tuple-element.79) | copy-start | bytes 1769476
  76.9 13.3 %all-to-all-start.1 = ((bf16[2,2,128,768]{3,2,1,0:T(8,128)(2,1)}), bf16[2,2,128,768]{3,2,1,0:T(8,128)(2,1)S(1)}, u32[]{:S(2)}, u32[]{:S(2)}) async-start(bf16[2,2,128,768]{3,2,1,0:T(8,128)(2,1)} %get-tuple-element.78), calls=%async_computation.1 | async-start | bytes 1572864 | tf_op jit(solution)/shard_map/all_to_all | solution.py:750
  84.5 9.6 %copy-start.18 = (f32[768]{0:T(1024)S(1)}, f32[768]{0:T(1024)}, u32[]{:S(2)}) copy-start(f32[768]{0:T(1024)} %param.31) | copy-start | bytes 9220
  90.2 27.4 %all-to-all-start = ((bf16[2,2,128,768]{3,2,1,0:T(8,128)(2,1)}), bf16[2,2,128,768]{3,2,1,0:T(8,128)(2,1)S(1)}, u32[]{:S(2)}, u32[]{:S(2)}) async-start(bf16[2,2,128,768]{3,2,1,0:T(8,128)(2,1)} %get-tuple-element.77), calls=%async_computation | async-start | bytes 1572864 | tf_op jit(solution)/shard_map/all_to_all | solution.py:750
  93.7 41.4 %reduce-scatter.2.cloned.1.call-start = ((), (), s32[]{:S(2)}) async-start(), calls=%async_computation.3 | async-start | bytes 983040 | tf_op jit(solution)/shard_map/reduce_scatter | solution.py:889
  94.1 0.9 copy-start.2
  94.5 9.4 %copy-start.5 = (bf16[192,768]{1,0:T(8,128)(2,1)S(1)}, bf16[192,768]{1,0:T(8,128)(2,1)}, u32[]{:S(2)}) copy-start(bf16[192,768]{1,0:T(8,128)(2,1)} %wo_ref.1) | copy-start | bytes 884740
  107.6 1.7 copy-start.9
  107.6 1.7 copy-start.10
  107.6 1.7 copy-start.11
  108.2 0.7 copy-start.14
  108.6 0.7 copy-start.15
  111.0 2.4 copy-start.6
  111.0 2.6 copy-start.1
  111.0 2.8 copy-start.13
  117.6 17.6 %copy-start.16 = (f32[768]{0:T(1024)S(1)}, f32[768]{0:T(1024)}, u32[]{:S(2)}) copy-start(f32[768]{0:T(1024)} %param.25) | copy-start | bytes 9220
  276.8 4.5 %copy-start.8 = (f32[768,192]{1,0:T(8,128)S(1)}, f32[768,192]{1,0:T(8,128)}, u32[]{:S(2)}) copy-start(f32[768,192]{1,0:T(8,128)} %get-tuple-element.113) | copy-start | bytes 1769476
  276.8 5.6 %copy-start.3 = (bf16[128,768]{1,0:T(8,128)(2,1)S(1)}, bf16[128,768]{1,0:T(8,128)(2,1)}, u32[]{:S(2)}) copy-start(bf16[128,768]{1,0:T(8,128)(2,1)} %reduce-scatter.2.cloned.1.call-done) | copy-start | bytes 589828
Sparse Core Ops, SparseCore 0:
  111.1 23.9 reduce-scatter.1

commit v3 on v2

v3 whole, which is shorter than its diff:
```python
import functools
import math

import jax
import jax.numpy as jnp
from jax import lax
from jax.experimental import pallas as pl
from jax.experimental.pallas import tpu as pltpu
from jax.sharding import PartitionSpec as P

HD = 64
EXP_DEV = 2
EPSILON = 1e-05
MASKED = -1e30
MESH = pl.DeviceIdType.MESH
BF = jnp.bfloat16
F32 = jnp.float32
CHUNK = 32


def tp_peers():
    me = lax.axis_index("tp")
    one = me + 1 - 2 * (me % 2)
    return (me, one, (me + 2) % 4, (one + 2) % 4)


def remote(src, dst, send, recv, where):
    return pltpu.make_async_remote_copy(
        src_ref=src, dst_ref=dst, send_sem=send, recv_sem=recv,
        device_id=where, device_id_type=MESH,
    )


def entry_barrier(ep_count, dp_count):
    barrier = pltpu.get_barrier_semaphore()
    _, tp1, tp2, tp3 = tp_peers()
    ep, dp = lax.axis_index("ep"), lax.axis_index("dp")
    for peer in (tp1, tp2, tp3):
        pl.semaphore_signal(barrier, inc=1, device_id={"tp": peer}, device_id_type=MESH)
    for off in range(1, ep_count):
        pl.semaphore_signal(
            barrier, inc=1, device_id={"ep": (ep + off) % ep_count}, device_id_type=MESH
        )
    for off in range(1, dp_count):
        pl.semaphore_signal(
            barrier, inc=1, device_id={"dp": (dp + off) % dp_count}, device_id_type=MESH
        )
    pl.semaphore_wait(barrier, 3 + ep_count - 1 + dp_count - 1)


def gelu_pair(hidden):
    phi = 0.5 * (1.0 + lax.erf(hidden * math.sqrt(0.5)))
    dens = jnp.exp(-0.5 * hidden * hidden) * (1.0 / math.sqrt(2.0 * math.pi))
    return hidden * phi, phi + hidden * dens


def row_of(ref):
    return ref[...].reshape(1, -1)


def columns_of(ref):
    value = ref[...].astype(F32)
    padded = jnp.concatenate([value, jnp.zeros((6, value.shape[1]), F32)], axis=0)
    flipped = padded.T
    return flipped[:, 0:1], flipped[:, 1:2]


def fill_bias(seg_ref, key_ref, bias):
    segment = seg_ref[...]
    group_rows = segment.shape[1]
    lane = lax.broadcasted_iota(jnp.int32, segment.shape, 1)
    starts = (segment != pltpu.roll(segment, 1, 1)) | (lane == 0)
    keep = (key_ref[...] == 1) | starts
    segment = segment.astype(F32)
    column = jnp.broadcast_to(segment, (8, group_rows)).T[:, 0:1]
    kept = jnp.where(keep, segment, -1.0)
    bias[...] = jnp.where(column == kept, 0.0, MASKED)


def ln_rows(values, gain, bias):
    center = jnp.mean(values, axis=-1, keepdims=True)
    shifted = values - center
    spread = jnp.mean(shifted * shifted, axis=-1, keepdims=True)
    return shifted * lax.rsqrt(spread + EPSILON) * gain + bias


def route_picks(routes_ref, capacity, slots):
    first, second = (column.astype(jnp.int32) for column in columns_of(routes_ref))
    rows = first.shape[0]
    lane = lax.broadcasted_iota(jnp.int32, (rows, 128), 1)
    marks = jnp.where((lane == first) | (lane == second), 1.0, 0.0)
    row_id = lax.broadcasted_iota(jnp.int32, (rows, rows), 0)
    col_id = lax.broadcasted_iota(jnp.int32, (rows, rows), 1)
    lower = jnp.where(row_id > col_id, 1.0, 0.0).astype(BF)
    before = jnp.dot(lower, marks.astype(BF), preferred_element_type=F32)
    slot = lax.broadcasted_iota(jnp.int32, (rows, slots), 1)
    picks = []
    for route in (first, second):
        place = jnp.sum(jnp.where(lane == route, before, 0.0), axis=1, keepdims=True)
        chosen = route * capacity + place.astype(jnp.int32)
        picks.append(jnp.where(slot == chosen, 1.0, 0.0).astype(BF))
    return picks[0], picks[1], marks


def dot_tn(left, right):
    return lax.dot_general(left, right, (((0,), (0,)), ((), ())), preferred_element_type=F32)


def dot_nt(left, right):
    return lax.dot_general(left, right, (((1,), (1,)), ((), ())), preferred_element_type=F32)


def dot_nn(left, right):
    return jnp.dot(left, right, preferred_element_type=F32)


def front_kernel(
    ep_count, heads,
    tok_ref, seg_ref, key_ref, routes_ref, gates_ref, cot_ref, g1_ref, b1_ref, wq_ref, wk_ref, wv_ref, wo_ref,
    g2_ref, b2_ref, fin_hbm, fout_hbm, tin_hbm, tout_hbm,
    group_ref, qkv_ref, heads_ref, lse_ref, middle_ref, back_ref, out_ref, gx, gs,
    weights, joined, bias, part, core_slot, mix, x_slot, sx, ss, ax, as_, out_acc, back_acc,
    w_sem, a_send, a_recv, c_send, c_recv, m_send, m_recv, e_send, e_recv, t_send, t_recv,
):
    tp, tp1, tp2, tp3 = tp_peers()
    ep = lax.axis_index("ep")
    rows, width = tok_ref.shape
    cols = wq_ref.shape[0]
    hidden = fin_hbm.shape[1]
    capacity = sx.shape[2]
    slots = ep_count * EXP_DEV * capacity
    loads = []
    for index, source in enumerate((fin_hbm, tin_hbm)):
        loads.append(pltpu.make_async_copy(source, weights[0].at[index], w_sem.at[0, index]))
    for index, source in enumerate((fout_hbm, tout_hbm)):
        loads.append(pltpu.make_async_copy(source, weights[1].at[index], w_sem.at[1, index]))

    barrier = pltpu.get_barrier_semaphore()
    for peer in (tp1, tp2, tp3):
        pl.semaphore_signal(barrier, inc=1, device_id={"tp": peer}, device_id_type=MESH)
    for off in range(1, ep_count):
        pl.semaphore_signal(
            barrier, inc=1, device_id={"ep": (ep + off) % ep_count}, device_id_type=MESH
        )
    residual = tok_ref[...].astype(F32)
    group_ref[tp] = ln_rows(residual, row_of(g1_ref), row_of(b1_ref)).astype(BF)
    pl.semaphore_wait(barrier, 3 + ep_count - 1)

    def gather_copy(slot, index, peer):
        return remote(group_ref.at[slot], group_ref.at[slot], a_send.at[index], a_recv.at[index], {"tp": peer})

    sends = [gather_copy(tp, 1, tp2), gather_copy(tp, 0, tp1)]
    for copy in sends:
        copy.start()
    for copy in (loads[0], loads[2], loads[1], loads[3]):
        copy.start()

    pick0, pick1, _ = route_picks(routes_ref, capacity, slots)
    upstream = cot_ref[...].astype(F32)
    gate0, gate1 = columns_of(gates_ref)
    share0 = (gate0 * upstream).astype(BF)
    share1 = (gate1 * upstream).astype(BF)
    ss[...] = (dot_tn(pick0, share0) + dot_tn(pick1, share1)).astype(BF).reshape(ss.shape)

    def owner_copies(kind, source, target):
        return [
            remote(
                source.at[(ep + off) % ep_count], target.at[ep], e_send.at[kind, off - 1], e_recv.at[kind, off - 1],
                {"ep": (ep + off) % ep_count},
            )
            for off in range(1, ep_count)
        ]

    def owner_waits(kind, target):
        for off in range(1, ep_count):
            source = (ep + ep_count - off) % ep_count
            remote(
                target.at[source], target.at[source], e_send.at[kind, off - 1], e_recv.at[kind, off - 1],
                {"ep": source},
            ).wait_recv()

    share_sends = owner_copies(1, ss, as_)
    for copy in share_sends:
        copy.start()
    as_[ep] = ss[ep]

    for index, ref in enumerate((wq_ref, wk_ref, wv_ref)):
        joined[index * cols : (index + 1) * cols, :] = ref[...]

    group_rows = seg_ref.shape[1]
    fill_bias(seg_ref, key_ref, bias)

    def project(slot):
        at = pl.ds(pl.multiple_of(slot * rows, rows), rows)
        qkv_ref[at, :] = dot_nt(group_ref[slot], joined[...]).astype(BF)

    project(tp)
    gather_copy(tp1, 0, tp1).wait_recv()
    project(tp1)
    gather_copy(tp2, 1, tp2).wait_recv()
    sends.append(gather_copy(tp2, 2, tp1))
    sends[-1].start()
    project(tp2)
    gather_copy(tp3, 2, tp1).wait_recv()
    project(tp3)

    def token_copy(kind, buf, source, hop, peer):
        return remote(source, buf.at[hop], t_send.at[kind, hop - 1], t_recv.at[kind, hop - 1], {"tp": peer})

    owner_waits(1, as_)
    train = EXP_DEV - 1
    token_sends = [
        token_copy(1, gs, as_.at[:, train], 2, tp2), token_copy(1, gs, as_.at[:, train], 1, tp1)
    ]
    for copy in token_sends:
        copy.start()
    gs[0] = as_[:, train]

    scale = HD ** (-0.5)
    block = min(256, group_rows)
    for head in range(heads):
        def attend(index, _, head=head):
            at = pl.ds(pl.multiple_of(index * block, block), block)
            query = qkv_ref[at, head * HD : (head + 1) * HD]
            keys = qkv_ref[:, cols + head * HD : cols + (head + 1) * HD]
            values = qkv_ref[:, 2 * cols + head * HD : 2 * cols + (head + 1) * HD]
            scores = dot_nt(query, keys) * scale + bias[at, :]
            highest = jnp.max(scores, axis=-1, keepdims=True)
            weight = jnp.exp(scores - highest)
            total = jnp.sum(weight, axis=-1, keepdims=True)
            probs = (weight * (1.0 / total)).astype(BF)
            heads_ref[at, head * HD : (head + 1) * HD] = dot_nn(probs, values).astype(BF)
            lse_ref[at, head : head + 1] = highest + jnp.log(total)
            return 0

        for index in range(group_rows // block):
            attend(index, 0)

    def partial(slot):
        at = pl.ds(pl.multiple_of(slot * rows, rows), rows)
        return dot_nn(heads_ref[at, :], wo_ref[...])

    def core_copy(index):
        return remote(part.at[index], core_slot.at[index], c_send.at[index], c_recv.at[index], {"tp": tp1})

    part[0] = partial(tp3)
    core_copy(0).start()
    part[1] = partial(tp1)
    core_copy(1).start()
    crossing = partial(tp2)
    own = residual + partial(tp)
    token_copy(1, gs, as_.at[:, train], 2, tp2).wait_recv()
    token_sends.append(token_copy(1, gs, gs.at[2], 3, tp1))
    token_sends[-1].start()
    core_copy(0).wait_recv()
    mix[...] = (crossing + core_slot[0]).astype(BF)
    cross = remote(mix, x_slot, m_send, m_recv, {"tp": tp2})
    cross.start()
    core_copy(1).wait_recv()
    own = own + core_slot[1]
    cross.wait_recv()
    middle = own + x_slot[...].astype(F32)
    middle_ref[...] = middle
    normed = ln_rows(middle, row_of(g2_ref), row_of(b2_ref)).astype(BF)
    sx[...] = dot_tn(pick0 + pick1, normed).astype(BF).reshape(sx.shape)
    input_sends = owner_copies(0, sx, ax)
    for copy in input_sends:
        copy.start()
    ax[ep] = sx[ep]
    for copy in loads:
        copy.wait()
    owner_waits(0, ax)
    token_sends.append(token_copy(0, gx, ax.at[:, train], 2, tp2))
    token_sends.append(token_copy(0, gx, ax.at[:, train], 1, tp1))
    for copy in token_sends[-2:]:
        copy.start()
    gx[0] = ax[:, train]

    step = width
    for expert in range(EXP_DEV):
        inputs = ax[:, expert].reshape(-1, width)
        shares = as_[:, expert].reshape(-1, width)

        def piece(index, _, expert=expert, inputs=inputs, shares=shares):
            at = pl.ds(pl.multiple_of(index * step, step), step)
            inner, outer = weights[0].at[expert], weights[1].at[expert]
            before = dot_nn(inputs, inner[:, at])
            through = dot_nt(shares, outer[at, :])
            value, grad = gelu_pair(before)
            slope = (through * grad).astype(BF)
            produced = dot_nn(value.astype(BF), outer[at, :])
            returned = dot_nt(slope, inner[:, at])

            @pl.when(index == 0)
            def _():
                out_acc[...] = produced
                back_acc[...] = returned

            @pl.when(index > 0)
            def _():
                out_acc[...] += produced
                back_acc[...] += returned

            return 0

        lax.fori_loop(0, hidden // step, piece, 0)
        out_ref[:, expert] = out_acc[...].astype(BF).reshape(ep_count, capacity, width)
        back_ref[:, expert] = back_acc[...].astype(BF).reshape(ep_count, capacity, width)
        if expert == 0:
            token_copy(0, gx, ax.at[:, train], 2, tp2).wait_recv()
            token_sends.append(token_copy(0, gx, gx.at[2], 3, tp1))
            token_sends[-1].start()

    for kind, buf in ((0, gx), (1, gs)):
        token_copy(kind, buf, buf.at[1], 1, tp1).wait_recv()
        token_copy(kind, buf, buf.at[3], 3, tp1).wait_recv()
    for copy in sends + share_sends + input_sends + token_sends + [core_copy(0), core_copy(1), cross]:
        copy.wait_send()


def front(tokens, segment, key_mask, routes, gates, cot, g1, b1, wq, wk, wv, wo, g2, b2, fin, fout, tin, tout):
    ep_count = lax.axis_size("ep")
    rows, width = tokens.shape
    group_rows = segment.shape[1]
    cols = wq.shape[0]
    hidden = fin.shape[1]
    experts = EXP_DEV * ep_count
    capacity = 4 * rows // experts
    dma = pltpu.SemaphoreType.DMA
    vmem = pl.BlockSpec(memory_space=pltpu.VMEM)
    hbm = pl.BlockSpec(memory_space=pl.ANY)
    struct = jax.ShapeDtypeStruct
    block = (ep_count, EXP_DEV, capacity, width)
    gathered = (4, ep_count, capacity, width)
    others = ep_count - 1
    return pl.pallas_call(
        functools.partial(front_kernel, ep_count, cols // HD),
        out_shape=(
            struct((4, rows, width), BF),
            struct((group_rows, 3 * cols), BF),
            struct((group_rows, cols), BF),
            struct((group_rows, 8), F32),
            struct((rows, width), F32),
            struct(block, BF), struct(block, BF), struct(gathered, BF), struct(gathered, BF),
        ),
        in_specs=[vmem] * 14 + [hbm] * 4,
        out_specs=tuple([vmem] * 9),
        scratch_shapes=[
            [pltpu.VMEM((2, width, hidden), BF), pltpu.VMEM((2, hidden, width), BF)],
            pltpu.VMEM((3 * cols, width), BF),
            pltpu.VMEM((group_rows, group_rows), F32),
            pltpu.VMEM((2, rows, width), F32),
            pltpu.VMEM((2, rows, width), F32),
            pltpu.VMEM((rows, width), BF),
            pltpu.VMEM((rows, width), BF),
            pltpu.VMEM(block, BF), pltpu.VMEM(block, BF), pltpu.VMEM(block, BF), pltpu.VMEM(block, BF),
            pltpu.VMEM((ep_count * capacity, width), F32),
            pltpu.VMEM((ep_count * capacity, width), F32),
            dma((2, 2)), dma((3,)), dma((3,)), dma((2,)), dma((2,)), dma(()), dma(()),
            dma((2, others)), dma((2, others)), dma((2, 3)), dma((2, 3)),
        ],
        compiler_params=pltpu.CompilerParams(
            collective_id=1, has_side_effects=True, vmem_limit_bytes=62 * 1024 * 1024
        ),
        name="front",
    )(tokens, segment, key_mask, routes, gates, cot, g1, b1, wq, wk, wv, wo, g2, b2, fin, fout, tin, tout)


def ln_backward(values, gain, upstream):
    center = jnp.mean(values, axis=-1, keepdims=True)
    shifted = values - center
    spread = jnp.mean(shifted * shifted, axis=-1, keepdims=True)
    scale = lax.rsqrt(spread + EPSILON)
    unit = shifted * scale
    inner = upstream * gain
    along = jnp.mean(inner * unit, axis=-1, keepdims=True)
    grad = scale * (inner - jnp.mean(inner, axis=-1, keepdims=True) - unit * along)
    return grad, jnp.sum(upstream * unit, axis=0, keepdims=True), jnp.sum(upstream, axis=0, keepdims=True)


class Chain:
    def __init__(self, base, count, own, stage, red_a, red_b, final, sems, hooks):
        self.base, self.count, self.own, self.stage = base, count, own, stage
        self.red_a, self.red_b, self.final, self.hooks = red_a, red_b, final, hooks
        self.red_send, self.recv_a, self.recv_b, self.bc_send, self.bc_recv = sems
        self.dp = lax.axis_index("dp")

    def place(self, half):
        return 3 - self.dp if half == 0 else self.dp

    def peers(self, half):
        down, up = (self.dp + 3) % 4, (self.dp + 1) % 4
        return (down, up) if half == 0 else (up, down)

    def red(self, half, index, near):
        toward, away = self.peers(half)
        target, sem = (self.red_b, self.recv_b) if near else (self.red_a, self.recv_a)
        return remote(
            self.stage.at[half, index], target.at[half, index], self.red_send.at[half, index], sem.at[half, index],
            {"dp": away if near else toward},
        )

    def spread(self, half, index, near):
        toward, away = self.peers(half)
        ref = self.final(half, index)
        return remote(
            ref, ref, self.bc_send.at[1 if near else 0, half, index], self.bc_recv.at[half, index],
            {"dp": toward if near else away},
        )

    def step(self, s):
        for half in (0, 1):
            place = self.place(half)
            index = s - self.base - (2 * place - 4 * (place // 3))

            @pl.when((index >= 0) & (index < self.count))
            def _():
                own = self.own(half, index)

                @pl.when(place == 0)
                def _():
                    self.stage[half, index] = own.astype(BF)
                    self.red(half, index, False).start()

                @pl.when(place == 3)
                def _():
                    self.stage[half, index] = own.astype(BF)
                    self.red(half, index, True).start()

                @pl.when(place == 1)
                def _():
                    self.red(half, index, False).wait_recv()
                    self.stage[half, index] = (own + self.red_a[half, index].astype(F32)).astype(BF)
                    self.red(half, index, False).start()

                @pl.when(place == 2)
                def _():
                    self.red(half, index, False).wait_recv()
                    self.red(half, index, True).wait_recv()
                    total = own + self.red_a[half, index].astype(F32) + self.red_b[half, index].astype(F32)
                    self.final(half, index)[...] = total.astype(BF)

        for half in (0, 1):
            place = self.place(half)
            index = s - self.base - (8 - 2 * place + 4 * (place // 3))

            @pl.when((index >= 0) & (index < self.count))
            def _():
                @pl.when(place == 2)
                def _():
                    self.spread(half, index, False).start()
                    self.spread(half, index, True).start()

                @pl.when(place != 2)
                def _():
                    self.spread(half, index, False).wait_recv()

                @pl.when(place == 1)
                def _():
                    self.spread(half, index, False).start()

                self.hooks[0](half, index)

            for later, hook in enumerate(self.hooks[1:]):
                after = index - 2 * (later + 1)
                pl.when((after >= 0) & (after < self.count))(functools.partial(hook, half, after))

    def drain(self, index):
        for half in (0, 1):
            place = self.place(half)

            @pl.when(place != 2)
            def _():
                self.red(half, index, False).wait_send()

            @pl.when((place == 1) | (place == 2))
            def _():
                self.spread(half, index, False).wait_send()

            @pl.when(place == 2)
            def _():
                self.spread(half, index, True).wait_send()


def back_kernel(
    ep_count, heads, n,
    tok_ref, seg_ref, key_ref, routes_ref, gates_ref, cot_ref, g1_ref, wq_ref, wk_ref, wv_ref, wo_ref, g2_ref,
    group_ref, qkv_ref, heads_ref, lse_ref, middle_ref, back_ref, out_ref, gx_ref, gs_ref, w_in_hbm, w_out_hbm,
    rg_hbm, pfin, small_out, grad_ref, layer_ref,
    w_in, w_out, act, slope, own, red_a, red_b, stage, fin, acc, pred_a, pred_b, pstage, pgbuf, yslot,
    ret_back, ret_out, piece, up_heads, pgrad, joined, bias, part, core_slot, mix, x_slot,
    sm, sm_tp, sm_ep, sm_dp, sm_a, sm_b,
    w_sem, red_send, recv_a, recv_b, bc_send, bc_recv, x_send, x_recv, out_sem,
    pred_send, precv_a, precv_b, pbc_send, pbc_recv, y_send, y_recv, g_send, g_recv,
    b_send, b_recv, a_send, a_recv, c_send, c_recv, m_send, m_recv, s_send, s_recv,
):
    tp, tp1, tp2, tp3 = tp_peers()
    ep, dp = lax.axis_index("ep"), lax.axis_index("dp")
    quarter, width = w_out.shape
    rows = tok_ref.shape[0]
    group_rows = qkv_ref.shape[0]
    cols = wq_ref.shape[0]
    start = pl.multiple_of(tp * quarter, quarter)
    in_copy = pltpu.make_async_copy(w_in_hbm.at[:, pl.ds(start, quarter)], w_in, w_sem.at[0])
    out_copy = pltpu.make_async_copy(w_out_hbm.at[pl.ds(start, quarter), :], w_out, w_sem.at[1])
    in_copy.start()
    out_copy.start()
    entry_barrier(ep_count, 4)

    def ep_copies(kind, source, target):
        return [
            remote(
                source.at[(ep + off) % ep_count], target.at[ep], b_send.at[kind, off - 1], b_recv.at[kind, off - 1],
                {"ep": (ep + off) % ep_count},
            )
            for off in range(1, ep_count)
        ]

    def ep_waits(kind, target):
        for off in range(1, ep_count):
            source = (ep + ep_count - off) % ep_count
            remote(
                target.at[source], target.at[source], b_send.at[kind, off - 1], b_recv.at[kind, off - 1],
                {"ep": source},
            ).wait_recv()

    sends = ep_copies(0, back_ref, ret_back) + ep_copies(1, out_ref, ret_out)
    for copy in sends:
        copy.start()
    ret_back[ep] = back_ref[ep]
    ret_out[ep] = out_ref[ep]
    in_copy.wait()
    out_copy.wait()

    tokens = gx_ref.shape[1] * gx_ref.shape[2]

    def hidden_block(index, _):
        hidden = dot_nn(gx_ref[index].reshape(tokens, width), w_in[...])
        through = dot_nt(gs_ref[index].reshape(tokens, width), w_out[...])
        value, grad = gelu_pair(hidden)
        at = pl.ds(pl.multiple_of(index * tokens, tokens), tokens)
        act[at, :] = value.astype(BF)
        slope[at, :] = (through * grad).astype(BF)
        return 0

    lax.fori_loop(0, 4, hidden_block, 0)
    span = 128

    def outer(index, _):
        at = pl.ds(pl.multiple_of(index * span, span), span)
        own[0, at, :] = dot_tn(gx_ref[:, :, :, at].reshape(-1, span), slope[...])
        own[1, at, :] = dot_tn(act[:, at], gs_ref[...].reshape(-1, width))
        return 0

    lax.fori_loop(0, width // span, outer, 0)

    def x_copy(half, index, hop):
        source, peer = ((0, tp1), (0, tp2), (2, tp1))[hop - 1]
        return remote(
            fin.at[half, index, source], fin.at[half, index, hop],
            x_send.at[hop - 1, half, index], x_recv.at[hop - 1, half, index], {"tp": peer},
        )

    def out_copy_of(half, index):
        return pltpu.make_async_copy(fin.at[half, index], rg_hbm.at[half, index], out_sem.at[half, index])

    def cross_first(half, index):
        x_copy(half, index, 2).start()
        x_copy(half, index, 1).start()

    def cross_second(half, index):
        x_copy(half, index, 2).wait_recv()
        x_copy(half, index, 3).start()

    def cross_third(half, index):
        x_copy(half, index, 1).wait_recv()
        x_copy(half, index, 3).wait_recv()
        out_copy_of(half, index).start()

    expert_chain = Chain(
        0, n, lambda half, index: own[half, pl.ds(pl.multiple_of(index * CHUNK, CHUNK), CHUNK), :],
        stage, red_a, red_b, lambda half, index: fin.at[half, index, 0],
        (red_send, recv_a, recv_b, bc_send, bc_recv), (cross_first, cross_second, cross_third),
    )

    def y_gather(half, index, off):
        chunk = 2 * index + half
        return remote(
            pfin.at[ep, chunk], pfin.at[ep, chunk], g_send.at[off - 1, half, index], g_recv.at[off - 1, half, index],
            {"ep": (ep + off) % ep_count},
        )

    def y_first(half, index):
        for off in range(1, ep_count):
            y_gather(half, index, off).start()

    proj_n = acc.shape[0] // 2
    proj_chain = Chain(
        n, proj_n, lambda half, index: acc[2 * index + half], pstage, pred_a, pred_b,
        lambda half, index: pfin.at[ep, 2 * index + half],
        (pred_send, precv_a, precv_b, pbc_send, pbc_recv), (y_first,),
    )
    clock = [0]

    def run(count, proj=False):
        def body(s, _):
            expert_chain.step(s)
            if proj:
                proj_chain.step(s)
            return 0

        lax.fori_loop(clock[0], clock[0] + count, body, 0)
        clock[0] += count
        assert proj or clock[0] <= n

    run(2)
    capacity = back_ref.shape[2]
    slots = ep_count * EXP_DEV * capacity
    pick0, pick1, marks = route_picks(routes_ref, capacity, slots)
    upstream = cot_ref[...].astype(F32)
    middle = middle_ref[...]
    ep_waits(0, ret_back)
    second = dot_nn(pick0 + pick1, ret_back[...].reshape(slots, width))
    inner_grad, gain_two, bias_two = ln_backward(middle, row_of(g2_ref), second)
    middle_grad = upstream + inner_grad
    grad_ref[...] = middle_grad
    piece[tp] = middle_grad.astype(BF)

    def gather_copy(slot, index, peer):
        return remote(piece.at[slot], piece.at[slot], a_send.at[index], a_recv.at[index], {"tp": peer})

    sends += [gather_copy(tp, 1, tp2), gather_copy(tp, 0, tp1)]
    for copy in sends[-2:]:
        copy.start()
    sm[...] = jnp.zeros_like(sm)
    sm[2:3, :] = gain_two
    sm[3:4, :] = bias_two
    sm[4:5, 0:128] = jnp.sum(marks, axis=0, keepdims=True)
    for index, ref in enumerate((wq_ref, wk_ref, wv_ref)):
        joined[index * cols : (index + 1) * cols, :] = ref[...]
    fill_bias(seg_ref, key_ref, bias)
    run(1)

    def head_rows(slot):
        at = pl.ds(pl.multiple_of(slot * rows, rows), rows)
        up_heads[at, :] = dot_nt(piece[slot], wo_ref[...]).astype(BF)

    head_rows(tp)
    gather_copy(tp1, 0, tp1).wait_recv()
    head_rows(tp1)
    gather_copy(tp2, 1, tp2).wait_recv()
    sends.append(gather_copy(tp2, 2, tp1))
    sends[-1].start()
    head_rows(tp2)
    run(1)
    gather_copy(tp3, 2, tp1).wait_recv()
    head_rows(tp3)

    def y_scatter(batch, off):
        peer = (ep + off) % ep_count
        return remote(
            pgbuf.at[batch, peer], yslot.at[batch, off - 1], y_send.at[batch, off - 1], y_recv.at[batch, off - 1],
            {"ep": peer},
        )

    def proj_start(batch, value):
        pgbuf[batch] = value.astype(BF).reshape(pgbuf.shape[1:])
        for off in range(1, ep_count):
            y_scatter(batch, off).start()

    def proj_sum(batch):
        total = pgbuf[batch, ep].astype(F32)
        for off in range(1, ep_count):
            y_scatter(batch, off).wait_recv()
            total = total + yslot[batch, off - 1].astype(F32)
        acc[3 * batch : 3 * batch + 3] = total.reshape((3,) + acc.shape[1:])

    proj_start(0, dot_tn(heads_ref[...], piece[...].reshape(group_rows, width)))
    run(1)
    scale = HD ** (-0.5)
    block = min(256, group_rows)
    for head in range(heads):
        low, high = head * HD, (head + 1) * HD
        key_sum = value_sum = None
        for index in range(group_rows // block):
            at = slice(index * block, (index + 1) * block)
            query = qkv_ref[at, low:high]
            keys = qkv_ref[:, cols + low : cols + high]
            values = qkv_ref[:, 2 * cols + low : 2 * cols + high]
            above = up_heads[at, low:high]
            scores = dot_nt(query, keys) * scale + bias[at, :]
            probs = jnp.exp(scores - lse_ref[at, head : head + 1])
            prob_grad = dot_nt(above, values)
            centered = jnp.sum(probs * prob_grad, axis=-1, keepdims=True)
            score_grad = (probs * (prob_grad - centered)).astype(BF)
            pgrad[at, low:high] = (dot_nn(score_grad, keys) * scale).astype(BF)
            key_part = dot_tn(score_grad, query)
            value_part = dot_tn(probs.astype(BF), above)
            key_sum = key_part if key_sum is None else key_sum + key_part
            value_sum = value_part if value_sum is None else value_sum + value_part
            if index + 1 == group_rows // block:
                pgrad[:, cols + low : cols + high] = (key_sum * scale).astype(BF)
                pgrad[:, 2 * cols + low : 2 * cols + high] = value_sum.astype(BF)
            run(1)

    def partial(slot):
        at = pl.ds(pl.multiple_of(slot * rows, rows), rows)
        return dot_nn(pgrad[at, :], joined[...])

    def core_copy(index):
        return remote(part.at[index], core_slot.at[index], c_send.at[index], c_recv.at[index], {"tp": tp1})

    part[0] = partial(tp3).astype(BF)
    core_copy(0).start()
    part[1] = partial(tp1).astype(BF)
    core_copy(1).start()
    crossing = partial(tp2)
    mine = partial(tp)
    core_copy(0).wait_recv()
    mix[...] = (crossing + core_slot[0].astype(F32)).astype(BF)
    cross = remote(mix, x_slot, m_send, m_recv, {"tp": tp2})
    cross.start()
    normed = group_ref[...].reshape(group_rows, width)
    for batch, part_index in ((1, 2), (2, 0), (3, 1)):
        proj_start(batch, dot_tn(pgrad[:, part_index * cols : (part_index + 1) * cols], normed))
        run(1)
    core_copy(1).wait_recv()
    cross.wait_recv()
    first = mine + core_slot[1].astype(F32) + x_slot[...].astype(F32)
    residual_part, gain_one, bias_one = ln_backward(tok_ref[...].astype(F32), row_of(g1_ref), first)
    grad_ref[...] += residual_part
    sm[0:1, :] = gain_one
    sm[1:2, :] = bias_one

    small = []

    def small_copy(slot, source, target, where):
        small.append(remote(source, target, s_send.at[slot], s_recv.at[slot], where))
        small[-1].start()

    for hop, peer in ((1, tp1), (2, tp2), (3, tp3)):
        small_copy(hop - 1, sm, sm_tp.at[hop - 1], {"tp": peer})
    run(1)
    ep_waits(1, ret_out)
    returned = ret_out[...].reshape(slots, width)
    gate0, gate1 = columns_of(gates_ref)
    mixture = gate0 * dot_nn(pick0, returned) + gate1 * dot_nn(pick1, returned)
    layer_ref[...] = (middle_ref[...] + mixture).astype(BF)
    for copy in small:
        copy.wait_recv()
    sm_a[...] = sm[...] + sm_tp[0] + sm_tp[1] + sm_tp[2]
    for off in range(1, ep_count):
        small_copy(2 + off, sm_a, sm_ep.at[off - 1], {"ep": (ep + off) % ep_count})
    for batch in range(4):
        proj_sum(batch)
    run(1)
    for copy in small[3:]:
        copy.wait_recv()
    total = sm_a[...]
    for off in range(1, ep_count):
        total = total + sm_ep[off - 1]
    sm_b[...] = total
    for off in range(1, 4):
        small_copy(1 + ep_count + off, sm_b, sm_dp.at[off - 1], {"dp": (dp + off) % 4})
    run(2)
    for copy in small[2 + ep_count :]:
        copy.wait_recv()
    small_out[...] = sm_b[...] + sm_dp[0] + sm_dp[1] + sm_dp[2]
    run(max(n + 12, n + proj_n + 8) - clock[0], proj=True)

    def y_finish(index, _):
        for half in (0, 1):
            chunk = 2 * index + half
            for off in range(1, ep_count):
                source = (ep + ep_count - off) % ep_count
                y_gather(half, index, off).wait_send()
                remote(
                    pfin.at[source, chunk], pfin.at[source, chunk],
                    g_send.at[off - 1, half, index], g_recv.at[off - 1, half, index], {"ep": source},
                ).wait_recv()
        proj_chain.drain(index)
        return 0

    lax.fori_loop(0, proj_n, y_finish, 0)
    for batch in range(4):
        for off in range(1, ep_count):
            y_scatter(batch, off).wait_send()
    for copy in sends + small + [core_copy(0), core_copy(1), cross]:
        copy.wait_send()

    def drain(index, _):
        expert_chain.drain(index)
        for half in (0, 1):
            for hop in (1, 2, 3):
                x_copy(half, index, hop).wait_send()
            out_copy_of(half, index).wait()
        return 0

    lax.fori_loop(0, n, drain, 0)


def back(tokens, segment, key_mask, routes, gates, cot, g1, wq, wk, wv, wo, g2, kept, tin, tout):
    ep_count = lax.axis_size("ep")
    assert lax.axis_size("dp") == 4 and lax.axis_size("tp") == 4
    rows, width = tokens.shape
    group_rows = segment.shape[1]
    cols = wq.shape[0]
    quarter = tin.shape[1] // 4
    assert quarter == width and 4 * cols == width
    gx = kept[-2]
    gathered = 4 * gx.shape[1] * gx.shape[2]
    n = width // CHUNK
    proj = 12
    chunk = width // (proj * ep_count)
    dma = pltpu.SemaphoreType.DMA
    vmem = pl.BlockSpec(memory_space=pltpu.VMEM)
    hbm = pl.BlockSpec(memory_space=pl.ANY)
    struct = jax.ShapeDtypeStruct
    block = kept[5].shape
    others = ep_count - 1
    small = (8, width)
    proj_half = (2, proj // 2, chunk, width)
    pg_shape = (4, ep_count, cols // ep_count, width)
    y_shape = (4, others, cols // ep_count, width)
    many = 3 + others + 3
    return pl.pallas_call(
        functools.partial(back_kernel, ep_count, cols // HD, n),
        out_shape=(
            struct((2, n, 4, CHUNK, width), BF),
            struct((ep_count, proj, chunk, width), BF),
            struct(small, F32), struct((rows, width), F32), struct((rows, width), BF),
        ),
        in_specs=[vmem] * (12 + len(kept)) + [hbm] * 2,
        out_specs=(hbm, vmem, vmem, vmem, vmem),
        scratch_shapes=[
            pltpu.VMEM((width, quarter), BF), pltpu.VMEM((quarter, width), BF),
            pltpu.VMEM((gathered, quarter), BF), pltpu.VMEM((gathered, quarter), BF),
            pltpu.VMEM((2, width, width), F32),
            pltpu.VMEM((2, n, CHUNK, width), BF), pltpu.VMEM((2, n, CHUNK, width), BF),
            pltpu.VMEM((2, n, CHUNK, width), BF), pltpu.VMEM((2, n, 4, CHUNK, width), BF),
            pltpu.VMEM((proj, chunk, width), F32),
            pltpu.VMEM(proj_half, BF), pltpu.VMEM(proj_half, BF), pltpu.VMEM(proj_half, BF),
            pltpu.VMEM(pg_shape, BF), pltpu.VMEM(y_shape, BF),
            pltpu.VMEM(block, BF), pltpu.VMEM(block, BF),
            pltpu.VMEM((4, rows, width), BF),
            pltpu.VMEM((group_rows, cols), BF), pltpu.VMEM((group_rows, 3 * cols), BF),
            pltpu.VMEM((3 * cols, width), BF), pltpu.VMEM((group_rows, group_rows), F32),
            pltpu.VMEM((2, rows, width), BF), pltpu.VMEM((2, rows, width), BF),
            pltpu.VMEM((rows, width), BF), pltpu.VMEM((rows, width), BF),
            pltpu.VMEM(small, F32), pltpu.VMEM((3,) + small, F32), pltpu.VMEM((others,) + small, F32),
            pltpu.VMEM((3,) + small, F32), pltpu.VMEM(small, F32), pltpu.VMEM(small, F32),
            dma((2,)),
            dma((2, n)), dma((2, n)), dma((2, n)), dma((2, 2, n)), dma((2, n)),
            dma((3, 2, n)), dma((3, 2, n)), dma((2, n)),
            dma((2, proj // 2)), dma((2, proj // 2)), dma((2, proj // 2)), dma((2, 2, proj // 2)), dma((2, proj // 2)),
            dma((4, others)), dma((4, others)), dma((others, 2, proj // 2)), dma((others, 2, proj // 2)),
            dma((2, others)), dma((2, others)), dma((3,)), dma((3,)), dma((2,)), dma((2,)), dma(()), dma(()),
            dma((many,)), dma((many,)),
        ],
        compiler_params=pltpu.CompilerParams(
            collective_id=0, has_side_effects=True, vmem_limit_bytes=62 * 1024 * 1024
        ),
        name="back",
    )(tokens, segment, key_mask, routes, gates, cot, g1, wq, wk, wv, wo, g2, *kept, tin, tout)


def finish_kernel(
    tp_ref, rg_ref, pfin_ref, small_ref, grad_ref, layer_ref,
    gin_ref, gout_ref, o_ref, v_ref, q_ref, k_ref, tokens_ref, result_ref, a_ref, b_ref, c_ref, d_ref, count_ref,
):
    width = gin_ref.shape[0]
    gin_ref[...] = rg_ref[0, :, 0].reshape(width, -1).astype(F32)
    gout_ref[...] = rg_ref[1, :, 0].reshape(-1, width).astype(F32)

    @pl.when(pl.program_id(0) == 0)
    def _():
        owners = pfin_ref.shape[0]
        span = q_ref.shape[0] // owners
        for index, ref in enumerate((o_ref, v_ref, q_ref, k_ref)):
            for owner in range(owners):
                value = pfin_ref[owner, 3 * index : 3 * index + 3].reshape(span, width)
                ref[owner * span : (owner + 1) * span, :] = value.astype(F32)
        tokens_ref[...] = grad_ref[...]
        result_ref[...] = layer_ref[...]
        for index, ref in enumerate((a_ref, b_ref, c_ref, d_ref)):
            ref[...] = small_ref[index : index + 1, :]
        count_ref[...] = small_ref[4:5, 0:128].astype(jnp.int32)


def finish(rg, pfin, small, grad, layer, cols):
    _, n, _, chunk, width = rg.shape
    hidden = 4 * width
    me = lax.axis_index("tp").astype(jnp.int32).reshape(1)
    struct = jax.ShapeDtypeStruct

    def where(quarter, me_ref):
        mine = me_ref[0]
        low = (quarter % 2) != (mine % 2)
        high = (quarter // 2) != (mine // 2)
        return jnp.where(low, 1, 0) + jnp.where(high, 2, 0)

    def whole(shape):
        return pl.BlockSpec(shape, lambda q, t: (0,) * len(shape))

    outs = [struct((cols, width), F32)] * 4 + [struct(grad.shape, F32), struct(layer.shape, BF)]
    outs += [struct((1, width), F32)] * 4 + [struct((1, 128), jnp.int32)]
    return pl.pallas_call(
        finish_kernel,
        grid_spec=pltpu.PrefetchScalarGridSpec(
            num_scalar_prefetch=1,
            grid=(4,),
            in_specs=[
                pl.BlockSpec((2, n, 1, chunk, width), lambda q, t: (0, 0, where(q, t), 0, 0)),
                whole(pfin.shape), whole(small.shape), whole(grad.shape), whole(layer.shape),
            ],
            out_specs=[
                pl.BlockSpec((width, width), lambda q, t: (0, q)),
                pl.BlockSpec((width, width), lambda q, t: (q, 0)),
            ] + [whole(out.shape) for out in outs],
        ),
        out_shape=[struct((width, hidden), F32), struct((hidden, width), F32)] + outs,
        name="finish",
    )(me, rg, pfin, small, grad, layer)


def local(
    tokens,
    segment,
    key_mask,
    routes,
    gates,
    ln1_gain,
    ln1_bias,
    query_weight,
    key_weight,
    value_weight,
    out_weight,
    ln2_gain,
    ln2_bias,
    frozen_in,
    frozen_out,
    train_in,
    train_out,
    cotangent,
):
    vectors = (ln1_gain, ln1_bias, ln2_gain, ln2_bias)
    flat = (query_weight.T, key_weight.T, value_weight.T, out_weight)
    cols, width = out_weight.shape
    token_args = (tokens[0], segment, key_mask, routes[0].T, gates[0].T, cotangent[0])
    kept = front(
        *token_args, *vectors[:2], *flat, *vectors[2:], frozen_in[0], frozen_out[0], train_in[0], train_out[0]
    )
    rg, pfin, small, grad, layer = back(*token_args, ln1_gain, *flat, ln2_gain, kept, train_in[0], train_out[0])
    grad_in, grad_out, out, value, query, key, grad, layer, *sums, counts = finish(
        rg, pfin, small, grad, layer, cols
    )
    gain_one, bias_one, gain_two, bias_two = (row.reshape(width) for row in sums)
    experts = EXP_DEV * lax.axis_size("ep")
    return (
        layer[None], grad[None], gain_one, bias_one, query.T, key.T, value.T, out, gain_two, bias_two,
        grad_in[None], grad_out[None], counts[0, :experts],
    )


def solution(mesh):
    in_specs = (
        P(("ep", "dp"), "tp", None),
        P(("ep", "dp"), None),
        P(("ep", "dp"), None),
        P(("ep", "dp"), "tp", None),
        P(("ep", "dp"), "tp", None),
        P(),
        P(),
        P(None, "tp"),
        P(None, "tp"),
        P(None, "tp"),
        P("tp", None),
        P(),
        P(),
        P("ep", None, None),
        P("ep", None, None),
        P("ep", None, None),
        P("ep", None, None),
        P(("ep", "dp"), "tp", None),
    )
    out_specs = (
        P(("ep", "dp"), "tp", None),
        P(("ep", "dp"), "tp", None),
        P(),
        P(),
        P(None, "tp"),
        P(None, "tp"),
        P(None, "tp"),
        P("tp", None),
        P(),
        P(),
        P("ep", None, None),
        P("ep", None, None),
        P(),
    )
    return jax.shard_map(local, mesh=mesh, in_specs=in_specs, out_specs=out_specs, check_vma=False)
```

time: 292 us -> 190 us (0.65)
  local copies, waits for them, and re-layouts: 26.5 us -> 1.17 us
  waiting for transfers between devices: 21.3 us -> 0 us
  between operations: 14.5 us -> 0.68 us
  matrix products: 9.89 us -> 0 us
  Pallas kernels: 192 us -> 183 us
  blocking collectives: 8.8 us -> 0 us
  starting transfers between devices: 7.91 us -> 0 us
  other arithmetic: 9.33 us -> 5.15 us
    reduce_scatter x1 -> x0, waiting for transfers between devices: 16.2 us -> none  [local(): lax.psum_scatter(contract(projected_grad, joined, 1, 1).astype(jnp.bfloat...]
    unnamed x48 -> x0, local copies, waits for them, and re-layouts: 15 us -> none
    dot_general x13 -> x0, matrix products: 9.89 us -> none  [the longest x8 6.54 us: contract(): lax.dot_general(left, right, (((left_dim,), (right_dim,)), ((), ())), pre...]
    pallas_call x1, Pallas kernels: 124 us -> 114 us  [back(): pl.pallas_call(functools.partial(back_kernel, ep_count, cols // HD, n), o...]
    all_gather x1 -> x0, blocking collectives: 8.8 us -> none  [local(): piece = lax.all_gather(attn_grad, 'tp', axis=0, tiled=True)]
    all_to_all x2 -> x0, starting transfers between devices: 7.87 us -> none  [to_sources(): return lax.all_to_all(buffer, 'ep', split_axis=0, concat_axis=0, tiled=True)]
    reshape x9 -> x0, local copies, waits for them, and re-layouts: 5.22 us -> none  [the longest x4 5.07 us: local(): line = lambda vector: vector.reshape(1, width)]
    pallas_call x0 -> x4, other arithmetic: none -> 5.15 us  [finish(): pl.pallas_call(finish_kernel, grid_spec=pltpu.PrefetchScalarGridSpec(num_...]
  transfers between devices with their start and end apart: 3 -> 0, of which waited for: 2 -> 0; matrix products, arithmetic and copies ran while one was open for 7% -> 0% of each run, Pallas kernels for 0% -> 0%
where the time goes in v3:
time: 190 us
  Pallas kernels  183 us (96%)
  other arithmetic  5.15 us (3%)
    pallas_call x1, Pallas kernels, back(): pl.pallas_call(functools.partial(back_kernel, ep_count, cols // HD, n), o...  114 us
    pallas_call x1, Pallas kernels, front(): pl.pallas_call(functools.partial(front_kernel, ep_count, cols // HD), out...  56.2 us
    pallas_call x1, Pallas kernels, finish(): pl.pallas_call(finish_kernel, grid_spec=pltpu.PrefetchScalarGridSpec(num_...  12.2 us
    pallas_call x4, other arithmetic, finish(): pl.pallas_call(finish_kernel, grid_spec=pltpu.PrefetchScalarGridSpec(num_...  5.15 us

profile of v3, /device:TPU:0, one launch (start us, length us, event | category | flops | bytes accessed | tf_op | source)
XLA Modules:
  0.0 189.8 jit_solution(14372537668469066761)
XLA Ops:
  0.6 56.2 %front.1 = (bf16[4,128,768]{2,1,0:T(8,128)(2,1)}, bf16[512,576]{1,0:T(8,128)(2,1)}, bf16[512,192]{1,0:T(8,128)(2,1)}, f32[512,8]{1,0:T(8,128)}, f32[128,768]{1,0...) custom-call(bf16[128,768]{1,0:T(8,128)(2,1)} %bitcast.37, ...), custom_call_target="tpu_custom_call" | custom-call | tf_op jit(solution)/shard_map/front/pallas_call | solution.py:336
  56.9 114.4 %back.1 = (bf16[2,24,4,32,768]{4,3,2,1,0:T(8,128)(2,1)}, bf16[2,12,32,768]{3,2,1,0:T(8,128)(2,1)}, f32[8,768]{1,0:T(8,128)}, f32[128,768]{1,0:T(8,128)}, bf16[128,768]{1,0:T(8,128)(2,1)}) custom-call(bf16[128,768]{1,0:T(8,128)(2,1)} %bitcast.38, s32[1,512]{1,0:T(1,128)} %seg_ref.3, s32[1,512]{1,0:T(1,128)} %key_ref.3, s32[2,128]{1,0:T(2,128)} %bitcast.42, ...), custom_call_target="tpu_custom_call" | custom-call | tf_op jit(solution)/shard_map/back/pallas_call | solution.py:826
  171.3 12.2 %finish.1 = (f32[768,3072]{1,0:T(8,128)}, f32[3072,768]{1,0:T(8,128)}, f32[192,768]{1,0:T(8,128)}, f32[192,768]{1,0:T(8,128)}, f32[192,768]{1,0:T(8,128)}, /*ind...) custom-call(s32[1]{0:T(128)} %bitcast.tp_ref, ...), custom_call_target="tpu_custom_call" | custom-call | tf_op jit(solution)/shard_map/finish/pallas_call | solution.py:907
  183.5 1.2 slice_bitcast_fusion
  184.6 1.3 reduce
  185.9 1.3 reduce.1
  187.2 1.3 reduce.2
  188.5 1.3 reduce.3

commit v4 on v3

v4 whole, which is shorter than its diff:
```python
import functools
import math

import jax
import jax.numpy as jnp
from jax import lax
from jax.experimental import pallas as pl
from jax.experimental.pallas import tpu as pltpu
from jax.sharding import PartitionSpec as P

HD = 64
EXP_DEV = 2
EPSILON = 1e-05
MASKED = -1e30
MESH = pl.DeviceIdType.MESH
BF = jnp.bfloat16
F32 = jnp.float32
CHUNK = 32


def tp_peers():
    me = lax.axis_index("tp")
    one = me + 1 - 2 * (me % 2)
    return (me, one, (me + 2) % 4, (one + 2) % 4)


def remote(src, dst, send, recv, where):
    return pltpu.make_async_remote_copy(
        src_ref=src, dst_ref=dst, send_sem=send, recv_sem=recv,
        device_id=where, device_id_type=MESH,
    )


def entry_barrier(ep_count, dp_count):
    barrier = pltpu.get_barrier_semaphore()
    _, tp1, tp2, tp3 = tp_peers()
    ep, dp = lax.axis_index("ep"), lax.axis_index("dp")
    for peer in (tp1, tp2, tp3):
        pl.semaphore_signal(barrier, inc=1, device_id={"tp": peer}, device_id_type=MESH)
    for off in range(1, ep_count):
        pl.semaphore_signal(
            barrier, inc=1, device_id={"ep": (ep + off) % ep_count}, device_id_type=MESH
        )
    for off in range(1, dp_count):
        pl.semaphore_signal(
            barrier, inc=1, device_id={"dp": (dp + off) % dp_count}, device_id_type=MESH
        )
    pl.semaphore_wait(barrier, 3 + ep_count - 1 + dp_count - 1)


def gelu_pair(hidden):
    phi = 0.5 * (1.0 + lax.erf(hidden * math.sqrt(0.5)))
    dens = jnp.exp(-0.5 * hidden * hidden) * (1.0 / math.sqrt(2.0 * math.pi))
    return hidden * phi, phi + hidden * dens


def row_of(ref):
    return ref[...].reshape(1, -1)


def columns_of(ref):
    value = ref[...].astype(F32)
    padded = jnp.concatenate([value, jnp.zeros((6, value.shape[1]), F32)], axis=0)
    flipped = padded.T
    return flipped[:, 0:1], flipped[:, 1:2]


def fill_bias(seg_ref, key_ref, bias):
    segment = seg_ref[...]
    group_rows = segment.shape[1]
    lane = lax.broadcasted_iota(jnp.int32, segment.shape, 1)
    starts = (segment != pltpu.roll(segment, 1, 1)) | (lane == 0)
    keep = (key_ref[...] == 1) | starts
    segment = segment.astype(F32)
    column = jnp.broadcast_to(segment, (8, group_rows)).T[:, 0:1]
    kept = jnp.where(keep, segment, -1.0)
    bias[...] = jnp.where(column == kept, 0.0, MASKED)


def ln_rows(values, gain, bias):
    center = jnp.mean(values, axis=-1, keepdims=True)
    shifted = values - center
    spread = jnp.mean(shifted * shifted, axis=-1, keepdims=True)
    return shifted * lax.rsqrt(spread + EPSILON) * gain + bias


def route_picks(routes_ref, capacity, slots):
    first, second = (column.astype(jnp.int32) for column in columns_of(routes_ref))
    rows = first.shape[0]
    lane = lax.broadcasted_iota(jnp.int32, (rows, 128), 1)
    marks = jnp.where((lane == first) | (lane == second), 1.0, 0.0)
    row_id = lax.broadcasted_iota(jnp.int32, (rows, rows), 0)
    col_id = lax.broadcasted_iota(jnp.int32, (rows, rows), 1)
    lower = jnp.where(row_id > col_id, 1.0, 0.0).astype(BF)
    before = jnp.dot(lower, marks.astype(BF), preferred_element_type=F32)
    slot = lax.broadcasted_iota(jnp.int32, (rows, slots), 1)
    picks = []
    for route in (first, second):
        place = jnp.sum(jnp.where(lane == route, before, 0.0), axis=1, keepdims=True)
        chosen = route * capacity + place.astype(jnp.int32)
        picks.append(jnp.where(slot == chosen, 1.0, 0.0).astype(BF))
    return picks[0], picks[1], marks


def dot_tn(left, right):
    return lax.dot_general(left, right, (((0,), (0,)), ((), ())), preferred_element_type=F32)


def dot_nt(left, right):
    return lax.dot_general(left, right, (((1,), (1,)), ((), ())), preferred_element_type=F32)


def dot_nn(left, right):
    return jnp.dot(left, right, preferred_element_type=F32)


def ln_backward(values, gain, upstream):
    center = jnp.mean(values, axis=-1, keepdims=True)
    shifted = values - center
    spread = jnp.mean(shifted * shifted, axis=-1, keepdims=True)
    scale = lax.rsqrt(spread + EPSILON)
    unit = shifted * scale
    inner = upstream * gain
    along = jnp.mean(inner * unit, axis=-1, keepdims=True)
    grad = scale * (inner - jnp.mean(inner, axis=-1, keepdims=True) - unit * along)
    return grad, jnp.sum(upstream * unit, axis=0, keepdims=True), jnp.sum(upstream, axis=0, keepdims=True)


class Chain:
    def __init__(self, base, count, own, stage, final, sems, hooks):
        self.base, self.count, self.own, self.stage = base, count, own, stage
        self.final, self.hooks = final, hooks
        self.red_send, self.recv_a, self.recv_b, self.bc_send, self.bc_recv = sems
        self.dp = lax.axis_index("dp")

    def place(self, half):
        return 3 - self.dp if half == 0 else self.dp

    def peers(self, half):
        down, up = (self.dp + 3) % 4, (self.dp + 1) % 4
        return (down, up) if half == 0 else (up, down)

    def red(self, half, index, near):
        toward, away = self.peers(half)
        landing = self.stage.at[half, index]
        target, sem = (self.final(half, index), self.recv_b) if near else (landing, self.recv_a)
        return remote(
            landing, target, self.red_send.at[half, index], sem.at[half, index],
            {"dp": away if near else toward},
        )

    def spread(self, half, index, near):
        toward, away = self.peers(half)
        ref = self.final(half, index)
        return remote(
            ref, ref, self.bc_send.at[1 if near else 0, half, index], self.bc_recv.at[half, index],
            {"dp": toward if near else away},
        )

    def step(self, s):
        for half in (0, 1):
            place = self.place(half)
            index = s - self.base - (2 * place - 4 * (place // 3))

            @pl.when((index >= 0) & (index < self.count))
            def _():
                own = self.own(half, index)

                @pl.when(place == 0)
                def _():
                    self.stage[half, index] = own.astype(BF)
                    self.red(half, index, False).start()

                @pl.when(place == 3)
                def _():
                    self.stage[half, index] = own.astype(BF)
                    self.red(half, index, True).start()

                @pl.when(place == 1)
                def _():
                    self.red(half, index, False).wait_recv()
                    self.stage[half, index] = (own + self.stage[half, index].astype(F32)).astype(BF)
                    self.red(half, index, False).start()

                @pl.when(place == 2)
                def _():
                    self.red(half, index, False).wait_recv()
                    self.red(half, index, True).wait_recv()
                    total = own + self.stage[half, index].astype(F32) + self.final(half, index)[...].astype(F32)
                    self.final(half, index)[...] = total.astype(BF)

        for half in (0, 1):
            place = self.place(half)
            index = s - self.base - (8 - 2 * place + 4 * (place // 3))

            @pl.when((index >= 0) & (index < self.count))
            def _():
                @pl.when(place == 2)
                def _():
                    self.spread(half, index, False).start()
                    self.spread(half, index, True).start()

                @pl.when(place != 2)
                def _():
                    self.spread(half, index, False).wait_recv()

                @pl.when(place == 1)
                def _():
                    self.spread(half, index, False).start()

                self.hooks[0](half, index)

            for later, hook in enumerate(self.hooks[1:]):
                after = index - 2 * (later + 1)
                pl.when((after >= 0) & (after < self.count))(functools.partial(hook, half, after))

    def drain(self, index):
        for half in (0, 1):
            place = self.place(half)

            @pl.when(place != 2)
            def _():
                self.red(half, index, False).wait_send()

            @pl.when((place == 1) | (place == 2))
            def _():
                self.spread(half, index, False).wait_send()

            @pl.when(place == 2)
            def _():
                self.spread(half, index, True).wait_send()


def layer_kernel(
    ep_count, heads, n,
    tok_ref, seg_ref, key_ref, routes_ref, gates_ref, cot_ref, g1_ref, b1_ref, wq_ref, wk_ref, wv_ref, wo_ref,
    g2_ref, b2_ref, fin_hbm, fout_hbm, tin_hbm, tout_hbm,
    rg_hbm, pfin, small_out, grad_ref, layer_ref,
    weights, group_ref, qkv_ref, heads_ref, lse_ref, middle_ref, gx, gs, picks, joined, bias,
    part, core_slot, mix, x_slot, sx, ss, ax, as_, out_acc, back_acc, out_ref, back_ref,
    act, slope, own, stage, fin, acc, pstage, pgbuf, yslot, ret_back, ret_out,
    piece, up_heads, pgrad, bpart, bcore_slot, bmix, bx_slot,
    sm, sm_tp, sm_ep, sm_dp, sm_a, sm_b,
    w_sem, a_send, a_recv, c_send, c_recv, m_send, m_recv, e_send, e_recv, t_send, t_recv,
    red_send, recv_a, recv_b, bc_send, bc_recv, x_send, x_recv, out_sem,
    pred_send, precv_a, precv_b, pbc_send, pbc_recv, y_send, y_recv, g_send, g_recv,
    b_send, b_recv, s_send, s_recv,
):
    tp, tp1, tp2, tp3 = tp_peers()
    ep, dp = lax.axis_index("ep"), lax.axis_index("dp")
    rows, width = tok_ref.shape
    cols = wq_ref.shape[0]
    group_rows = seg_ref.shape[1]
    pieces = weights.shape[0]
    capacity = sx.shape[2]
    slots = ep_count * EXP_DEV * capacity
    tokens = ep_count * capacity
    frozen, train = 0, 1
    offsets = range(1, ep_count)

    def weight_loads(expert, index):
        source_in, source_out = ((fin_hbm, fout_hbm), (tin_hbm, tout_hbm))[expert]
        at = pl.ds(pl.multiple_of(index * width, width), width)
        return [
            pltpu.make_async_copy(source_in.at[:, at], weights.at[index, 0], w_sem.at[expert, 0, index]),
            pltpu.make_async_copy(source_out.at[at, :], weights.at[index, 1], w_sem.at[expert, 1, index]),
        ]

    residual = tok_ref[...].astype(F32)
    group_ref[tp] = ln_rows(residual, row_of(g1_ref), row_of(b1_ref)).astype(BF)
    entry_barrier(ep_count, 4)
    sends = []

    def send(copy):
        sends.append(copy)
        copy.start()

    def gather_copy(stage_of, buf, slot, index, peer):
        return remote(
            buf.at[slot], buf.at[slot], a_send.at[stage_of, index], a_recv.at[stage_of, index], {"tp": peer}
        )

    send(gather_copy(0, group_ref, tp, 1, tp2))
    send(gather_copy(0, group_ref, tp, 0, tp1))
    for index in range(pieces):
        for copy in weight_loads(train, index):
            copy.start()

    pick0, pick1, marks = route_picks(routes_ref, capacity, slots)
    picks[0] = pick0
    picks[1] = pick1
    sm[...] = jnp.zeros_like(sm)
    sm[4:5, 0:128] = jnp.sum(marks, axis=0, keepdims=True)
    upstream = cot_ref[...].astype(F32)
    gate0, gate1 = columns_of(gates_ref)
    share0 = (gate0 * upstream).astype(BF)
    share1 = (gate1 * upstream).astype(BF)
    ss[...] = (dot_tn(pick0, share0) + dot_tn(pick1, share1)).astype(BF).reshape(ss.shape)

    def landing(kind, expert, source):
        if expert == train:
            return (gx, gs)[kind].at[0, source]
        return (ax, as_)[kind].at[source]

    def owner_copy(kind, expert, off):
        peer = (ep + off) % ep_count
        return remote(
            (sx, ss)[kind].at[peer, expert], landing(kind, expert, ep),
            e_send.at[kind, expert, off - 1], e_recv.at[kind, expert, off - 1], {"ep": peer},
        )

    def owner_wait(kind, expert, off):
        source = (ep + ep_count - off) % ep_count
        target = landing(kind, expert, source)
        remote(
            target, target, e_send.at[kind, expert, off - 1], e_recv.at[kind, expert, off - 1], {"ep": source}
        ).wait_recv()

    def token_copy(kind, rel, hop):
        buf = (gx, gs)[kind]
        origin = (ep + ep_count - rel) % ep_count
        source, peer = ((0, tp1), (0, tp2), (2, tp1))[hop - 1]
        return remote(
            buf.at[source, origin], buf.at[hop, origin],
            t_send.at[kind, rel, hop - 1], t_recv.at[kind, rel, hop - 1], {"tp": peer},
        )

    def dispatch(kind, source):
        for off in offsets:
            send(owner_copy(kind, train, off))
        (gx, gs)[kind][0, ep] = source[ep, train]
        send(token_copy(kind, 0, 2))
        send(token_copy(kind, 0, 1))
        for off in offsets:
            send(owner_copy(kind, frozen, off))
        (ax, as_)[kind][ep] = source[ep, frozen]

    def pass_on(kind):
        for off in offsets:
            owner_wait(kind, train, off)
            send(token_copy(kind, off, 2))
            send(token_copy(kind, off, 1))

    def forward(kind, rel):
        token_copy(kind, rel, 2).wait_recv()
        send(token_copy(kind, rel, 3))

    dispatch(1, ss)
    for index, ref in enumerate((wq_ref, wk_ref, wv_ref)):
        joined[index * cols : (index + 1) * cols, :] = ref[...]
    fill_bias(seg_ref, key_ref, bias)

    def project(slot):
        at = pl.ds(pl.multiple_of(slot * rows, rows), rows)
        qkv_ref[at, :] = dot_nt(group_ref[slot], joined[...]).astype(BF)

    project(tp)
    gather_copy(0, group_ref, tp1, 0, tp1).wait_recv()
    project(tp1)
    gather_copy(0, group_ref, tp2, 1, tp2).wait_recv()
    send(gather_copy(0, group_ref, tp2, 2, tp1))
    project(tp2)
    pass_on(1)
    gather_copy(0, group_ref, tp3, 2, tp1).wait_recv()
    project(tp3)

    scale = HD ** (-0.5)
    block = min(256, group_rows)
    for head in range(heads):
        low, high = head * HD, (head + 1) * HD
        for index in range(group_rows // block):
            at = slice(index * block, (index + 1) * block)
            query = qkv_ref[at, low:high]
            keys = qkv_ref[:, cols + low : cols + high]
            values = qkv_ref[:, 2 * cols + low : 2 * cols + high]
            scores = dot_nt(query, keys) * scale + bias[at, :]
            highest = jnp.max(scores, axis=-1, keepdims=True)
            weight = jnp.exp(scores - highest)
            total = jnp.sum(weight, axis=-1, keepdims=True)
            probs = (weight * (1.0 / total)).astype(BF)
            heads_ref[at, low:high] = dot_nn(probs, values).astype(BF)
            lse_ref[at, head : head + 1] = highest + jnp.log(total)

    def partial(slot):
        at = pl.ds(pl.multiple_of(slot * rows, rows), rows)
        return dot_nn(heads_ref[at, :], wo_ref[...])

    def core_copy(index):
        return remote(part.at[index], core_slot.at[index], c_send.at[0, index], c_recv.at[0, index], {"tp": tp1})

    part[0] = partial(tp3)
    send(core_copy(0))
    part[1] = partial(tp1)
    send(core_copy(1))
    crossing = partial(tp2)
    mine = tok_ref[...].astype(F32) + partial(tp)
    core_copy(0).wait_recv()
    mix[...] = (crossing + core_slot[0]).astype(BF)
    cross = remote(mix, x_slot, m_send.at[0], m_recv.at[0], {"tp": tp2})
    send(cross)
    forward(1, 0)
    core_copy(1).wait_recv()
    mine = mine + core_slot[1]
    cross.wait_recv()
    middle = mine + x_slot[...].astype(F32)
    middle_ref[...] = middle
    normed = ln_rows(middle, row_of(g2_ref), row_of(b2_ref)).astype(BF)
    sx[...] = dot_tn(picks[0] + picks[1], normed).astype(BF).reshape(sx.shape)
    dispatch(0, sx)
    for off in offsets:
        forward(1, off)
    pass_on(0)

    def expert_piece(index, inputs, shares):
        before = dot_nn(inputs, weights[index, 0])
        through = dot_nt(shares, weights[index, 1])
        value, grad = gelu_pair(before)
        slopes = (through * grad).astype(BF)
        produced = dot_nn(value.astype(BF), weights[index, 1])
        returned = dot_nt(slopes, weights[index, 0])

        @pl.when(index == 0)
        def _():
            out_acc[...] = produced
            back_acc[...] = returned

        @pl.when(index > 0)
        def _():
            out_acc[...] += produced
            back_acc[...] += returned

    def return_copy(kind, expert, off):
        peer = (ep + off) % ep_count
        source, target = ((back_ref, ret_back), (out_ref, ret_out))[kind]
        return remote(
            source.at[peer, expert], target.at[ep, expert],
            b_send.at[kind, expert, off - 1], b_recv.at[kind, expert, off - 1], {"ep": peer},
        )

    def return_wait(kind):
        target = (ret_back, ret_out)[kind]
        for expert in range(EXP_DEV):
            for off in offsets:
                source = (ep + ep_count - off) % ep_count
                remote(
                    target.at[source, expert], target.at[source, expert],
                    b_send.at[kind, expert, off - 1], b_recv.at[kind, expert, off - 1], {"ep": source},
                ).wait_recv()

    def give_back(expert):
        back_ref[:, expert] = back_acc[...].astype(BF).reshape(ep_count, capacity, width)
        out_ref[:, expert] = out_acc[...].astype(BF).reshape(ep_count, capacity, width)
        for kind in (0, 1):
            for off in offsets:
                send(return_copy(kind, expert, off))
        ret_back[ep, expert] = back_ref[ep, expert]
        ret_out[ep, expert] = out_ref[ep, expert]

    def train_piece(index, _):
        for copy in weight_loads(train, index):
            copy.wait()
        expert_piece(index, gx[0].reshape(tokens, width), gs[0].reshape(tokens, width))

        @pl.when(index == 1)
        def _():
            token_copy(0, 0, 2).wait_recv()
            token_copy(0, 0, 3).start()

        return 0

    lax.fori_loop(0, pieces, train_piece, 0)
    sends.append(token_copy(0, 0, 3))
    give_back(train)
    for off in offsets:
        forward(0, off)

    def hidden_block(index, _):
        for hop, when in ((1, 1), (3, 3)):
            @pl.when(index == when)
            def _(hop=hop):
                for kind in (0, 1):
                    for rel in range(ep_count):
                        token_copy(kind, rel, hop).wait_recv()

        before = dot_nn(gx[index].reshape(tokens, width), weights[tp, 0])
        through = dot_nt(gs[index].reshape(tokens, width), weights[tp, 1])
        value, grad = gelu_pair(before)
        at = pl.ds(pl.multiple_of(index * tokens, tokens), tokens)
        act[at, :] = value.astype(BF)
        slope[at, :] = (through * grad).astype(BF)
        return 0

    lax.fori_loop(0, 4, hidden_block, 0)
    for index in range(pieces):
        for copy in weight_loads(frozen, index):
            copy.start()

    def x_copy(half, index, hop):
        source, peer = ((0, tp1), (0, tp2), (2, tp1))[hop - 1]
        return remote(
            fin.at[half, index, source], fin.at[half, index, hop],
            x_send.at[hop - 1, half, index], x_recv.at[hop - 1, half, index], {"tp": peer},
        )

    def out_copy_of(half, index):
        return pltpu.make_async_copy(fin.at[half, index], rg_hbm.at[half, index], out_sem.at[half, index])

    def cross_first(half, index):
        x_copy(half, index, 2).start()
        x_copy(half, index, 1).start()

    def cross_second(half, index):
        x_copy(half, index, 2).wait_recv()
        x_copy(half, index, 3).start()

    def cross_third(half, index):
        x_copy(half, index, 1).wait_recv()
        x_copy(half, index, 3).wait_recv()
        out_copy_of(half, index).start()

    expert_chain = Chain(
        0, n, lambda half, index: own[half, pl.ds(pl.multiple_of(index * CHUNK, CHUNK), CHUNK), :],
        stage, lambda half, index: fin.at[half, index, 0],
        (red_send, recv_a, recv_b, bc_send, bc_recv), (cross_first, cross_second, cross_third),
    )
    span = 128

    def outer(index, _):
        at = pl.ds(pl.multiple_of(index * span, span), span)
        own[0, at, :] = dot_tn(gx[:, :, :, at].reshape(-1, span), slope[...])
        own[1, at, :] = dot_tn(act[:, at], gs[...].reshape(-1, width))
        expert_chain.step(index)
        return 0

    first_steps = width // span
    lax.fori_loop(0, first_steps, outer, 0)

    def frozen_piece(index, _):
        for copy in weight_loads(frozen, index):
            copy.wait()
        expert_piece(index, ax[...].reshape(tokens, width), as_[...].reshape(tokens, width))
        expert_chain.step(first_steps + index)
        return 0

    for kind in (0, 1):
        for off in offsets:
            owner_wait(kind, frozen, off)
    lax.fori_loop(0, pieces, frozen_piece, 0)
    give_back(frozen)
    clock = [first_steps + pieces]
    proj_chain = None

    def run(count):
        def body(s, _):
            expert_chain.step(s)
            if proj_chain is not None:
                proj_chain.step(s)
            return 0

        lax.fori_loop(clock[0], clock[0] + count, body, 0)
        clock[0] += count

    run(2)
    return_wait(0)
    second = dot_nn(picks[0] + picks[1], ret_back[...].reshape(slots, width))
    inner_grad, gain_two, bias_two = ln_backward(middle_ref[...], row_of(g2_ref), second)
    middle_grad = cot_ref[...].astype(F32) + inner_grad
    grad_ref[...] = middle_grad
    piece[tp] = middle_grad.astype(BF)
    send(gather_copy(1, piece, tp, 1, tp2))
    send(gather_copy(1, piece, tp, 0, tp1))
    sm[2:3, :] = gain_two
    sm[3:4, :] = bias_two
    run(1)

    def head_rows(slot):
        at = pl.ds(pl.multiple_of(slot * rows, rows), rows)
        up_heads[at, :] = dot_nt(piece[slot], wo_ref[...]).astype(BF)

    head_rows(tp)
    gather_copy(1, piece, tp1, 0, tp1).wait_recv()
    head_rows(tp1)
    gather_copy(1, piece, tp2, 1, tp2).wait_recv()
    send(gather_copy(1, piece, tp2, 2, tp1))
    head_rows(tp2)
    run(1)
    gather_copy(1, piece, tp3, 2, tp1).wait_recv()
    head_rows(tp3)

    def y_scatter(batch, off):
        peer = (ep + off) % ep_count
        return remote(
            pgbuf.at[batch, peer], yslot.at[batch, off - 1], y_send.at[batch, off - 1], y_recv.at[batch, off - 1],
            {"ep": peer},
        )

    def proj_start(batch, value):
        pgbuf[batch] = value.astype(BF).reshape(pgbuf.shape[1:])
        for off in offsets:
            send(y_scatter(batch, off))

    def proj_sum(batch):
        total = pgbuf[batch, ep].astype(F32)
        for off in offsets:
            y_scatter(batch, off).wait_recv()
            total = total + yslot[batch, off - 1].astype(F32)
        acc[3 * batch : 3 * batch + 3] = total.reshape((3,) + acc.shape[1:])

    proj_start(0, dot_tn(heads_ref[...], piece[...].reshape(group_rows, width)))
    run(1)
    for head in range(heads):
        low, high = head * HD, (head + 1) * HD
        key_sum = value_sum = None
        for index in range(group_rows // block):
            at = slice(index * block, (index + 1) * block)
            query = qkv_ref[at, low:high]
            keys = qkv_ref[:, cols + low : cols + high]
            values = qkv_ref[:, 2 * cols + low : 2 * cols + high]
            above = up_heads[at, low:high]
            scores = dot_nt(query, keys) * scale + bias[at, :]
            probs = jnp.exp(scores - lse_ref[at, head : head + 1])
            prob_grad = dot_nt(above, values)
            centered = jnp.sum(probs * prob_grad, axis=-1, keepdims=True)
            score_grad = (probs * (prob_grad - centered)).astype(BF)
            pgrad[at, low:high] = (dot_nn(score_grad, keys) * scale).astype(BF)
            key_part = dot_tn(score_grad, query)
            value_part = dot_tn(probs.astype(BF), above)
            key_sum = key_part if key_sum is None else key_sum + key_part
            value_sum = value_part if value_sum is None else value_sum + value_part
        pgrad[:, cols + low : cols + high] = (key_sum * scale).astype(BF)
        pgrad[:, 2 * cols + low : 2 * cols + high] = value_sum.astype(BF)
        run(1)

    def back_partial(slot):
        at = pl.ds(pl.multiple_of(slot * rows, rows), rows)
        return dot_nn(pgrad[at, :], joined[...])

    def back_core_copy(index):
        return remote(bpart.at[index], bcore_slot.at[index], c_send.at[1, index], c_recv.at[1, index], {"tp": tp1})

    bpart[0] = back_partial(tp3).astype(BF)
    send(back_core_copy(0))
    bpart[1] = back_partial(tp1).astype(BF)
    send(back_core_copy(1))
    crossing = back_partial(tp2)
    mine = back_partial(tp)
    back_core_copy(0).wait_recv()
    bmix[...] = (crossing + bcore_slot[0].astype(F32)).astype(BF)
    back_cross = remote(bmix, bx_slot, m_send.at[1], m_recv.at[1], {"tp": tp2})
    send(back_cross)
    normed = group_ref[...].reshape(group_rows, width)
    for batch, part_index in ((1, 2), (2, 0), (3, 1)):
        proj_start(batch, dot_tn(pgrad[:, part_index * cols : (part_index + 1) * cols], normed))
        run(1)
    back_core_copy(1).wait_recv()
    back_cross.wait_recv()
    first = mine + bcore_slot[1].astype(F32) + bx_slot[...].astype(F32)
    residual_part, gain_one, bias_one = ln_backward(tok_ref[...].astype(F32), row_of(g1_ref), first)
    grad_ref[...] += residual_part
    sm[0:1, :] = gain_one
    sm[1:2, :] = bias_one

    small = []

    def small_copy(slot, source, target, where):
        small.append(remote(source, target, s_send.at[slot], s_recv.at[slot], where))
        send(small[-1])

    for hop, peer in ((1, tp1), (2, tp2), (3, tp3)):
        small_copy(hop - 1, sm, sm_tp.at[hop - 1], {"tp": peer})
    for batch in range(4):
        proj_sum(batch)

    def y_gather(half, index, off):
        chunk = 2 * index + half
        return remote(
            pfin.at[ep, chunk], pfin.at[ep, chunk], g_send.at[off - 1, half, index], g_recv.at[off - 1, half, index],
            {"ep": (ep + off) % ep_count},
        )

    def y_first(half, index):
        for off in offsets:
            y_gather(half, index, off).start()

    proj_n = acc.shape[0] // 2
    proj_base = max(n, clock[0])
    proj_chain = Chain(
        proj_base, proj_n, lambda half, index: acc[2 * index + half], pstage,
        lambda half, index: pfin.at[ep, 2 * index + half],
        (pred_send, precv_a, precv_b, pbc_send, pbc_recv), (y_first,),
    )
    run(1)
    return_wait(1)
    returned = ret_out[...].reshape(slots, width)
    gate0, gate1 = columns_of(gates_ref)
    mixture = gate0 * dot_nn(picks[0], returned) + gate1 * dot_nn(picks[1], returned)
    layer_ref[...] = (middle_ref[...] + mixture).astype(BF)
    for copy in small:
        copy.wait_recv()
    sm_a[...] = sm[...] + sm_tp[0] + sm_tp[1] + sm_tp[2]
    for off in offsets:
        small_copy(2 + off, sm_a, sm_ep.at[off - 1], {"ep": (ep + off) % ep_count})
    run(2)
    for copy in small[3:]:
        copy.wait_recv()
    total = sm_a[...]
    for off in offsets:
        total = total + sm_ep[off - 1]
    sm_b[...] = total
    for off in range(1, 4):
        small_copy(1 + ep_count + off, sm_b, sm_dp.at[off - 1], {"dp": (dp + off) % 4})
    run(2)
    for copy in small[2 + ep_count :]:
        copy.wait_recv()
    small_out[...] = sm_b[...] + sm_dp[0] + sm_dp[1] + sm_dp[2]
    run(max(n + 12, proj_base + proj_n + 8) - clock[0])

    def y_finish(index, _):
        for half in (0, 1):
            chunk = 2 * index + half
            for off in offsets:
                source = (ep + ep_count - off) % ep_count
                y_gather(half, index, off).wait_send()
                remote(
                    pfin.at[source, chunk], pfin.at[source, chunk],
                    g_send.at[off - 1, half, index], g_recv.at[off - 1, half, index], {"ep": source},
                ).wait_recv()
        proj_chain.drain(index)
        return 0

    lax.fori_loop(0, proj_n, y_finish, 0)
    for copy in sends:
        copy.wait_send()

    def drain(index, _):
        expert_chain.drain(index)
        for half in (0, 1):
            for hop in (1, 2, 3):
                x_copy(half, index, hop).wait_send()
            out_copy_of(half, index).wait()
        return 0

    lax.fori_loop(0, n, drain, 0)


def layer_step(tokens, segment, key_mask, routes, gates, cot, g1, b1, wq, wk, wv, wo, g2, b2, fin, fout, tin, tout):
    ep_count = lax.axis_size("ep")
    assert lax.axis_size("dp") == 4 and lax.axis_size("tp") == 4
    rows, width = tokens.shape
    group_rows = segment.shape[1]
    cols = wq.shape[0]
    hidden = tin.shape[1]
    quarter = hidden // 4
    assert quarter == width and 4 * cols == width
    capacity = 4 * rows // (EXP_DEV * ep_count)
    gathered = 4 * ep_count * capacity
    n = width // CHUNK
    proj = 12
    chunk = width // (proj * ep_count)
    dma = pltpu.SemaphoreType.DMA
    vmem = pl.BlockSpec(memory_space=pltpu.VMEM)
    hbm = pl.BlockSpec(memory_space=pl.ANY)
    struct = jax.ShapeDtypeStruct
    block = (ep_count, EXP_DEV, capacity, width)
    single = (ep_count, capacity, width)
    others = ep_count - 1
    small = (8, width)
    pg_shape = (4, ep_count, cols // ep_count, width)
    y_shape = (4, others, cols // ep_count, width)
    many = 3 + others + 3
    return pl.pallas_call(
        functools.partial(layer_kernel, ep_count, cols // HD, n),
        out_shape=(
            struct((2, n, 4, CHUNK, width), BF),
            struct((ep_count, proj, chunk, width), BF),
            struct(small, F32), struct((rows, width), F32), struct((rows, width), BF),
        ),
        in_specs=[vmem] * 14 + [hbm] * 4,
        out_specs=(hbm, vmem, vmem, vmem, vmem),
        scratch_shapes=[
            pltpu.VMEM((hidden // width, 2, width, width), BF),
            pltpu.VMEM((4, rows, width), BF), pltpu.VMEM((group_rows, 3 * cols), BF),
            pltpu.VMEM((group_rows, cols), BF), pltpu.VMEM((group_rows, 8), F32), pltpu.VMEM((rows, width), F32),
            pltpu.VMEM((4,) + single, BF), pltpu.VMEM((4,) + single, BF),
            pltpu.VMEM((2, rows, ep_count * EXP_DEV * capacity), BF),
            pltpu.VMEM((3 * cols, width), BF), pltpu.VMEM((group_rows, group_rows), F32),
            pltpu.VMEM((2, rows, width), F32), pltpu.VMEM((2, rows, width), F32),
            pltpu.VMEM((rows, width), BF), pltpu.VMEM((rows, width), BF),
            pltpu.VMEM(block, BF), pltpu.VMEM(block, BF), pltpu.VMEM(single, BF), pltpu.VMEM(single, BF),
            pltpu.VMEM((ep_count * capacity, width), F32), pltpu.VMEM((ep_count * capacity, width), F32),
            pltpu.VMEM(block, BF), pltpu.VMEM(block, BF),
            pltpu.VMEM((gathered, quarter), BF), pltpu.VMEM((gathered, quarter), BF),
            pltpu.VMEM((2, width, width), F32),
            pltpu.VMEM((2, n, CHUNK, width), BF), pltpu.VMEM((2, n, 4, CHUNK, width), BF),
            pltpu.VMEM((proj, chunk, width), F32), pltpu.VMEM((2, proj // 2, chunk, width), BF),
            pltpu.VMEM(pg_shape, BF), pltpu.VMEM(y_shape, BF),
            pltpu.VMEM(block, BF), pltpu.VMEM(block, BF),
            pltpu.VMEM((4, rows, width), BF),
            pltpu.VMEM((group_rows, cols), BF), pltpu.VMEM((group_rows, 3 * cols), BF),
            pltpu.VMEM((2, rows, width), BF), pltpu.VMEM((2, rows, width), BF),
            pltpu.VMEM((rows, width), BF), pltpu.VMEM((rows, width), BF),
            pltpu.VMEM(small, F32), pltpu.VMEM((3,) + small, F32), pltpu.VMEM((others,) + small, F32),
            pltpu.VMEM((3,) + small, F32), pltpu.VMEM(small, F32), pltpu.VMEM(small, F32),
            dma((2, 2, hidden // width)), dma((2, 3)), dma((2, 3)), dma((2, 2)), dma((2, 2)), dma((2,)), dma((2,)),
            dma((2, 2, others)), dma((2, 2, others)), dma((2, ep_count, 3)), dma((2, ep_count, 3)),
            dma((2, n)), dma((2, n)), dma((2, n)), dma((2, 2, n)), dma((2, n)),
            dma((3, 2, n)), dma((3, 2, n)), dma((2, n)),
            dma((2, proj // 2)), dma((2, proj // 2)), dma((2, proj // 2)), dma((2, 2, proj // 2)), dma((2, proj // 2)),
            dma((4, others)), dma((4, others)), dma((others, 2, proj // 2)), dma((others, 2, proj // 2)),
            dma((2, 2, others)), dma((2, 2, others)), dma((many,)), dma((many,)),
        ],
        compiler_params=pltpu.CompilerParams(
            collective_id=0, has_side_effects=True, vmem_limit_bytes=62 * 1024 * 1024
        ),
        name="layer",
    )(tokens, segment, key_mask, routes, gates, cot, g1, b1, wq, wk, wv, wo, g2, b2, fin, fout, tin, tout)


def finish_kernel(
    tp_ref, rg_ref, pfin_ref, small_ref, grad_ref, layer_ref,
    gin_ref, gout_ref, o_ref, v_ref, q_ref, k_ref, tokens_ref, result_ref, a_ref, b_ref, c_ref, d_ref, count_ref,
):
    width = gin_ref.shape[0]
    gin_ref[...] = rg_ref[0, :, 0].reshape(width, -1).astype(F32)
    gout_ref[...] = rg_ref[1, :, 0].reshape(-1, width).astype(F32)

    @pl.when(pl.program_id(0) == 0)
    def _():
        owners = pfin_ref.shape[0]
        span = q_ref.shape[0] // owners
        for index, ref in enumerate((o_ref, v_ref, q_ref, k_ref)):
            for owner in range(owners):
                value = pfin_ref[owner, 3 * index : 3 * index + 3].reshape(span, width)
                ref[owner * span : (owner + 1) * span, :] = value.astype(F32)
        tokens_ref[...] = grad_ref[...]
        result_ref[...] = layer_ref[...]
        for index, ref in enumerate((a_ref, b_ref, c_ref, d_ref)):
            ref[...] = small_ref[index : index + 1, :].reshape(width)
        count_ref[...] = small_ref[4:5, 0:128].astype(jnp.int32).reshape(128)[: count_ref.shape[0]]


def finish(rg, pfin, small, grad, layer, cols, experts):
    _, n, _, chunk, width = rg.shape
    hidden = 4 * width
    me = lax.axis_index("tp").astype(jnp.int32).reshape(1)
    struct = jax.ShapeDtypeStruct

    def where(quarter, me_ref):
        mine = me_ref[0]
        low = (quarter % 2) != (mine % 2)
        high = (quarter // 2) != (mine // 2)
        return jnp.where(low, 1, 0) + jnp.where(high, 2, 0)

    def whole(shape):
        return pl.BlockSpec(shape, lambda q, t: (0,) * len(shape))

    outs = [struct((cols, width), F32)] * 4 + [struct(grad.shape, F32), struct(layer.shape, BF)]
    outs += [struct((width,), F32)] * 4 + [struct((experts,), jnp.int32)]
    return pl.pallas_call(
        finish_kernel,
        grid_spec=pltpu.PrefetchScalarGridSpec(
            num_scalar_prefetch=1,
            grid=(4,),
            in_specs=[
                pl.BlockSpec((2, n, 1, chunk, width), lambda q, t: (0, 0, where(q, t), 0, 0)),
                whole(pfin.shape), whole(small.shape), whole(grad.shape), whole(layer.shape),
            ],
            out_specs=[
                pl.BlockSpec((width, width), lambda q, t: (0, q)),
                pl.BlockSpec((width, width), lambda q, t: (q, 0)),
            ] + [whole(out.shape) for out in outs],
        ),
        out_shape=[struct((width, hidden), F32), struct((hidden, width), F32)] + outs,
        name="finish",
    )(me, rg, pfin, small, grad, layer)


def local(
    tokens,
    segment,
    key_mask,
    routes,
    gates,
    ln1_gain,
    ln1_bias,
    query_weight,
    key_weight,
    value_weight,
    out_weight,
    ln2_gain,
    ln2_bias,
    frozen_in,
    frozen_out,
    train_in,
    train_out,
    cotangent,
):
    vectors = (ln1_gain, ln1_bias, ln2_gain, ln2_bias)
    flat = (query_weight.T, key_weight.T, value_weight.T, out_weight)
    cols = out_weight.shape[0]
    token_args = (tokens[0], segment, key_mask, routes[0].T, gates[0].T, cotangent[0])
    rg, pfin, small, grad, layer = layer_step(
        *token_args, *vectors[:2], *flat, *vectors[2:], frozen_in[0], frozen_out[0], train_in[0], train_out[0]
    )
    grad_in, grad_out, out, value, query, key, grad, layer, *sums, counts = finish(
        rg, pfin, small, grad, layer, cols, EXP_DEV * lax.axis_size("ep")
    )
    gain_one, bias_one, gain_two, bias_two = sums
    return (
        layer[None], grad[None], gain_one, bias_one, query.T, key.T, value.T, out, gain_two, bias_two,
        grad_in[None], grad_out[None], counts,
    )


def solution(mesh):
    in_specs = (
        P(("ep", "dp"), "tp", None),
        P(("ep", "dp"), None),
        P(("ep", "dp"), None),
        P(("ep", "dp"), "tp", None),
        P(("ep", "dp"), "tp", None),
        P(),
        P(),
        P(None, "tp"),
        P(None, "tp"),
        P(None, "tp"),
        P("tp", None),
        P(),
        P(),
        P("ep", None, None),
        P("ep", None, None),
        P("ep", None, None),
        P("ep", None, None),
        P(("ep", "dp"), "tp", None),
    )
    out_specs = (
        P(("ep", "dp"), "tp", None),
        P(("ep", "dp"), "tp", None),
        P(),
        P(),
        P(None, "tp"),
        P(None, "tp"),
        P(None, "tp"),
        P("tp", None),
        P(),
        P(),
        P("ep", None, None),
        P("ep", None, None),
        P(),
    )
    return jax.shard_map(local, mesh=mesh, in_specs=in_specs, out_specs=out_specs, check_vma=False)
```

time: 190 us -> 157 us (0.83)
  Pallas kernels: 183 us -> 156 us
  other arithmetic: 5.15 us -> 0 us
    pallas_call x2 -> x1, Pallas kernels: 171 us -> 144 us  [layer_step(): pl.pallas_call(functools.partial(layer_kernel, ep_count, cols // HD, n),...]
    pallas_call x4 -> x0, other arithmetic: 5.15 us -> none  [finish(): pl.pallas_call(finish_kernel, grid_spec=pltpu.PrefetchScalarGridSpec(num_...]
where the time goes in v4:
time: 157 us
  Pallas kernels  156 us (99%)
    pallas_call x1, Pallas kernels, layer_step(): pl.pallas_call(functools.partial(layer_kernel, ep_count, cols // HD, n),...  144 us
    pallas_call x1, Pallas kernels, finish(): pl.pallas_call(finish_kernel, grid_spec=pltpu.PrefetchScalarGridSpec(num_...  12.2 us

profile of v4, /device:TPU:0, one launch (start us, length us, event | category | flops | bytes accessed | tf_op | source)
XLA Modules:
  0.0 156.9 jit_solution(14170777022472091713)
XLA Ops:
  0.7 143.9 %layer.1 = (bf16[2,24,4,32,768]{4,3,2,1,0:T(8,128)(2,1)}, bf16[2,12,32,768]{3,2,1,0:T(8,128)(2,1)}, f32[8,768]{1,0:T(8,128)}, f32[128,768]{1,0:T(8,128)}, bf16[128,768]{1,0:T(8,128)(2,1)}) custom-call(bf16[128,768]{1,0:T(8,128)(2,1)} %bitcast.30, s32[1,512]{1,0:T(1,128)} %seg_ref.1, s32[1,512]{1,0:T(1,128)} %key_ref.1, s32[2,128]{1,0:T(2,128)} %bitcast.32, ...), custom_call_target="tpu_custom_call" | custom-call | tf_op jit(solution)/shard_map/layer/pallas_call | solution.py:771
  144.6 12.2 %finish.1 = (f32[768,3072]{1,0:T(8,128)}, f32[3072,768]{1,0:T(8,128)}, f32[192,768]{1,0:T(8,128)}, f32[192,768]{1,0:T(8,128)}, f32[192,768]{1,0:T(8,128)}, /*ind...) custom-call(s32[1]{0:T(128)} %bitcast.tp_ref, ...), custom_call_target="tpu_custom_call" | custom-call | tf_op jit(solution)/shard_map/finish/pallas_call | solution.py:859

commit v5 on v4

--- a/solution.py
+++ b/solution.py
@@ -16,6 +16,10 @@
 BF = jnp.bfloat16
 F32 = jnp.float32
 CHUNK = 32
+STEPS = (6, 3, 3, 1, 1, 3, 3, 3)
+LAGS = (6, 8)
+AHEAD = 2
+FIRST = 1
 
 
 def tp_peers():
@@ -127,9 +131,9 @@
 
 
 class Chain:
-    def __init__(self, base, count, own, stage, final, sems, hooks):
+    def __init__(self, base, count, own, stage, near, home, final, sems, hooks):
         self.base, self.count, self.own, self.stage = base, count, own, stage
-        self.final, self.hooks = final, hooks
+        self.near, self.home, self.final, self.hooks = near, home, final, hooks
         self.red_send, self.recv_a, self.recv_b, self.bc_send, self.bc_recv = sems
         self.dp = lax.axis_index("dp")
 
@@ -143,38 +147,39 @@
     def red(self, half, index, near):
         toward, away = self.peers(half)
         landing = self.stage.at[half, index]
-        target, sem = (self.final(half, index), self.recv_b) if near else (landing, self.recv_a)
+        target, sem = (self.near(half, index), self.recv_b) if near else (landing, self.recv_a)
         return remote(
             landing, target, self.red_send.at[half, index], sem.at[half, index],
             {"dp": away if near else toward},
         )
 
-    def spread(self, half, index, near):
+    def spread(self, half, index, near, source=None):
         toward, away = self.peers(half)
         ref = self.final(half, index)
         return remote(
-            ref, ref, self.bc_send.at[1 if near else 0, half, index], self.bc_recv.at[half, index],
+            (source or self.final)(half, index), ref, self.bc_send.at[1 if near else 0, half, index], self.bc_recv.at[half, index],
             {"dp": toward if near else away},
         )
+
+    def offer(self, index):
+        for half in (0, 1):
+            place = self.place(half)
+
+            @pl.when((place == 0) | (place == 3))
+            def _():
+                self.stage[half, index] = self.own(half, index).astype(BF)
+
+            pl.when(place == 0)(lambda: self.red(half, index, False).start())
+            pl.when(place == 3)(lambda: self.red(half, index, True).start())
 
     def step(self, s):
         for half in (0, 1):
             place = self.place(half)
-            index = s - self.base - (2 * place - 4 * (place // 3))
-
-            @pl.when((index >= 0) & (index < self.count))
+            index = s - self.base - 2 * place
+
+            @pl.when((index >= 0) & (index < self.count) & ((place == 1) | (place == 2)))
             def _():
                 own = self.own(half, index)
-
-                @pl.when(place == 0)
-                def _():
-                    self.stage[half, index] = own.astype(BF)
-                    self.red(half, index, False).start()
-
-                @pl.when(place == 3)
-                def _():
-                    self.stage[half, index] = own.astype(BF)
-                    self.red(half, index, True).start()
 
                 @pl.when(place == 1)
                 def _():
@@ -186,8 +191,8 @@
                 def _():
                     self.red(half, index, False).wait_recv()
                     self.red(half, index, True).wait_recv()
-                    total = own + self.stage[half, index].astype(F32) + self.final(half, index)[...].astype(F32)
-                    self.final(half, index)[...] = total.astype(BF)
+                    total = own + self.stage[half, index].astype(F32) + self.near(half, index)[...].astype(F32)
+                    self.home(half, index)[...] = total.astype(BF)
 
         for half in (0, 1):
             place = self.place(half)
@@ -197,8 +202,8 @@
             def _():
                 @pl.when(place == 2)
                 def _():
-                    self.spread(half, index, False).start()
-                    self.spread(half, index, True).start()
+                    self.spread(half, index, False, self.home).start()
+                    self.spread(half, index, True, self.home).start()
 
                 @pl.when(place != 2)
                 def _():
@@ -211,7 +216,7 @@
                 self.hooks[0](half, index)
 
             for later, hook in enumerate(self.hooks[1:]):
-                after = index - 2 * (later + 1)
+                after = index - LAGS[later]
                 pl.when((after >= 0) & (after < self.count))(functools.partial(hook, half, after))
 
     def drain(self, index):
@@ -235,10 +240,10 @@
     ep_count, heads, n,
     tok_ref, seg_ref, key_ref, routes_ref, gates_ref, cot_ref, g1_ref, b1_ref, wq_ref, wk_ref, wv_ref, wo_ref,
     g2_ref, b2_ref, fin_hbm, fout_hbm, tin_hbm, tout_hbm,
-    rg_hbm, pfin, small_out, grad_ref, layer_ref,
+    rg, pfin, small_out, grad_ref, layer_ref,
     weights, group_ref, qkv_ref, heads_ref, lse_ref, middle_ref, gx, gs, picks, joined, bias,
     part, core_slot, mix, x_slot, sx, ss, ax, as_, out_acc, back_acc, out_ref, back_ref,
-    act, slope, own, stage, fin, acc, pstage, pgbuf, yslot, ret_back, ret_out,
+    act, slope, own, stage, near_slot, acc, pstage, pgbuf, yslot, ret_back, ret_out,
     piece, up_heads, pgrad, bpart, bcore_slot, bmix, bx_slot,
     sm, sm_tp, sm_ep, sm_dp, sm_a, sm_b,
     w_sem, a_send, a_recv, c_send, c_recv, m_send, m_recv, e_send, e_recv, t_send, t_recv,
@@ -258,12 +263,16 @@
     frozen, train = 0, 1
     offsets = range(1, ep_count)
 
+    def slot_of(expert, index):
+        return index if expert == train else (tp + 1 + index) % pieces
+
     def weight_loads(expert, index):
+        slot = slot_of(expert, index)
         source_in, source_out = ((fin_hbm, fout_hbm), (tin_hbm, tout_hbm))[expert]
         at = pl.ds(pl.multiple_of(index * width, width), width)
         return [
-            pltpu.make_async_copy(source_in.at[:, at], weights.at[index, 0], w_sem.at[expert, 0, index]),
-            pltpu.make_async_copy(source_out.at[at, :], weights.at[index, 1], w_sem.at[expert, 1, index]),
+            pltpu.make_async_copy(source_in.at[:, at], weights.at[slot, 0], w_sem.at[expert, 0, index]),
+            pltpu.make_async_copy(source_out.at[at, :], weights.at[slot, 1], w_sem.at[expert, 1, index]),
         ]
 
     residual = tok_ref[...].astype(F32)
@@ -411,13 +420,14 @@
         forward(1, off)
     pass_on(0)
 
-    def expert_piece(index, inputs, shares):
-        before = dot_nn(inputs, weights[index, 0])
-        through = dot_nt(shares, weights[index, 1])
+    def expert_piece(expert, index, inputs, shares):
+        slot = slot_of(expert, index)
+        before = dot_nn(inputs, weights[slot, 0])
+        through = dot_nt(shares, weights[slot, 1])
         value, grad = gelu_pair(before)
         slopes = (through * grad).astype(BF)
-        produced = dot_nn(value.astype(BF), weights[index, 1])
-        returned = dot_nt(slopes, weights[index, 0])
+        produced = dot_nn(value.astype(BF), weights[slot, 1])
+        returned = dot_nt(slopes, weights[slot, 0])
 
         @pl.when(index == 0)
         def _():
@@ -459,7 +469,12 @@
     def train_piece(index, _):
         for copy in weight_loads(train, index):
             copy.wait()
-        expert_piece(index, gx[0].reshape(tokens, width), gs[0].reshape(tokens, width))
+        expert_piece(train, index, gx[0].reshape(tokens, width), gs[0].reshape(tokens, width))
+
+        @pl.when(index != tp)
+        def _():
+            for copy in weight_loads(frozen, (index + pieces - 1 - tp) % pieces):
+                copy.start()
 
         @pl.when(index == 1)
         def _():
@@ -473,6 +488,17 @@
     give_back(train)
     for off in offsets:
         forward(0, off)
+
+    def frozen_piece(index, _):
+        for copy in weight_loads(frozen, index):
+            copy.wait()
+        expert_piece(frozen, index, ax[...].reshape(tokens, width), as_[...].reshape(tokens, width))
+        return 0
+
+    for kind in (0, 1):
+        for off in offsets:
+            owner_wait(kind, frozen, off)
+    lax.fori_loop(0, AHEAD, frozen_piece, 0)
 
     def hidden_block(index, _):
         for hop, when in ((1, 1), (3, 3)):
@@ -491,23 +517,33 @@
         return 0
 
     lax.fori_loop(0, 4, hidden_block, 0)
-    for index in range(pieces):
-        for copy in weight_loads(frozen, index):
-            copy.start()
-
-    def x_copy(half, index, hop):
+    for copy in weight_loads(frozen, pieces - 1):
+        copy.start()
+
+    def x_copy(half, index, hop, owner=False):
         source, peer = ((0, tp1), (0, tp2), (2, tp1))[hop - 1]
+        from_ref = stage.at[half, index] if owner else rg.at[half, index, source]
         return remote(
-            fin.at[half, index, source], fin.at[half, index, hop],
+            from_ref, rg.at[half, index, hop],
             x_send.at[hop - 1, half, index], x_recv.at[hop - 1, half, index], {"tp": peer},
         )
 
     def out_copy_of(half, index):
-        return pltpu.make_async_copy(fin.at[half, index], rg_hbm.at[half, index], out_sem.at[half, index])
+        return pltpu.make_async_copy(stage.at[half, index], rg.at[half, index, 0], out_sem.at[half, index])
 
     def cross_first(half, index):
-        x_copy(half, index, 2).start()
-        x_copy(half, index, 1).start()
+        owner = expert_chain.place(half) == 2
+
+        @pl.when(owner)
+        def _():
+            x_copy(half, index, 2, True).start()
+            x_copy(half, index, 1, True).start()
+            out_copy_of(half, index).start()
+
+        @pl.when(jnp.logical_not(owner))
+        def _():
+            x_copy(half, index, 2).start()
+            x_copy(half, index, 1).start()
 
     def cross_second(half, index):
         x_copy(half, index, 2).wait_recv()
@@ -516,11 +552,11 @@
     def cross_third(half, index):
         x_copy(half, index, 1).wait_recv()
         x_copy(half, index, 3).wait_recv()
-        out_copy_of(half, index).start()
 
     expert_chain = Chain(
         0, n, lambda half, index: own[half, pl.ds(pl.multiple_of(index * CHUNK, CHUNK), CHUNK), :],
-        stage, lambda half, index: fin.at[half, index, 0],
+        stage, lambda half, index: near_slot.at[half, index], lambda half, index: stage.at[half, index],
+        lambda half, index: rg.at[half, index, 0],
         (red_send, recv_a, recv_b, bc_send, bc_recv), (cross_first, cross_second, cross_third),
     )
     span = 128
@@ -529,38 +565,32 @@
         at = pl.ds(pl.multiple_of(index * span, span), span)
         own[0, at, :] = dot_tn(gx[:, :, :, at].reshape(-1, span), slope[...])
         own[1, at, :] = dot_tn(act[:, at], gs[...].reshape(-1, width))
-        expert_chain.step(index)
+        @pl.when(index < blocks - 1)
+        def _():
+            for part_of in range(share_of):
+                expert_chain.offer(index * share_of + part_of)
+
         return 0
 
-    first_steps = width // span
-    lax.fori_loop(0, first_steps, outer, 0)
-
-    def frozen_piece(index, _):
-        for copy in weight_loads(frozen, index):
-            copy.wait()
-        expert_piece(index, ax[...].reshape(tokens, width), as_[...].reshape(tokens, width))
-        expert_chain.step(first_steps + index)
-        return 0
-
-    for kind in (0, 1):
-        for off in offsets:
-            owner_wait(kind, frozen, off)
-    lax.fori_loop(0, pieces, frozen_piece, 0)
-    give_back(frozen)
-    clock = [first_steps + pieces]
+    blocks, share_of = width // span, span // CHUNK
+    lax.fori_loop(0, FIRST, outer, 0)
+    clock = [0]
     proj_chain = None
 
     def run(count):
         def body(s, _):
-            expert_chain.step(s)
             if proj_chain is not None:
                 proj_chain.step(s)
+            expert_chain.step(s)
             return 0
 
         lax.fori_loop(clock[0], clock[0] + count, body, 0)
         clock[0] += count
 
-    run(2)
+    lax.fori_loop(AHEAD, pieces, frozen_piece, 0)
+    give_back(frozen)
+    lax.fori_loop(FIRST, blocks, outer, 0)
+    run(STEPS[0])
     return_wait(0)
     second = dot_nn(picks[0] + picks[1], ret_back[...].reshape(slots, width))
     inner_grad, gain_two, bias_two = ln_backward(middle_ref[...], row_of(g2_ref), second)
@@ -571,7 +601,7 @@
     send(gather_copy(1, piece, tp, 0, tp1))
     sm[2:3, :] = gain_two
     sm[3:4, :] = bias_two
-    run(1)
+    run(STEPS[1])
 
     def head_rows(slot):
         at = pl.ds(pl.multiple_of(slot * rows, rows), rows)
@@ -583,7 +613,7 @@
     gather_copy(1, piece, tp2, 1, tp2).wait_recv()
     send(gather_copy(1, piece, tp2, 2, tp1))
     head_rows(tp2)
-    run(1)
+    run(STEPS[2])
     gather_copy(1, piece, tp3, 2, tp1).wait_recv()
     head_rows(tp3)
 
@@ -607,7 +637,6 @@
         acc[3 * batch : 3 * batch + 3] = total.reshape((3,) + acc.shape[1:])
 
     proj_start(0, dot_tn(heads_ref[...], piece[...].reshape(group_rows, width)))
-    run(1)
     for head in range(heads):
         low, high = head * HD, (head + 1) * HD
         key_sum = value_sum = None
@@ -629,7 +658,7 @@
             value_sum = value_part if value_sum is None else value_sum + value_part
         pgrad[:, cols + low : cols + high] = (key_sum * scale).astype(BF)
         pgrad[:, 2 * cols + low : 2 * cols + high] = value_sum.astype(BF)
-        run(1)
+        run(STEPS[3])
 
     def back_partial(slot):
         at = pl.ds(pl.multiple_of(slot * rows, rows), rows)
@@ -642,16 +671,17 @@
     send(back_core_copy(0))
     bpart[1] = back_partial(tp1).astype(BF)
     send(back_core_copy(1))
+    normed = group_ref[...].reshape(group_rows, width)
+    for batch, part_index in ((1, 2), (2, 0), (3, 1)):
+        proj_start(batch, dot_tn(pgrad[:, part_index * cols : (part_index + 1) * cols], normed))
     crossing = back_partial(tp2)
     mine = back_partial(tp)
+    run(STEPS[4])
     back_core_copy(0).wait_recv()
     bmix[...] = (crossing + bcore_slot[0].astype(F32)).astype(BF)
     back_cross = remote(bmix, bx_slot, m_send.at[1], m_recv.at[1], {"tp": tp2})
     send(back_cross)
-    normed = group_ref[...].reshape(group_rows, width)
-    for batch, part_index in ((1, 2), (2, 0), (3, 1)):
-        proj_start(batch, dot_tn(pgrad[:, part_index * cols : (part_index + 1) * cols], normed))
-        run(1)
+    run(STEPS[5])
     back_core_copy(1).wait_recv()
     back_cross.wait_recv()
     first = mine + bcore_slot[1].astype(F32) + bx_slot[...].astype(F32)
@@ -683,13 +713,18 @@
             y_gather(half, index, off).start()
 
     proj_n = acc.shape[0] // 2
-    proj_base = max(n, clock[0])
+    proj_base = n - share_of
+    assert proj_n >= share_of and clock[0] <= proj_base + 2
     proj_chain = Chain(
         proj_base, proj_n, lambda half, index: acc[2 * index + half], pstage,
-        lambda half, index: pfin.at[ep, 2 * index + half],
+        *[lambda half, index: pfin.at[ep, 2 * index + half]] * 3,
         (pred_send, precv_a, precv_b, pbc_send, pbc_recv), (y_first,),
     )
-    run(1)
+    for index in range(proj_n):
+        proj_chain.offer(index)
+        if index < share_of:
+            expert_chain.offer(n - share_of + index)
+    run(STEPS[6])
     return_wait(1)
     returned = ret_out[...].reshape(slots, width)
     gate0, gate1 = columns_of(gates_ref)
@@ -700,7 +735,7 @@
     sm_a[...] = sm[...] + sm_tp[0] + sm_tp[1] + sm_tp[2]
     for off in offsets:
         small_copy(2 + off, sm_a, sm_ep.at[off - 1], {"ep": (ep + off) % ep_count})
-    run(2)
+    run(STEPS[7])
     for copy in small[3:]:
         copy.wait_recv()
     total = sm_a[...]
@@ -709,11 +744,10 @@
     sm_b[...] = total
     for off in range(1, 4):
         small_copy(1 + ep_count + off, sm_b, sm_dp.at[off - 1], {"dp": (dp + off) % 4})
-    run(2)
+    run(max(n + 8 + LAGS[1], proj_base + proj_n + 8) - clock[0])
     for copy in small[2 + ep_count :]:
         copy.wait_recv()
     small_out[...] = sm_b[...] + sm_dp[0] + sm_dp[1] + sm_dp[2]
-    run(max(n + 12, proj_base + proj_n + 8) - clock[0])
 
     def y_finish(index, _):
         for half in (0, 1):
@@ -737,7 +771,7 @@
         for half in (0, 1):
             for hop in (1, 2, 3):
                 x_copy(half, index, hop).wait_send()
-            out_copy_of(half, index).wait()
+            pl.when(expert_chain.place(half) == 2)(out_copy_of(half, index).wait)
         return 0
 
     lax.fori_loop(0, n, drain, 0)
@@ -771,9 +805,9 @@
     return pl.pallas_call(
         functools.partial(layer_kernel, ep_count, cols // HD, n),
         out_shape=(
-            struct((2, n, 4, CHUNK, width), BF),
-            struct((ep_count, proj, chunk, width), BF),
-            struct(small, F32), struct((rows, width), F32), struct((rows, width), BF),
+            pltpu.VMEM((2, n, 4, CHUNK, width), BF),
+            pltpu.VMEM((ep_count, proj, chunk, width), BF),
+            pltpu.VMEM(small, F32), pltpu.VMEM((rows, width), F32), pltpu.VMEM((rows, width), BF),
         ),
         in_specs=[vmem] * 14 + [hbm] * 4,
         out_specs=(hbm, vmem, vmem, vmem, vmem),
@@ -791,7 +825,7 @@
             pltpu.VMEM(block, BF), pltpu.VMEM(block, BF),
             pltpu.VMEM((gathered, quarter), BF), pltpu.VMEM((gathered, quarter), BF),
             pltpu.VMEM((2, width, width), F32),
-            pltpu.VMEM((2, n, CHUNK, width), BF), pltpu.VMEM((2, n, 4, CHUNK, width), BF),
+            pltpu.VMEM((2, n, CHUNK, width), BF), pltpu.VMEM((2, n, CHUNK, width), BF),
             pltpu.VMEM((proj, chunk, width), F32), pltpu.VMEM((2, proj // 2, chunk, width), BF),
             pltpu.VMEM(pg_shape, BF), pltpu.VMEM(y_shape, BF),
             pltpu.VMEM(block, BF), pltpu.VMEM(block, BF),
@@ -810,7 +844,7 @@
             dma((2, 2, others)), dma((2, 2, others)), dma((many,)), dma((many,)),
         ],
         compiler_params=pltpu.CompilerParams(
-            collective_id=0, has_side_effects=True, vmem_limit_bytes=62 * 1024 * 1024
+            collective_id=0, has_side_effects=True, vmem_limit_bytes=51 * 1024 * 1024
         ),
         name="layer",
     )(tokens, segment, key_mask, routes, gates, cot, g1, b1, wq, wk, wv, wo, g2, b2, fin, fout, tin, tout)
@@ -820,11 +854,11 @@
     tp_ref, rg_ref, pfin_ref, small_ref, grad_ref, layer_ref,
     gin_ref, gout_ref, o_ref, v_ref, q_ref, k_ref, tokens_ref, result_ref, a_ref, b_ref, c_ref, d_ref, count_ref,
 ):
-    width = gin_ref.shape[0]
-    gin_ref[...] = rg_ref[0, :, 0].reshape(width, -1).astype(F32)
-    gout_ref[...] = rg_ref[1, :, 0].reshape(-1, width).astype(F32)
-
-    @pl.when(pl.program_id(0) == 0)
+    width = gin_ref.shape[1]
+    gin_ref[...] = rg_ref[0, :, 0].reshape(gin_ref.shape).astype(F32)
+    gout_ref[...] = rg_ref[1, :, 0].reshape(gout_ref.shape).astype(F32)
+
+    @pl.when((pl.program_id(0) == 0) & (pl.program_id(1) == 0))
     def _():
         owners = pfin_ref.shape[0]
         span = q_ref.shape[0] // owners
@@ -842,6 +876,7 @@
 def finish(rg, pfin, small, grad, layer, cols, experts):
     _, n, _, chunk, width = rg.shape
     hidden = 4 * width
+    parts = 1
     me = lax.axis_index("tp").astype(jnp.int32).reshape(1)
     struct = jax.ShapeDtypeStruct
 
@@ -852,7 +887,7 @@
         return jnp.where(low, 1, 0) + jnp.where(high, 2, 0)
 
     def whole(shape):
-        return pl.BlockSpec(shape, lambda q, t: (0,) * len(shape))
+        return pl.BlockSpec(shape, lambda q, i, t: (0,) * len(shape))
 
     outs = [struct((cols, width), F32)] * 4 + [struct(grad.shape, F32), struct(layer.shape, BF)]
     outs += [struct((width,), F32)] * 4 + [struct((experts,), jnp.int32)]
@@ -860,19 +895,20 @@
         finish_kernel,
         grid_spec=pltpu.PrefetchScalarGridSpec(
             num_scalar_prefetch=1,
-            grid=(4,),
+            grid=(4, parts),
             in_specs=[
-                pl.BlockSpec((2, n, 1, chunk, width), lambda q, t: (0, 0, where(q, t), 0, 0)),
-                whole(pfin.shape), whole(small.shape), whole(grad.shape), whole(layer.shape),
+                pl.BlockSpec((2, n // parts, 1, chunk, width), lambda q, i, t: (0, i, where(q, t), 0, 0)),
+                *[pl.BlockSpec(memory_space=pltpu.VMEM)] * 4,
             ],
             out_specs=[
-                pl.BlockSpec((width, width), lambda q, t: (0, q)),
-                pl.BlockSpec((width, width), lambda q, t: (q, 0)),
+                pl.BlockSpec((width // parts, width), lambda q, i, t: (i, q)),
+                pl.BlockSpec((width // parts, width), lambda q, i, t: (parts * q + i, 0)),
             ] + [whole(out.shape) for out in outs],
         ),
         out_shape=[struct((width, hidden), F32), struct((hidden, width), F32)] + outs,
+        compiler_params=pltpu.CompilerParams(vmem_limit_bytes=40 * 1024 * 1024),
         name="finish",
-    )(me, rg, pfin, small, grad, layer)
+    )(me, *[pltpu.with_memory_space_constraint(value, pltpu.VMEM) for value in (rg, pfin, small, grad, layer)])
 
 
 def local(

time: 157 us -> 150 us (0.955)
  Pallas kernels: 156 us -> 149 us
    pallas_call x1, Pallas kernels: 12.2 us -> 8.29 us  [finish(): pl.pallas_call(finish_kernel, grid_spec=pltpu.PrefetchScalarGridSpec(num_...]
    pallas_call x1, Pallas kernels: 144 us -> 141 us  [layer_step(): pl.pallas_call(functools.partial(layer_kernel, ep_count, cols // HD, n),...]
where the time goes in v5:
time: 150 us
  Pallas kernels  149 us (99%)
    pallas_call x1, Pallas kernels, layer_step(): pl.pallas_call(functools.partial(layer_kernel, ep_count, cols // HD, n),...  141 us
    pallas_call x1, Pallas kernels, finish(): pl.pallas_call(finish_kernel, grid_spec=pltpu.PrefetchScalarGridSpec(num_...  8.29 us

profile of v5, /device:TPU:0, one launch (start us, length us, event | category | flops | bytes accessed | tf_op | source)
XLA Modules:
  0.0 150.0 jit_solution(10419634448876502084)
XLA Ops:
  0.7 140.9 %layer.1 = (bf16[2,24,4,32,768]{4,3,2,1,0:T(8,128)(2,1)S(1)}, bf16[2,12,32,768]{3,2,1,0:T(8,128)(2,1)S(1)}, f32[8,768]{1,0:T(8,128)S(1)}, f32[128,768]{1,0:T(8,128)S(1)}, bf16[128,768]{1,0:T(8,128)(2,1)S(1)}) custom-call(bf16[128,768]{1,0:T(8,128)(2,1)} %bitcast.30, s32[1,512]{1,0:T(1,128)} %seg_ref.1, s32[1,512]{1,0:T(1,128)} %key_ref.1, ...), custom_call_target="tpu_custom_call" | custom-call | tf_op jit(solution)/shard_map/layer/pallas_call | solution.py:805
  141.5 8.3 %finish.1 = (f32[768,3072]{1,0:T(8,128)}, f32[3072,768]{1,0:T(8,128)}, f32[192,768]{1,0:T(8,128)}, f32[192,768]{1,0:T(8,128)}, f32[192,768]{1,0:T(8,128)}, /*ind...) custom-call(s32[1]{0:T(128)} %bitcast.tp_ref, ...), custom_call_target="tpu_custom_call" | custom-call | tf_op jit(solution)/shard_map/finish/pallas_call | solution.py:894

commit v6 on v5

--- a/solution.py
+++ b/solution.py
@@ -16,7 +16,8 @@
 BF = jnp.bfloat16
 F32 = jnp.float32
 CHUNK = 32
-STEPS = (6, 3, 3, 1, 1, 3, 3, 3)
+STEPS = (6, 3, 3, 1, 1, 3, 6, 6)
+GAP = 2
 LAGS = (6, 8)
 AHEAD = 2
 FIRST = 1
@@ -175,7 +176,7 @@
     def step(self, s):
         for half in (0, 1):
             place = self.place(half)
-            index = s - self.base - 2 * place
+            index = s - self.base - GAP * place
 
             @pl.when((index >= 0) & (index < self.count) & ((place == 1) | (place == 2)))
             def _():
@@ -196,7 +197,7 @@
 
         for half in (0, 1):
             place = self.place(half)
-            index = s - self.base - (8 - 2 * place + 4 * (place // 3))
+            index = s - self.base - GAP * (4 - place + 2 * (place // 3))
 
             @pl.when((index >= 0) & (index < self.count))
             def _():
@@ -369,7 +370,6 @@
     gather_copy(0, group_ref, tp2, 1, tp2).wait_recv()
     send(gather_copy(0, group_ref, tp2, 2, tp1))
     project(tp2)
-    pass_on(1)
     gather_copy(0, group_ref, tp3, 2, tp1).wait_recv()
     project(tp3)
 
@@ -407,6 +407,7 @@
     mix[...] = (crossing + core_slot[0]).astype(BF)
     cross = remote(mix, x_slot, m_send.at[0], m_recv.at[0], {"tp": tp2})
     send(cross)
+    pass_on(1)
     forward(1, 0)
     core_copy(1).wait_recv()
     mine = mine + core_slot[1]
@@ -681,7 +682,36 @@
     bmix[...] = (crossing + bcore_slot[0].astype(F32)).astype(BF)
     back_cross = remote(bmix, bx_slot, m_send.at[1], m_recv.at[1], {"tp": tp2})
     send(back_cross)
+    def y_gather(half, index, off):
+        chunk = 2 * index + half
+        return remote(
+            pfin.at[ep, chunk], pfin.at[ep, chunk], g_send.at[off - 1, half, index], g_recv.at[off - 1, half, index],
+            {"ep": (ep + off) % ep_count},
+        )
+
+    def y_first(half, index):
+        for off in offsets:
+            y_gather(half, index, off).start()
+
+    proj_n = acc.shape[0] // 2
+    proj_base = n - share_of
+    assert proj_n >= share_of and clock[0] <= proj_base + GAP
+    proj_chain = Chain(
+        proj_base, proj_n, lambda half, index: acc[2 * index + half], pstage,
+        *[lambda half, index: pfin.at[ep, 2 * index + half]] * 3,
+        (pred_send, precv_a, precv_b, pbc_send, pbc_recv), (y_first,),
+    )
+
+    def proj_offer(batches):
+        for batch in batches:
+            proj_sum(batch)
+        for index in range((3 * batches[0] + 1) // 2, 3 * (batches[-1] + 1) // 2):
+            proj_chain.offer(index)
+            if index < share_of:
+                expert_chain.offer(n - share_of + index)
+
     run(STEPS[5])
+    proj_offer((0, 1))
     back_core_copy(1).wait_recv()
     back_cross.wait_recv()
     first = mine + bcore_slot[1].astype(F32) + bx_slot[...].astype(F32)
@@ -698,32 +728,8 @@
 
     for hop, peer in ((1, tp1), (2, tp2), (3, tp3)):
         small_copy(hop - 1, sm, sm_tp.at[hop - 1], {"tp": peer})
-    for batch in range(4):
-        proj_sum(batch)
-
-    def y_gather(half, index, off):
-        chunk = 2 * index + half
-        return remote(
-            pfin.at[ep, chunk], pfin.at[ep, chunk], g_send.at[off - 1, half, index], g_recv.at[off - 1, half, index],
-            {"ep": (ep + off) % ep_count},
-        )
-
-    def y_first(half, index):
-        for off in offsets:
-            y_gather(half, index, off).start()
-
-    proj_n = acc.shape[0] // 2
-    proj_base = n - share_of
-    assert proj_n >= share_of and clock[0] <= proj_base + 2
-    proj_chain = Chain(
-        proj_base, proj_n, lambda half, index: acc[2 * index + half], pstage,
-        *[lambda half, index: pfin.at[ep, 2 * index + half]] * 3,
-        (pred_send, precv_a, precv_b, pbc_send, pbc_recv), (y_first,),
-    )
-    for index in range(proj_n):
-        proj_chain.offer(index)
-        if index < share_of:
-            expert_chain.offer(n - share_of + index)
+    proj_offer((2, 3))
+
     run(STEPS[6])
     return_wait(1)
     returned = ret_out[...].reshape(slots, width)
@@ -744,7 +750,7 @@
     sm_b[...] = total
     for off in range(1, 4):
         small_copy(1 + ep_count + off, sm_b, sm_dp.at[off - 1], {"dp": (dp + off) % 4})
-    run(max(n + 8 + LAGS[1], proj_base + proj_n + 8) - clock[0])
+    run(max(n + 4 * GAP + LAGS[1], proj_base + proj_n + 4 * GAP) - clock[0])
     for copy in small[2 + ep_count :]:
         copy.wait_recv()
     small_out[...] = sm_b[...] + sm_dp[0] + sm_dp[1] + sm_dp[2]

time: 150 us -> 147 us (0.980)
  Pallas kernels: 149 us -> 146 us
    pallas_call x1, Pallas kernels: 141 us -> 138 us  [layer_step(): pl.pallas_call(functools.partial(layer_kernel, ep_count, cols // HD, n),...]
where the time goes in v6:
time: 147 us
  Pallas kernels  146 us (99%)
    pallas_call x1, Pallas kernels, layer_step(): pl.pallas_call(functools.partial(layer_kernel, ep_count, cols // HD, n),...  138 us
    pallas_call x1, Pallas kernels, finish(): pl.pallas_call(finish_kernel, grid_spec=pltpu.PrefetchScalarGridSpec(num_...  8.29 us

profile of v6, /device:TPU:0, one launch (start us, length us, event | category | flops | bytes accessed | tf_op | source)
XLA Modules:
  0.0 147.2 jit_solution(11767343611449919451)
XLA Ops:
  0.7 138.0 %layer.1 = (bf16[2,24,4,32,768]{4,3,2,1,0:T(8,128)(2,1)S(1)}, bf16[2,12,32,768]{3,2,1,0:T(8,128)(2,1)S(1)}, f32[8,768]{1,0:T(8,128)S(1)}, f32[128,768]{1,0:T(8,128)S(1)}, bf16[128,768]{1,0:T(8,128)(2,1)S(1)}) custom-call(bf16[128,768]{1,0:T(8,128)(2,1)} %bitcast.30, s32[1,512]{1,0:T(1,128)} %seg_ref.1, s32[1,512]{1,0:T(1,128)} %key_ref.1, ...), custom_call_target="tpu_custom_call" | custom-call | tf_op jit(solution)/shard_map/layer/pallas_call | solution.py:811
  138.7 8.3 %finish.1 = (f32[768,3072]{1,0:T(8,128)}, f32[3072,768]{1,0:T(8,128)}, f32[192,768]{1,0:T(8,128)}, f32[192,768]{1,0:T(8,128)}, f32[192,768]{1,0:T(8,128)}, /*ind...) custom-call(s32[1]{0:T(128)} %bitcast.tp_ref, ...), custom_call_target="tpu_custom_call" | custom-call | tf_op jit(solution)/shard_map/finish/pallas_call | solution.py:900

commit v7 on v6

--- a/solution.py
+++ b/solution.py
@@ -19,7 +19,7 @@
 STEPS = (6, 3, 3, 1, 1, 3, 6, 6)
 GAP = 2
 LAGS = (6, 8)
-AHEAD = 2
+AHEAD = 1
 FIRST = 1
 
 
@@ -397,20 +397,20 @@
     def core_copy(index):
         return remote(part.at[index], core_slot.at[index], c_send.at[0, index], c_recv.at[0, index], {"tp": tp1})
 
-    part[0] = partial(tp3)
+    part[0] = partial(tp3).astype(BF)
     send(core_copy(0))
-    part[1] = partial(tp1)
+    part[1] = partial(tp1).astype(BF)
     send(core_copy(1))
     crossing = partial(tp2)
     mine = tok_ref[...].astype(F32) + partial(tp)
     core_copy(0).wait_recv()
-    mix[...] = (crossing + core_slot[0]).astype(BF)
+    mix[...] = (crossing + core_slot[0].astype(F32)).astype(BF)
     cross = remote(mix, x_slot, m_send.at[0], m_recv.at[0], {"tp": tp2})
     send(cross)
     pass_on(1)
     forward(1, 0)
     core_copy(1).wait_recv()
-    mine = mine + core_slot[1]
+    mine = mine + core_slot[1].astype(F32)
     cross.wait_recv()
     middle = mine + x_slot[...].astype(F32)
     middle_ref[...] = middle
@@ -824,7 +824,7 @@
             pltpu.VMEM((4,) + single, BF), pltpu.VMEM((4,) + single, BF),
             pltpu.VMEM((2, rows, ep_count * EXP_DEV * capacity), BF),
             pltpu.VMEM((3 * cols, width), BF), pltpu.VMEM((group_rows, group_rows), F32),
-            pltpu.VMEM((2, rows, width), F32), pltpu.VMEM((2, rows, width), F32),
+            pltpu.VMEM((2, rows, width), BF), pltpu.VMEM((2, rows, width), BF),
             pltpu.VMEM((rows, width), BF), pltpu.VMEM((rows, width), BF),
             pltpu.VMEM(block, BF), pltpu.VMEM(block, BF), pltpu.VMEM(single, BF), pltpu.VMEM(single, BF),
             pltpu.VMEM((ep_count * capacity, width), F32), pltpu.VMEM((ep_count * capacity, width), F32),

time: 147 us -> 146 us (level)
  no operation moved by 1% of the time
where the time goes in v7:
time: 146 us
  Pallas kernels  145 us (99%)
    pallas_call x1, Pallas kernels, layer_step(): pl.pallas_call(functools.partial(layer_kernel, ep_count, cols // HD, n),...  137 us
    pallas_call x1, Pallas kernels, finish(): pl.pallas_call(finish_kernel, grid_spec=pltpu.PrefetchScalarGridSpec(num_...  8.29 us

profile of v7, /device:TPU:0, one launch (start us, length us, event | category | flops | bytes accessed | tf_op | source)
XLA Modules:
  0.0 145.8 jit_solution(6357957892711019323)
XLA Ops:
  0.7 136.7 %layer.1 = (bf16[2,24,4,32,768]{4,3,2,1,0:T(8,128)(2,1)S(1)}, bf16[2,12,32,768]{3,2,1,0:T(8,128)(2,1)S(1)}, f32[8,768]{1,0:T(8,128)S(1)}, f32[128,768]{1,0:T(8,128)S(1)}, bf16[128,768]{1,0:T(8,128)(2,1)S(1)}) custom-call(bf16[128,768]{1,0:T(8,128)(2,1)} %bitcast.30, s32[1,512]{1,0:T(1,128)} %seg_ref.1, s32[1,512]{1,0:T(1,128)} %key_ref.1, ...), custom_call_target="tpu_custom_call" | custom-call | tf_op jit(solution)/shard_map/layer/pallas_call | solution.py:811
  137.4 8.3 %finish.1 = (f32[768,3072]{1,0:T(8,128)}, f32[3072,768]{1,0:T(8,128)}, f32[192,768]{1,0:T(8,128)}, f32[192,768]{1,0:T(8,128)}, f32[192,768]{1,0:T(8,128)}, /*ind...) custom-call(s32[1]{0:T(128)} %bitcast.tp_ref, ...), custom_call_target="tpu_custom_call" | custom-call | tf_op jit(solution)/shard_map/finish/pallas_call | solution.py:900
